TPU v7x, 256 devices: a whole 4x4x8 slice. The times are simulated.
256 devices in a mesh: rows: 32 (over x, z), cols: 8 (over y, core).
Axes of the slice: x: 4, y: 4, z: 8, core: 2. Of those that a mesh axis runs over, the one named last changes fastest.
Arguments:
- hankel: float32 [1024, 32768], P('rows', 'cols'), may hold values from -6 to 6
- shifted: float32 [1024, 32768], P('rows', 'cols'), may hold values from -6 to 6
- start_basis: float32 [32768, 128], P(('cols', 'rows')), may hold values from -0.03125 to 0.03125
Outputs:
- basis: float32 [1024, 128], P('rows')
- operator: float32 [128, 128], replicated
All inputs are finite; a program needn't handle non-finite values.
Results may differ from a plain program's by a relative error of at most 0.0002.
Values sent between devices are 32-bit elements; how exact they have to be, the bound alone decides.
No kernel may reach another device: no remote copies, remote signals or barrier semaphores. Data moves between devices by JAX's collectives and lax.ppermute only.
A program may use at most 64 MiB of HBM per device.

v0:
```python
import math

import jax
import jax.numpy as jnp
from jax import lax
from jax.sharding import Mesh
from jax.sharding import PartitionSpec as P

COLS = ("cols_0", "cols_1")
ROWS_COLS = ("rows_0", "rows_1", "cols_0", "cols_1")
ROWS = ("rows_0", "rows_1")
COLS_ROWS = ("cols_0", "cols_1", "rows_0", "rows_1")


def copy_for_each(shard, axis):
    size = lax.axis_size(axis)
    return lax.all_to_all(
        jnp.broadcast_to(shard[None], (size, *shard.shape)), axis, 0, 0, tiled=True
    )


def over_copies(shard, axis):
    everything = copy_for_each(shard, axis)
    return jnp.sum(everything, axis=0)


def over_axes(shard, axes):
    for axis in axes:
        shard = lax.psum(shard, axis)
    return shard


def split_up(shard, dim, size):
    dims = shard.shape
    blocks = shard.reshape(*dims[:dim], size, dims[dim] // size, *dims[dim + 1 :])
    return jnp.moveaxis(blocks, dim, 0)


def summed_on_arrival(shard, axis, dim):
    size = lax.axis_size(axis)
    blocks = lax.all_to_all(split_up(shard, dim, size), axis, 0, 0, tiled=True)
    return jnp.sum(blocks, axis=0)


def over_pieces(shard, axis):
    blocks = lax.all_gather(shard, axis)
    return blocks.sum(axis=0)


def in_one(arrays, axis):
    vector, at, done = (jnp.concatenate([a.reshape(-1) for a in arrays]), 0, [])
    total = over_copies(vector, axis)
    for a in arrays:
        done.append(total[at : at + a.size].reshape(a.shape))
        at += a.size
    return tuple(done)


def product(left, right):
    return jnp.dot(left, right, precision=lax.Precision.HIGHEST, preferred_element_type=jnp.float32)


def right_solve(values, lower):
    return lax.linalg.triangular_solve(lower, values, left_side=False, lower=True, transpose_a=True)


def reduce_columns(y_part, slab, col_index):
    y_full = over_copies(y_part, COLS)
    return (y_full, lax.dynamic_slice_in_dim(y_full, col_index * slab, slab, 0))


def factor(y_slice, total):
    gram = over_axes(product(y_slice.T, y_slice) / total, ROWS_COLS)
    return jnp.linalg.cholesky(gram)


def left_rows(y_full, lower, slab, col_index):
    u_full = right_solve(y_full, lower)
    return (u_full, lax.dynamic_slice_in_dim(u_full, col_index * slab, slab, 0))


def on_device(hankel, shifted, start_basis):
    rows_dev, cols_dev = hankel.shape
    total = rows_dev * lax.axis_size(ROWS)
    slab = rows_dev // lax.axis_size(COLS)
    col_index = lax.axis_index(COLS)
    inv_root = 1.0 / math.sqrt(total)
    block = hankel
    y_part = product(block, lax.all_gather(start_basis, ROWS, axis=0, tiled=True))
    y_full, y_slice = reduce_columns(y_part, slab, col_index)
    lower = factor(y_slice, total)
    u_full, u_slice = left_rows(y_full, lower, slab, col_index)
    block = hankel
    w_slice = summed_on_arrival(product(block.T, u_full), ROWS, 0)
    lower_w = jnp.linalg.cholesky(over_pieces(product(w_slice.T, w_slice), ROWS_COLS))
    piece = lax.all_gather(w_slice, ROWS, axis=0, tiled=True)
    block = hankel
    y_part = product(block, piece)
    z_part = product(shifted, piece)
    y_part = right_solve(y_part, lower_w)
    z_part = right_solve(z_part, lower_w)
    y_full, z_full = in_one((y_part, z_part), COLS)
    y_slice = lax.dynamic_slice_in_dim(y_full, col_index * slab, slab, 0)
    z_slice = lax.dynamic_slice_in_dim(z_full, col_index * slab, slab, 0)
    gram, cross = lax.psum(
        (product(y_slice.T, y_slice) / total, product(y_slice.T, z_slice) * inv_root), ROWS_COLS
    )
    lower = jnp.linalg.cholesky(gram)
    u_full, u_slice = left_rows(y_full, lower, slab, col_index)
    operator = lax.linalg.triangular_solve(lower, cross, left_side=True, lower=True)
    return (u_full, operator)


def solution(mesh):
    finer = Mesh(mesh.devices.reshape(4, 8, 4, 2), ("rows_0", "rows_1", "cols_0", "cols_1"))
    placed = (P(ROWS, COLS), P(ROWS, COLS), P(COLS_ROWS, None))
    return jax.shard_map(
        on_device, mesh=finer, in_specs=placed, out_specs=(P(ROWS, None), P()), check_vma=False
    )
```

profile of v0, /device:TPU:1, one launch (start us, length us, event | category | flops | bytes accessed | tf_op | source)
XLA Modules:
  0.0 904.3 jit_solution(3813198635280233504)
XLA Ops:
  7.9 80.5 %all-gather.5.cloned.1.call-done = f32[4096,128]{1,0:T(8,128)} async-done(((f32[128,128]{1,0:T(8,128)}), f32[4096,128]{1,0:T(8,128)}) %all-gather.5.cloned.1.call-update) | async-done | bytes 2097168 | tf_op jit(solution)/shard_map/all_gather | solution.py:89
  88.4 2.8 fusion.23
  91.9 8.8 all-to-all-start
  100.7 5.3 all-to-all-done
  106.0 0.9 convolution_multiply_fusion.2
  107.0 39.6 %all-reduce.7.cloned.1.call-done = f32[128,128]{0,1:T(8,128)} async-done(((f32[128,128]{0,1:T(8,128)}), f32[128,128]{0,1:T(8,128)}) %all-reduce.7.cloned.1.call-update) | async-done | bytes 65552 | tf_op jit(solution)/shard_map/psum | solution.py:29
  146.7 71.3 %all-reduce.9.cloned.1.call-done = f32[128,128]{0,1:T(8,128)} async-done(((f32[128,128]{0,1:T(8,128)}), f32[128,128]{0,1:T(8,128)}) %all-reduce.9.cloned.1.call-update) | async-done | bytes 65552 | tf_op jit(solution)/shard_map/psum | solution.py:29
  218.1 49.5 %all-reduce.11.cloned.1.call-done = f32[128,128]{0,1:T(8,128)} async-done(((f32[128,128]{0,1:T(8,128)}), f32[128,128]{0,1:T(8,128)}) %all-reduce.11.cloned.1.call-update) | async-done | bytes 65552 | tf_op jit(solution)/shard_map/psum | solution.py:29
  267.7 34.2 %all-reduce.13.cloned.1.call-done = f32[128,128]{0,1:T(8,128)} async-done(((f32[128,128]{0,1:T(8,128)}), f32[128,128]{0,1:T(8,128)}) %all-reduce.13.cloned.1.call-update) | async-done | bytes 65552 | tf_op jit(solution)/shard_map/psum | solution.py:29
  301.8 0.9 copy.25
  302.8 0.9 fusion.11
  303.6 11.7 %cholesky.59 = f32[128,128]{1,0:T(8,128)S(1)} custom-call(f32[128,128]{1,0:T(8,128)S(1)} %fusion.11), custom_call_target="Cholesky" | custom-call | tf_op jit(solution)/shard_map/jit(cholesky)/cholesky | solution.py:74
  316.7 9.8 %custom-call.12 = f32[1,128,128]{1,2,0:T(8,128)S(1)} custom-call(f32[1,128,128]{2,1,0:T(8,128)S(1)} %fusion), custom_call_target="InvertDiagBlocksLowerTriangular" | custom-call | tf_op jit(solution)/shard_map/triangular_solve/custom-call.0 | solution.py:64
  326.6 1.8 convolution_bitcast_fusion
  328.8 56.7 %all_to_all.16 = f32[32,128,128]{1,2,0:T(8,128)S(1)} all-to-all(f32[32,128,128]{1,2,0:T(8,128)S(1)} %bitcast.78), channel_id=1, replica_groups=mesh['rows_0'=4,'rows_1'=8,'cols_0'=4,'cols_1'=2] {'rows_0','rows_1'}, dimensions={0} | all-to-all | bytes 4194304 | tf_op jit(solution)/shard_map/all_to_all | solution.py:41
  386.3 1.8 fusion.24
  388.4 70.0 %all-gather.7.cloned.1.call-done = f32[4096,128]{0,1:T(8,128)} async-done(((f32[128,128]{0,1:T(8,128)}), f32[4096,128]{0,1:T(8,128)}) %all-gather.7.cloned.1.call-update) | async-done | bytes 2097168 | tf_op jit(solution)/shard_map/all_gather | solution.py:96
  458.4 3.8 convolution_bitcast_fusion.6
  462.2 2.1 convolution_bitcast_fusion.5
  464.3 126.1 %all-gather.9.cloned.1.call-done = f32[32768,128]{1,0:T(8,128)} async-done(((f32[128,128]{1,0:T(8,128)}), f32[32768,128]{1,0:T(8,128)}) %all-gather.9.cloned.1.call-update) | async-done | bytes 16777232 | tf_op jit(solution)/shard_map/all_gather | solution.py:46
  590.4 6.6 reduce_sum.38
  597.1 11.7 %cholesky.70 = f32[128,128]{1,0:T(8,128)S(1)} custom-call(f32[128,128]{1,0:T(8,128)S(1)} %fusion.9), custom_call_target="Cholesky" | custom-call | tf_op jit(solution)/shard_map/jit(cholesky)/cholesky | solution.py:95
  610.1 9.8 %custom-call.13 = f32[1,128,128]{1,2,0:T(8,128)S(1)} custom-call(f32[1,128,128]{2,1,0:T(8,128)S(1)} %fusion.1), custom_call_target="InvertDiagBlocksLowerTriangular" | custom-call | tf_op jit(solution)/shard_map/triangular_solve/custom-call.0 | solution.py:64
  620.5 10.9 %all_to_all.17 = f32[8,1,8192]{2,1,0:T(1,128)S(1)} all-to-all(f32[8,1,8192]{2,1,0:T(1,128)S(1)} %broadcast_in_dim.6), channel_id=1, replica_groups=mesh['rows_0'=4,'rows_1'=8,'cols_0'=4,'cols_1'=2] {'cols_0','cols_1'}, dimensions={0} | all-to-all | bytes 524288 | tf_op jit(solution)/shard_map/all_to_all | solution.py:17
  631.6 0.9 convolution_multiply_fusion.1
  632.5 0.9 convolution_multiply_fusion
  633.4 236.8 %all-reduce.15.cloned.1.call-done = (f32[128,128]{0,1:T(8,128)}, f32[128,128]{1,0:T(8,128)}) async-done(((f32[128,128]{0,1:T(8,128)}, f32[128,128]{1,0:T(8,128)}), (f32[128,128]{0,1:T(8,128)}, f32[128,128]{1,0:T(8,128)})) %all-reduce.15.cloned.1.call-update) | async-done | bytes 131088 | tf_op jit(solution)/shard_map/psum | solution.py:105
  870.3 0.9 copy.31
  871.2 0.9 fusion.6
  872.1 11.7 %cholesky.81 = f32[128,128]{1,0:T(8,128)S(1)} custom-call(f32[128,128]{1,0:T(8,128)S(1)} %fusion.6), custom_call_target="Cholesky" | custom-call | tf_op jit(solution)/shard_map/jit(cholesky)/cholesky | solution.py:108
  885.1 9.8 %custom-call.15 = f32[1,128,128]{1,2,0:T(8,128)S(1)} custom-call(f32[1,128,128]{2,1,0:T(8,128)S(1)} %fusion.2), custom_call_target="InvertDiagBlocksLowerTriangular" | custom-call | tf_op jit(solution)/shard_map/triangular_solve/custom-call.0 | solution.py:64
  895.7 1.8 fusion.3
  (45 shorter events, 8.6 us)
Async XLA Ops:
  7.2 81.3 %copy-start = (f32[32,4096]{1,0:T(8,128)S(1)}, f32[32,4096]{1,0:T(8,128)}, u32[]{:S(2)}) copy-start(f32[32,4096]{1,0:T(8,128)} %param.6) | copy-start | bytes 1572868
  7.2 81.3 %all-gather.5.cloned.1.call-start = ((), (), s32[]{:S(2)}) async-start(), calls=%async_computation.3 | async-start | bytes 2162688 | tf_op jit(solution)/shard_map/all_gather | solution.py:89
  91.9 14.1 %all-to-all-start = ((f32[8,32,128]{2,1,0:T(8,128)}), f32[8,32,128]{2,1,0:T(8,128)S(1)}, u32[]{:S(2)}, u32[]{:S(2)}) async-start(f32[8,32,128]{2,1,0:T(8,128)} %broadcast_in_dim.4), calls=%async_computation | async-start | bytes 262144 | tf_op jit(solution)/shard_map/all_to_all | solution.py:17
  100.7 45.9 %all-reduce.7.cloned.1.call-start = ((), (), s32[]{:S(2)}) async-start(), calls=%async_computation.4 | async-start | bytes 131072 | tf_op jit(solution)/shard_map/psum | solution.py:29
  107.0 111.0 %all-reduce.9.cloned.1.call-start = ((), (), s32[]{:S(2)}) async-start(), calls=%async_computation.5 | async-start | bytes 131072 | tf_op jit(solution)/shard_map/psum | solution.py:29
  146.7 120.9 %all-reduce.11.cloned.1.call-start = ((), (), s32[]{:S(2)}) async-start(), calls=%async_computation.6 | async-start | bytes 131072 | tf_op jit(solution)/shard_map/psum | solution.py:29
  218.0 83.8 %all-reduce.13.cloned.1.call-start = ((), (), s32[]{:S(2)}) async-start(), calls=%async_computation.7 | async-start | bytes 131072 | tf_op jit(solution)/shard_map/psum | solution.py:29
  267.6 190.8 %all-gather.7.cloned.1.call-start = ((), (), s32[]{:S(2)}) async-start(), calls=%async_computation.8 | async-start | bytes 2162688 | tf_op jit(solution)/shard_map/all_gather | solution.py:96
  385.5 76.7 %copy-start.2 = (f32[32,4096]{1,0:T(8,128)S(1)}, f32[32,4096]{1,0:T(8,128)}, u32[]{:S(2)}) copy-start(f32[32,4096]{1,0:T(8,128)} %param.7) | copy-start | bytes 1572868
  386.3 204.1 %all-gather.9.cloned.1.call-start = ((), (), s32[]{:S(2)}) async-start(), calls=%async_computation.9 | async-start | bytes 16842752 | tf_op jit(solution)/shard_map/all_gather | solution.py:46
  388.1 482.1 %all-reduce.15.cloned.1.call-start = ((), (), s32[]{:S(2)}) async-start(), calls=%async_computation.10 | async-start | bytes 262144 | tf_op jit(solution)/shard_map/psum | solution.py:105
  458.4 3.8 copy-start.1
Sparse Core Ops, SparseCore 0:
  10.6 77.7 all-gather.4
  107.1 39.5 all-reduce.6
  149.1 68.8 all-reduce.8
  220.2 47.3 all-reduce.10
  270.1 31.6 all-reduce.12
  386.4 71.9 all-gather.6
  462.7 127.6 all-gather.8
  633.6 236.6 all-reduce.14
where the time goes:
time: 905 us; the launch traced here: 904 us
  waiting for transfers between devices  714 us (79%)
  other arithmetic  77.8 us (9%)
  blocking collectives  67.6 us (7%)
  matrix products  18.1 us (2%)
  between operations  14.3 us (2%)
  starting transfers between devices  9.3 us (1%)
    psum x1, waiting for transfers between devices, on_device(): lax.psum((product(y_slice.T, y_slice) / total, product(y_slice.T, z_slice...  237 us
    psum x4, waiting for transfers between devices, over_axes(): shard = lax.psum(shard, axis)  195 us
    all_gather x1, waiting for transfers between devices, over_pieces(): blocks = lax.all_gather(shard, axis)  126 us
    all_gather x1, waiting for transfers between devices, on_device(): lax.all_gather(start_basis, ROWS, axis=0, tiled=True)  80.5 us
    all_gather x1, waiting for transfers between devices, on_device(): piece = lax.all_gather(w_slice, ROWS, axis=0, tiled=True)  70 us
    all_to_all x1, blocking collectives, summed_on_arrival(): blocks = lax.all_to_all(split_up(shard, dim, size), axis, 0, 0, tiled=True)  56.7 us
    another operation x6, other arithmetic, right_solve(): lax.linalg.triangular_solve(lower, values, left_side=False, lower=True, t...  31.4 us
  transfers between devices with their start and end apart: 9, of which 9 were waited for; matrix products, arithmetic and copies ran while one was open for 1% of the time, Pallas kernels for 0%

commit v1 on v0

v1 whole, which is shorter than its diff:
```python
import jax
import jax.numpy as jnp
from jax import lax
from jax.sharding import Mesh
from jax.sharding import PartitionSpec as P

ROWS = ("x", "z")
COLS = ("y", "core")
CHIPS = ("x", "z", "y")
CHANGE = ("x", "z", "core")


def einsum(spec, left, right):
    return jnp.einsum(
        spec, left, right, precision=lax.Precision.HIGHEST, preferred_element_type=jnp.float32
    )


def exchanged(blocks, axis):
    return lax.all_to_all(blocks, axis, 0, 0, tiled=True)


def from_other_core(value):
    return lax.ppermute(value, "core", [(0, 1), (1, 0)])


def by_suffix(block):
    rows, cols = block.shape
    groups = lax.axis_size(ROWS)
    pieces = block.reshape(2, rows // 2, groups, cols // groups).transpose(2, 0, 1, 3)
    pieces = pieces.reshape(2 * groups, rows // 2, cols // groups)
    return exchanged(pieces, CHANGE).reshape(groups, 2, rows // 2, cols // groups)


def summed_over_chips(part):
    chips = lax.axis_size(CHIPS)
    mine = jnp.sum(exchanged(part.reshape(chips, -1, part.shape[-1]), CHIPS), axis=0)
    copies = jnp.broadcast_to(mine[None], (chips, *mine.shape))
    return exchanged(copies, CHIPS).reshape(part.shape)


def inverse_or_zero(scale):
    return jnp.where(scale > 0, 1.0 / jnp.where(scale > 0, scale, 1.0), 0.0)


def on_device(hankel, shifted, start_basis):
    rows_dev, _ = hankel.shape
    rank = start_basis.shape[1]
    core = lax.axis_index("core")
    other_start = from_other_core(start_basis)
    h = by_suffix(hankel)
    t = by_suffix(shifted)
    start = jnp.where(
        core == 0, jnp.stack([start_basis, other_start]), jnp.stack([other_start, start_basis])
    )
    groups, _, half, _ = h.shape
    c_part = einsum("rkij,kjn->rin", h, start).reshape(groups * half, rank)
    c = summed_over_chips(c_part)
    c_scale = jnp.max(jnp.abs(c))
    c = c * inverse_or_zero(c_scale)
    x_part = einsum("rkij,rin->kjn", h, c.reshape(groups, half, rank))
    x_other, c_scale_other = from_other_core(x_part), from_other_core(c_scale)
    c_largest = inverse_or_zero(jnp.maximum(c_scale, c_scale_other))
    x = x_part * (c_scale * c_largest) + x_other * (c_scale_other * c_largest)
    c = c * (c_scale * c_largest)
    y_part = einsum("rkij,kjn->rin", h, x).reshape(groups * half, rank)
    z_part = einsum("rkij,kjn->rin", t, x).reshape(groups * half, rank)
    yz = summed_over_chips(jnp.concatenate([y_part, z_part], axis=0))
    y, z = yz[: groups * half], yz[groups * half :]
    y_scale = jnp.max(jnp.abs(y))
    y = y * inverse_or_zero(y_scale)
    grams = einsum("pm,qpn->qmn", y, jnp.stack([y, z, c]))
    mine = lax.dynamic_slice_in_dim(y, lax.axis_index(ROWS) * half, half, 0)
    grams_other, mine_other, y_scale_other = (
        from_other_core(grams), from_other_core(mine), from_other_core(y_scale)
    )
    y_top = jnp.maximum(y_scale, y_scale_other)
    y_largest = inverse_or_zero(y_top)
    f, f_other = y_scale * y_largest, y_scale_other * y_largest
    gram = grams[0] * (f * f) + grams_other[0] * (f_other * f_other)
    cross = grams[1] * f + grams_other[1] * f_other
    gram_w = grams[2] * f + grams_other[2] * f_other
    lower = jnp.linalg.cholesky(gram)
    lower_w = jnp.linalg.cholesky(gram_w)
    mine, mine_other = mine * f, mine_other * f_other
    y_rows = jnp.where(
        core == 0, jnp.concatenate([mine, mine_other]), jnp.concatenate([mine_other, mine])
    )
    total = rows_dev * groups
    basis = lax.linalg.triangular_solve(
        lower, y_rows * jnp.sqrt(float(total)), left_side=False, lower=True, transpose_a=True
    )
    operator = lax.linalg.triangular_solve(lower, cross, left_side=True, lower=True)
    operator = lax.linalg.triangular_solve(
        lower_w, operator, left_side=False, lower=True, transpose_a=True
    )
    return basis, operator * lax.rsqrt(y_top)


def solution(mesh):
    finer = Mesh(mesh.devices.reshape(4, 8, 4, 2), ("x", "z", "y", "core"))
    placed = (P(ROWS, COLS), P(ROWS, COLS), P((*COLS, *ROWS), None))
    return jax.shard_map(
        on_device, mesh=finer, in_specs=placed, out_specs=(P(ROWS, None), P()), check_vma=False
    )
```

time: 905 us -> 213 us (0.24)
  waiting for transfers between devices: 714 us -> 54.2 us
  starting transfers between devices: 9.3 us -> 43.5 us
  other arithmetic: 77.8 us -> 47.5 us
  blocking collectives: 67.6 us -> 46.4 us
  matrix products: 18.1 us -> 5.69 us
    psum x5 -> x0, waiting for transfers between devices: 431 us -> none  [the longest x1 237 us: on_device(): lax.psum((product(y_slice.T, y_slice) / total, product(y_slice.T, z_slice...]
    all_gather x3 -> x0, waiting for transfers between devices: 277 us -> none  [the longest x1 126 us: over_pieces(): blocks = lax.all_gather(shard, axis)]
    all_to_all x1 -> x4, waiting for transfers between devices: 5.27 us -> 53 us  [exchanged(): return lax.all_to_all(blocks, axis, 0, 0, tiled=True)]
    all_to_all x1 -> x4, starting transfers between devices: 8.85 us -> 36.3 us  [exchanged(): return lax.all_to_all(blocks, axis, 0, 0, tiled=True)]
    another operation x12 -> x7, other arithmetic: 56.2 us -> 33.3 us  [the longest x3 12.4 us: on_device(): lower_w = jnp.linalg.cholesky(gram_w)]
    all_to_all x2, blocking collectives: 67.6 us -> 46.4 us  [exchanged(): return lax.all_to_all(blocks, axis, 0, 0, tiled=True)]
    dot_general x8 -> x5, matrix products: 15.1 us -> 3.79 us  [einsum(): jnp.einsum(spec, left, right, precision=lax.Precision.HIGHEST, preferred_...]
  transfers between devices with their start and end apart: 9 -> 10, of which waited for: 9 -> 6; matrix products, arithmetic and copies ran while one was open for 1% -> 2% of each run, Pallas kernels for 0% -> 0%
where the time goes in v1:
time: 213 us
  waiting for transfers between devices  54.2 us (25%)
  other arithmetic  47.5 us (22%)
  blocking collectives  46.4 us (22%)
  starting transfers between devices  43.5 us (20%)
  between operations  9.1 us (4%)
  local copies, waits for them, and re-layouts  6.11 us (3%)
  matrix products  5.69 us (3%)
    all_to_all x4, waiting for transfers between devices, exchanged(): return lax.all_to_all(blocks, axis, 0, 0, tiled=True)  53 us
    all_to_all x2, blocking collectives, exchanged(): return lax.all_to_all(blocks, axis, 0, 0, tiled=True)  46.4 us
    all_to_all x4, starting transfers between devices, exchanged(): return lax.all_to_all(blocks, axis, 0, 0, tiled=True)  36.3 us
    another operation x3, other arithmetic, on_device(): lower_w = jnp.linalg.cholesky(gram_w)  12.4 us
    another operation x3, other arithmetic, on_device(): lower = jnp.linalg.cholesky(gram)  12.4 us
    another operation x2, other arithmetic, on_device(): lax.linalg.triangular_solve(lower, y_rows * jnp.sqrt(float(total)), left_...  10.5 us
    another operation x2, other arithmetic, on_device(): lax.linalg.triangular_solve(lower_w, operator, left_side=False, lower=Tru...  10.5 us
    ppermute x6, starting transfers between devices, from_other_core(): return lax.ppermute(value, 'core', [(0, 1), (1, 0)])  7.17 us
  transfers between devices with their start and end apart: 10, of which 6 were waited for; matrix products, arithmetic and copies ran while one was open for 2% of the time, Pallas kernels for 0%

profile of v1, /device:TPU:1, one launch (start us, length us, event | category | flops | bytes accessed | tf_op | source)
XLA Modules:
  0.0 212.5 jit_solution(14362125677489828974)
XLA Ops:
  0.6 1.1 copy.51
  1.8 1.1 copy.27
  2.9 13.1 %all-to-all-start = ((f32[64,16,128]{2,1,0:T(8,128)}), f32[64,16,128]{2,1,0:T(8,128)S(1)}, u32[]{:S(2)}, u32[]{:S(2)}) async-start(f32[64,16,128]{2,1,0:T(8,128)} %bitcast.4), calls=%async_computation | async-start | bytes 1048576 | tf_op jit(solution)/shard_map/all_to_all | solution.py:20
  16.6 0.9 collective-permute-done
  17.5 15.9 %all-to-all-done = f32[64,16,128]{2,1,0:T(8,128)S(1)} async-done(((f32[64,16,128]{2,1,0:T(8,128)}), f32[64,16,128]{2,1,0:T(8,128)S(1)}, u32[]{:S(2)}, u32[]{:S(2)}) %all-to-all-start) | async-done | bytes 524320 | tf_op jit(solution)/shard_map/all_to_all | solution.py:20
  33.4 0.8 convolution_bitcast_fusion.2
  34.3 22.0 %all_to_all.30 = f32[128,4,128]{2,1,0:T(4,128)S(1)} all-to-all(f32[128,4,128]{2,1,0:T(4,128)S(1)} %bitcast.120), channel_id=1, replica_groups=mesh['x'=4,'z'=8,'y'=4,'core'=2] {'x','z','y'}, dimensions={0} | all-to-all | bytes 524288 | tf_op jit(solution)/shard_map/all_to_all | solution.py:20
  56.5 0.7 broadcast_in_dim.4
  57.2 7.2 %all-to-all-start.2 = ((f32[128,4,128]{2,1,0:T(4,128)}), f32[128,4,128]{2,1,0:T(4,128)S(1)}, u32[]{:S(2)}, u32[]{:S(2)}) async-start(f32[128,4,128]{2,1,0:T(4,128)} %broadcast_in_dim.4), calls=%async_computation.2 | async-start | bytes 524288 | tf_op jit(solution)/shard_map/all_to_all | solution.py:20
  64.6 1.1 copy.34
  65.7 10.7 %all-to-all-done.2 = f32[128,4,128]{2,1,0:T(4,128)S(1)} async-done(((f32[128,4,128]{2,1,0:T(4,128)}), f32[128,4,128]{2,1,0:T(4,128)S(1)}, u32[]{:S(2)}, u32[]{:S(2)}) %all-to-all-start.2) | async-done | bytes 262176 | tf_op jit(solution)/shard_map/all_to_all | solution.py:20
  76.3 7.8 %all-to-all-start.3 = ((f32[64,16,128]{2,1,0:T(8,128)}), f32[64,16,128]{2,1,0:T(8,128)S(1)}, u32[]{:S(2)}, u32[]{:S(2)}) async-start(f32[64,16,128]{2,1,0:T(8,128)} %bitcast.23), calls=%async_computation.3 | async-start | bytes 1048576 | tf_op jit(solution)/shard_map/all_to_all | solution.py:20
  84.1 0.7 abs_reduce_fusion.1
  90.5 11.0 %all-to-all-done.3 = f32[64,16,128]{2,1,0:T(8,128)S(1)} async-done(((f32[64,16,128]{2,1,0:T(8,128)}), f32[64,16,128]{2,1,0:T(8,128)S(1)}, u32[]{:S(2)}, u32[]{:S(2)}) %all-to-all-start.3) | async-done | bytes 524320 | tf_op jit(solution)/shard_map/all_to_all | solution.py:20
  101.5 0.8 convolution_bitcast_fusion
  102.4 0.8 convolution_bitcast_fusion.1
  103.5 24.4 %all_to_all.31 = f32[128,8,128]{2,1,0:T(8,128)S(1)} all-to-all(f32[128,8,128]{2,1,0:T(8,128)S(1)} %maximum_bitcast_fusion), channel_id=1, replica_groups=mesh['x'=4,'z'=8,'y'=4,'core'=2] {'x','z','y'}, dimensions={0} | all-to-all | bytes 1048576 | tf_op jit(solution)/shard_map/all_to_all | solution.py:20
  128.0 0.8 broadcast_in_dim.5
  128.8 8.2 %all-to-all-start.5 = ((f32[128,8,128]{2,1,0:T(8,128)}), f32[128,8,128]{2,1,0:T(8,128)S(1)}, u32[]{:S(2)}, u32[]{:S(2)}) async-start(f32[128,8,128]{2,1,0:T(8,128)} %broadcast_in_dim.5), calls=%async_computation.5 | async-start | bytes 1048576 | tf_op jit(solution)/shard_map/all_to_all | solution.py:20
  137.2 15.4 %all-to-all-done.5 = f32[128,8,128]{2,1,0:T(8,128)S(1)} async-done(((f32[128,8,128]{2,1,0:T(8,128)}), f32[128,8,128]{2,1,0:T(8,128)S(1)}, u32[]{:S(2)}, u32[]{:S(2)}) %all-to-all-start.5) | async-done | bytes 524320 | tf_op jit(solution)/shard_map/all_to_all | solution.py:20
  153.2 4.9 %collective-permute-start.3 = (f32[]{:T(128)}, f32[]{:T(128)}, u32[]{:S(2)}, u32[]{:S(2)}) collective-permute-start(f32[]{:T(128)} %abs_reduce_fusion), channel_id=1, source_target_pairs={{0,1},{1,0},{2,3},{3,2},{4,5},{5,4},{6,7},{7,6},{8,9},{9,8},{10,11... | collective-permute-start | bytes 20 | tf_op jit(solution)/shard_map/ppermute | solution.py:24
  162.0 0.8 convolution_bitcast_fusion.3
  162.8 0.8 collective-permute-start.5
  164.9 11.7 %cholesky.44 = f32[128,128]{1,0:T(8,128)S(1)} custom-call(f32[128,128]{1,0:T(8,128)S(1)} %get-tuple-element.11), custom_call_target="Cholesky" | custom-call | tf_op jit(solution)/shard_map/jit(cholesky)/cholesky | solution.py:83
  176.6 0.6 compare_reduce_fusion.1
  177.3 0.7 fusion.21
  177.9 9.8 %custom-call.10 = f32[1,128,128]{1,2,0:T(8,128)S(1)} custom-call(f32[1,128,128]{2,1,0:T(8,128)S(1)} %fusion.21), custom_call_target="InvertDiagBlocksLowerTriangular" | custom-call | tf_op jit(solution)/shard_map/triangular_solve | solution.py:90
  187.8 11.7 %cholesky.55 = f32[128,128]{1,0:T(8,128)S(1)} custom-call(f32[128,128]{1,0:T(8,128)S(1)} %get-tuple-element.10), custom_call_target="Cholesky" | custom-call | tf_op jit(solution)/shard_map/jit(cholesky)/cholesky | solution.py:84
  200.1 0.7 fusion.22
  200.8 9.8 %custom-call.11 = f32[1,128,128]{1,2,0:T(8,128)S(1)} custom-call(f32[1,128,128]{2,1,0:T(8,128)S(1)} %fusion.22), custom_call_target="InvertDiagBlocksLowerTriangular" | custom-call | tf_op jit(solution)/shard_map/triangular_solve | solution.py:94
  210.6 0.8 fusion.34
  211.7 0.8 broadcast_multiply_fusion.2
  (39 shorter events, 5.7 us)
Async XLA Ops:
  2.9 13.1 %copy-start.1 = (f32[128,128]{1,0:T(8,128)S(1)}, f32[128,128]{1,0:T(8,128)}, u32[]{:S(2)}) copy-start(f32[128,128]{1,0:T(8,128)} %param.6) | copy-start | bytes 196612
  2.9 30.4 %all-to-all-start = ((f32[64,16,128]{2,1,0:T(8,128)}), f32[64,16,128]{2,1,0:T(8,128)S(1)}, u32[]{:S(2)}, u32[]{:S(2)}) async-start(f32[64,16,128]{2,1,0:T(8,128)} %bitcast.4), calls=%async_computation | async-start | bytes 1048576 | tf_op jit(solution)/shard_map/all_to_all | solution.py:20
  16.0 1.4 collective-permute-start
  56.3 8.1 %copy-start = (f32[32,4096]{1,0:T(8,128)S(1)}, f32[32,4096]{1,0:T(8,128)}, u32[]{:S(2)}) copy-start(f32[32,4096]{1,0:T(8,128)} %param.5) | copy-start | bytes 1572868
  57.2 19.1 %all-to-all-start.2 = ((f32[128,4,128]{2,1,0:T(4,128)}), f32[128,4,128]{2,1,0:T(4,128)S(1)}, u32[]{:S(2)}, u32[]{:S(2)}) async-start(f32[128,4,128]{2,1,0:T(4,128)} %broadcast_in_dim.4), calls=%async_computation.2 | async-start | bytes 524288 | tf_op jit(solution)/shard_map/all_to_all | solution.py:20
  76.3 25.1 %all-to-all-start.3 = ((f32[64,16,128]{2,1,0:T(8,128)}), f32[64,16,128]{2,1,0:T(8,128)S(1)}, u32[]{:S(2)}, u32[]{:S(2)}) async-start(f32[64,16,128]{2,1,0:T(8,128)} %bitcast.23), calls=%async_computation.3 | async-start | bytes 1048576 | tf_op jit(solution)/shard_map/all_to_all | solution.py:20
  84.9 1.9 collective-permute-start.1
  89.5 12.0 %collective-permute-start.2 = (f32[2,128,128]{1,2,0:T(8,128)S(1)}, f32[2,128,128]{1,2,0:T(8,128)S(1)}, u32[]{:S(2)}, u32[]{:S(2)}) collective-permute-start(f32[2,128,128]{1,2,0:T(8,128)S(1)} %convolution_bitcast_fusion.4), channel_id=1, source_target_pairs={{0,1},{1,0},{2,3},{3,2},{4,5},{5,4},{6,7},{7,6},{8,9},{9,8},{10,11... | collective-permute-start | bytes 393224 | tf_op jit(solution)/shard_map/ppermute | solution.py:24
  128.8 23.8 %all-to-all-start.5 = ((f32[128,8,128]{2,1,0:T(8,128)}), f32[128,8,128]{2,1,0:T(8,128)S(1)}, u32[]{:S(2)}, u32[]{:S(2)}) async-start(f32[128,8,128]{2,1,0:T(8,128)} %broadcast_in_dim.5), calls=%async_computation.5 | async-start | bytes 1048576 | tf_op jit(solution)/shard_map/all_to_all | solution.py:20
  153.2 6.6 %collective-permute-start.3 = (f32[]{:T(128)}, f32[]{:T(128)}, u32[]{:S(2)}, u32[]{:S(2)}) collective-permute-start(f32[]{:T(128)} %abs_reduce_fusion), channel_id=1, source_target_pairs={{0,1},{1,0},{2,3},{3,2},{4,5},{5,4},{6,7},{7,6},{8,9},{9,8},{10,11... | collective-permute-start | bytes 20 | tf_op jit(solution)/shard_map/ppermute | solution.py:24
  161.9 2.4 %collective-permute-start.4 = (f32[16,128]{1,0:T(8,128)S(1)}, f32[16,128]{1,0:T(8,128)S(1)}, u32[]{:S(2)}, u32[]{:S(2)}) collective-permute-start(f32[16,128]{1,0:T(8,128)S(1)} %get-tuple-element.4), channel_id=1, source_target_pairs={{0,1},{1,0},{2,3},{3,2},{4,5},{5,4},{6,7},{7,6},{8,9},{9,8},{10,11... | collective-permute-start | bytes 24584 | tf_op jit(solution)/shard_map/ppermute | solution.py:24
  162.8 1.9 collective-permute-start.5

commit v2 on v1

v2 whole, which is shorter than its diff:
```python
import functools

import jax
import jax.numpy as jnp
from jax import lax
from jax.experimental import pallas as pl
from jax.experimental.pallas import tpu as pltpu
from jax.sharding import Mesh
from jax.sharding import PartitionSpec as P

ROWS = ("x", "z")
COLS = ("y", "core")
CHIPS = ("x", "z", "y")
CHANGE = ("x", "z", "core")
SUB, LANE = 8, 128


def exchanged(blocks, axis):
    return lax.all_to_all(blocks, axis, 0, 0, tiled=True)


def from_other_core(value):
    return lax.ppermute(value, "core", [(0, 1), (1, 0)])


def call(kernel, name, shapes, scalars, arrays):
    return pl.pallas_call(
        kernel,
        name=name,
        out_shape=[jax.ShapeDtypeStruct(shape, jnp.float32) for shape in shapes],
        in_specs=[pl.BlockSpec(memory_space=pltpu.SMEM)] * len(scalars)
        + [pl.BlockSpec(memory_space=pltpu.VMEM)] * len(arrays),
        out_specs=[pl.BlockSpec(memory_space=pltpu.VMEM)] * len(shapes),
        compiler_params=pltpu.CompilerParams(vmem_limit_bytes=24 << 20),
    )(*scalars, *arrays)


def dot(left, right, left_dim=1, right_dim=0):
    return lax.dot_general(
        left,
        right,
        (((left_dim,), (right_dim,)), ((), ())),
        precision=lax.Precision.HIGHEST,
        preferred_element_type=jnp.float32,
    )


def inverse_or_zero(scale):
    return jnp.where(scale > 0, 1.0 / jnp.where(scale > 0, scale, 1.0), 0.0)


def largest(value):
    return jnp.max(jnp.max(jnp.abs(value), axis=0, keepdims=True), axis=1, keepdims=True)


def split_kernel(h_ref, t_ref, out_ref):
    groups, _, half2, lanes = out_ref.shape
    half = half2 // 2
    for at, ref in ((0, h_ref), (half, t_ref)):
        for g in range(groups):
            for part in range(2):
                out_ref[g, part, at : at + half, :] = ref[
                    part * half : (part + 1) * half, g * lanes : (g + 1) * lanes
                ]


def block_of(ht_ref, part, which):
    groups, _, half2, lanes = ht_ref.shape
    half = half2 // 2
    block = ht_ref[:, part, which * half : (which + 1) * half, :]
    return block.reshape(groups * half, lanes)


def columns_kernel(core_ref, ht_ref, own_ref, other_ref, out_ref):
    first = core_ref[0] == 0
    own, other = own_ref[...], other_ref[...]
    out_ref[...] = dot(block_of(ht_ref, 0, 0), jnp.where(first, own, other)) + dot(
        block_of(ht_ref, 1, 0), jnp.where(first, other, own)
    )


def sum_kernel(in_ref, out_ref, *, rows):
    tiles = [in_ref[SUB * i : SUB * (i + 1), :] for i in range(in_ref.shape[0] // SUB)]
    while len(tiles) > 1:
        tiles = [a + b for a, b in zip(tiles[::2], tiles[1::2])]
    total = tiles[0]
    if rows < SUB:
        total = total + pltpu.roll(total, rows, 0)
    for i in range(out_ref.shape[0] // SUB):
        out_ref[SUB * i : SUB * (i + 1), :] = total


def across_kernel(ht_ref, c_ref, out_ref):
    c = c_ref[...]
    scale = largest(c)
    c = c * inverse_or_zero(scale)
    for part in range(2):
        out_ref[part * LANE : (part + 1) * LANE, :] = dot(block_of(ht_ref, part, 0), c, 0, 0)
    out_ref[2 * LANE :, :] = jnp.broadcast_to(scale, (SUB, LANE))


def image_kernel(ht_ref, own_ref, other_ref, out_ref):
    scale, scale_other = own_ref[2 * LANE : 2 * LANE + 1, :], other_ref[2 * LANE : 2 * LANE + 1, :]
    top = inverse_or_zero(jnp.maximum(scale, scale_other))
    x = own_ref[: 2 * LANE, :] * (scale * top) + other_ref[: 2 * LANE, :] * (scale_other * top)
    rows = out_ref.shape[0] // 2
    for which in range(2):
        out_ref[which * rows : (which + 1) * rows, :] = dot(
            block_of(ht_ref, 0, which), x[:LANE]
        ) + dot(block_of(ht_ref, 1, which), x[LANE:])


def gram_kernel(at_ref, yz_ref, c_ref, own_ref, other_ref, out_ref, *, half):
    scale, scale_other = own_ref[2 * LANE : 2 * LANE + 1, :], other_ref[2 * LANE : 2 * LANE + 1, :]
    top = inverse_or_zero(jnp.maximum(scale, scale_other))
    c = c_ref[...]
    c = c * (inverse_or_zero(scale) * (scale * top))
    rows = yz_ref.shape[0] // 2
    y = yz_ref[:rows, :]
    y_scale = largest(y)
    back = inverse_or_zero(y_scale)
    y = y * back
    out_ref[:LANE, :] = dot(y, y, 0, 0)
    out_ref[LANE : 2 * LANE, :] = dot(y, yz_ref[rows:, :], 0, 0)
    out_ref[2 * LANE : 3 * LANE, :] = dot(c, y, 0, 0)
    start = pl.multiple_of(at_ref[0] * half, half)
    out_ref[3 * LANE : 3 * LANE + half, :] = yz_ref[pl.ds(start, half), :] * back
    out_ref[3 * LANE + half :, :] = jnp.broadcast_to(y_scale, (SUB, LANE))


def inverse_factors(matrices):
    size = matrices[0].shape[0]
    blocks = size // SUB
    lane = lax.broadcasted_iota(jnp.int32, (SUB, size), 1)
    sub = lax.broadcasted_iota(jnp.int32, (SUB, size), 0)
    work = [[m[SUB * i : SUB * (i + 1), :] for i in range(blocks)] for m in matrices]

    def columns(rows, low):
        return [
            jnp.broadcast_to(rows[:, low + j : low + j + 1], (SUB, size)) for j in range(SUB)
        ]

    def row(values, j):
        return jnp.broadcast_to(values[j : j + 1, :], (SUB, size))

    for k in range(blocks):
        low = SUB * k
        inside = (lane >= low) & (lane < low + SUB)
        done = []
        for mine in work:
            column = columns(mine[k], low)
            w = jnp.where(inside, (lane == sub + low).astype(jnp.float32), mine[k])
            steps, pivots = [], jnp.ones((SUB, size), jnp.float32)
            for j in range(SUB):
                pivot = row(column[j], j)
                inverse = 1.0 / pivot
                pivots = jnp.where(sub == j, pivot, pivots)
                factor = jnp.where(sub > j, column[j] * inverse, 0.0)
                ahead = {}
                for i in range(j + 1, SUB):
                    ahead[i] = row(column[i], j)
                    column[i] = column[i] - factor * ahead[i]
                reduced = row(w, j)
                w = w - factor * reduced
                steps.append((inverse, ahead, reduced))
            root = lax.rsqrt(pivots)
            root = root * (1.5 - 0.5 * pivots * root * root)
            mine[k] = jnp.where(lane <= sub + low, w * root, 0.0)
            done.append(steps)
        for mine, steps in zip(work, done):
            for i in range(k + 1, blocks):
                column = columns(mine[i], low)
                w = jnp.where(inside, 0.0, mine[i])
                for j, (inverse, ahead, reduced) in enumerate(steps):
                    factor = column[j] * inverse
                    for n in range(j + 1, SUB):
                        column[n] = column[n] - factor * ahead[n]
                    w = w - factor * reduced
                mine[i] = w
    return [jnp.concatenate(mine, axis=0) for mine in work]


def final_kernel(core_ref, own_ref, other_ref, basis_ref, operator_ref, *, half, total):
    at = 3 * LANE + half
    scale, scale_other = own_ref[at : at + 1, :], other_ref[at : at + 1, :]
    top = jnp.maximum(scale, scale_other)
    back = inverse_or_zero(top)
    f, f_other = scale * back, scale_other * back
    gram = own_ref[:LANE, :] * (f * f) + other_ref[:LANE, :] * (f_other * f_other)
    cross = own_ref[LANE : 2 * LANE, :] * f + other_ref[LANE : 2 * LANE, :] * f_other
    gram_w = own_ref[2 * LANE : 3 * LANE, :] * f + other_ref[2 * LANE : 3 * LANE, :] * f_other
    lower, lower_w = inverse_factors([gram, gram_w])
    root = jnp.sqrt(jnp.float32(total))
    core = core_ref[0]
    for ref, factor, place in ((own_ref, f, core), (other_ref, f_other, 1 - core)):
        rows = ref[3 * LANE : at, :] * (factor * root)
        basis_ref[pl.ds(pl.multiple_of(place * half, half), half), :] = dot(rows, lower, 1, 1)
    operator_ref[...] = dot(dot(lower, cross), lower_w, 1, 1) * lax.rsqrt(top)


def summed_over_chips(part):
    chips = lax.axis_size(CHIPS)
    rows = part.shape[0] // chips
    blocks = exchanged(part.reshape(chips, rows, LANE), CHIPS).reshape(part.shape)
    (copies,) = call(
        functools.partial(sum_kernel, rows=rows), f"sum_{rows}", [part.shape], [], [blocks]
    )
    return exchanged(copies.reshape(chips, rows, LANE), CHIPS).reshape(part.shape)


def on_device(hankel, shifted, start_basis):
    rows_dev = hankel.shape[0]
    groups, half = lax.axis_size(ROWS), rows_dev // 2
    rows = groups * half
    core = lax.axis_index("core").astype(jnp.int32).reshape(1)
    place = lax.axis_index(ROWS).astype(jnp.int32).reshape(1)
    other_start = from_other_core(start_basis)
    (pieces,) = call(split_kernel, "split", [(groups, 2, rows_dev, LANE)], [], [hankel, shifted])
    pieces = exchanged(pieces.reshape(2 * groups, rows_dev, LANE), CHANGE)
    ht = pieces.reshape(groups, 2, rows_dev, LANE)
    (c_part,) = call(
        columns_kernel, "columns", [(rows, LANE)], [core], [ht, start_basis, other_start]
    )
    c = summed_over_chips(c_part)
    (x_part,) = call(across_kernel, "across", [(2 * LANE + SUB, LANE)], [], [ht, c])
    x_other = from_other_core(x_part)
    (yz_part,) = call(image_kernel, "image", [(2 * rows, LANE)], [], [ht, x_part, x_other])
    yz = summed_over_chips(yz_part)
    (grams,) = call(
        functools.partial(gram_kernel, half=half),
        "grams",
        [(3 * LANE + half + SUB, LANE)],
        [place],
        [yz, c, x_part, x_other],
    )
    return call(
        functools.partial(final_kernel, half=half, total=rows_dev * groups),
        "factors",
        [(rows_dev, LANE), (LANE, LANE)],
        [core],
        [grams, from_other_core(grams)],
    )


def solution(mesh):
    finer = Mesh(mesh.devices.reshape(4, 8, 4, 2), ("x", "z", "y", "core"))
    placed = (P(ROWS, COLS), P(ROWS, COLS), P((*COLS, *ROWS), None))

    def whole(*blocks):
        return tuple(on_device(*blocks))

    return jax.shard_map(
        whole, mesh=finer, in_specs=placed, out_specs=(P(ROWS, None), P()), check_vma=False
    )
```

time: 213 us -> 156 us (0.73)
  other arithmetic: 47.5 us -> 0 us
  blocking collectives: 46.4 us -> 63.8 us
  starting transfers between devices: 43.5 us -> 30 us
  Pallas kernels: 0 us -> 12.6 us
  between operations: 9.1 us -> 0.71 us
  waiting for transfers between devices: 54.2 us -> 46 us
  matrix products: 5.69 us -> 0 us
  local copies, waits for them, and re-layouts: 6.11 us -> 2.08 us
    another operation x10 -> x0, other arithmetic: 45.7 us -> none  [the longest x3 12.4 us: on_device(): lower_w = jnp.linalg.cholesky(gram_w)]
    all_to_all x2 -> x3, blocking collectives: 46.4 us -> 63.8 us  [exchanged(): return lax.all_to_all(blocks, axis, 0, 0, tiled=True)]
    all_to_all x4 -> x2, starting transfers between devices: 36.3 us -> 21.3 us  [exchanged(): return lax.all_to_all(blocks, axis, 0, 0, tiled=True)]
    pallas_call x0 -> x8, Pallas kernels: none -> 12.6 us  [call(): pl.pallas_call(kernel, name=name, out_shape=[jax.ShapeDtypeStruct(shape,...]
    all_to_all x4 -> x2, waiting for transfers between devices: 53 us -> 43 us  [exchanged(): return lax.all_to_all(blocks, axis, 0, 0, tiled=True)]
    dot_general x5 -> x0, matrix products: 3.79 us -> none  [einsum(): jnp.einsum(spec, left, right, precision=lax.Precision.HIGHEST, preferred_...]
    transpose x4 -> x0, local copies, waits for them, and re-layouts: 2.27 us -> none  [by_suffix(): block.reshape(2, rows // 2, groups, cols // groups).transpose(2, 0, 1, 3)]
    ppermute x6 -> x3, starting transfers between devices: 7.17 us -> 8.74 us  [from_other_core(): return lax.ppermute(value, 'core', [(0, 1), (1, 0)])]
  transfers between devices with their start and end apart: 10 -> 5, of which waited for: 6 -> 5; matrix products, arithmetic and copies ran while one was open for 2% -> 0% of each run, Pallas kernels for 0% -> 0%
where the time goes in v2:
time: 156 us; the launch traced here: 155 us
  blocking collectives  63.8 us (41%)
  waiting for transfers between devices  46 us (29%)
  starting transfers between devices  30 us (19%)
  Pallas kernels  12.6 us (8%)
  local copies, waits for them, and re-layouts  2.08 us (1%)
    all_to_all x3, blocking collectives, exchanged(): return lax.all_to_all(blocks, axis, 0, 0, tiled=True)  63.8 us
    all_to_all x2, waiting for transfers between devices, exchanged(): return lax.all_to_all(blocks, axis, 0, 0, tiled=True)  43 us
    all_to_all x2, starting transfers between devices, exchanged(): return lax.all_to_all(blocks, axis, 0, 0, tiled=True)  21.3 us
    pallas_call x8, Pallas kernels, call(): pl.pallas_call(kernel, name=name, out_shape=[jax.ShapeDtypeStruct(shape,...  12.6 us
    ppermute x3, starting transfers between devices, from_other_core(): return lax.ppermute(value, 'core', [(0, 1), (1, 0)])  8.74 us
  transfers between devices with their start and end apart: 5, of which 5 were waited for; matrix products, arithmetic and copies ran while one was open for 0% of the time, Pallas kernels for 0%

profile of v2, /device:TPU:1, one launch (start us, length us, event | category | flops | bytes accessed | tf_op | source)
XLA Modules:
  0.0 155.3 jit_solution(16563768393329956805)
XLA Ops:
  0.6 0.0 copy-start
  0.6 1.0 copy-done
  1.7 0.0 copy-start.1
  1.7 1.0 copy-done.1
  2.7 1.0 split.1
  3.8 0.0 copy-start.2
  3.8 13.1 %all-to-all-start = ((f32[64,32,128]{2,1,0:T(8,128)}), f32[64,32,128]{2,1,0:T(8,128)S(1)}, u32[]{:S(2)}, u32[]{:S(2)}) async-start(f32[64,32,128]{2,1,0:T(8,128)} %bitcast.2), calls=%async_computation | async-start | bytes 2097152 | tf_op jit(solution)/shard_map/all_to_all | solution.py:19
  16.9 0.0 copy-done.2
  16.9 0.5 collective-permute-start
  17.4 0.9 collective-permute-done.other_ref
  18.3 27.1 %all-to-all-done = f32[64,32,128]{2,1,0:T(8,128)S(1)} async-done(((f32[64,32,128]{2,1,0:T(8,128)}), f32[64,32,128]{2,1,0:T(8,128)S(1)}, u32[]{:S(2)}, u32[]{:S(2)}) %all-to-all-start) | async-done | bytes 1048608 | tf_op jit(solution)/shard_map/all_to_all | solution.py:19
  45.4 0.6 columns.1
  46.0 22.3 %all_to_all.25 = f32[128,4,128]{2,1,0:T(4,128)S(1)} all-to-all(f32[128,4,128]{2,1,0:T(4,128)S(1)} %bitcast.22), channel_id=1, replica_groups=mesh['x'=4,'z'=8,'y'=4,'core'=2] {'x','z','y'}, dimensions={0} | all-to-all | bytes 524288 | tf_op jit(solution)/shard_map/all_to_all | solution.py:19
  68.4 18.6 %all_to_all.26 = f32[128,4,128]{2,1,0:T(4,128)S(1)} all-to-all(f32[128,4,128]{2,1,0:T(4,128)S(1)} %bitcast.21), channel_id=1, replica_groups=mesh['x'=4,'z'=8,'y'=4,'core'=2] {'x','z','y'}, dimensions={0} | all-to-all | bytes 524288 | tf_op jit(solution)/shard_map/all_to_all | solution.py:19
  87.1 0.7 across.1.own_ref
  87.8 3.8 %collective-permute-start.1 = (f32[264,128]{1,0:T(8,128)S(1)}, f32[264,128]{1,0:T(8,128)S(1)}, u32[]{:S(2)}, u32[]{:S(2)}) collective-permute-start(f32[264,128]{1,0:T(8,128)S(1)} %across.1.own_ref), channel_id=1, source_target_pairs={{0,1},{1,0},{2,3},{3,2},{4,5},{5,4},{6,7},{7,6},{8,9},{9,8},{10,11... | collective-permute-start | bytes 405512 | tf_op jit(solution)/shard_map/ppermute | solution.py:23
  91.5 1.0 collective-permute-done.1.other_ref
  92.5 1.0 image.1
  93.5 22.8 %all_to_all.27 = f32[128,8,128]{2,1,0:T(8,128)S(1)} all-to-all(f32[128,8,128]{2,1,0:T(8,128)S(1)} %bitcast.17), channel_id=1, replica_groups=mesh['x'=4,'z'=8,'y'=4,'core'=2] {'x','z','y'}, dimensions={0} | all-to-all | bytes 1048576 | tf_op jit(solution)/shard_map/all_to_all | solution.py:19
  116.4 0.9 sum_8.1
  117.2 8.2 %all-to-all-start.4 = ((f32[128,8,128]{2,1,0:T(8,128)}), f32[128,8,128]{2,1,0:T(8,128)S(1)}, u32[]{:S(2)}, u32[]{:S(2)}) async-start(f32[128,8,128]{2,1,0:T(8,128)} %bitcast.10), calls=%async_computation.4 | async-start | bytes 1048576 | tf_op jit(solution)/shard_map/all_to_all | solution.py:19
  125.4 15.9 %all-to-all-done.4 = f32[128,8,128]{2,1,0:T(8,128)S(1)} async-done(((f32[128,8,128]{2,1,0:T(8,128)}), f32[128,8,128]{2,1,0:T(8,128)S(1)}, u32[]{:S(2)}, u32[]{:S(2)}) %all-to-all-start.4) | async-done | bytes 524320 | tf_op jit(solution)/shard_map/all_to_all | solution.py:19
  141.4 0.9 grams.1.own_ref
  142.3 4.4 %collective-permute-start.2 = (f32[408,128]{1,0:T(8,128)S(1)}, f32[408,128]{1,0:T(8,128)S(1)}, u32[]{:S(2)}, u32[]{:S(2)}) collective-permute-start(f32[408,128]{1,0:T(8,128)S(1)} %grams.1.own_ref), channel_id=1, source_target_pairs={{0,1},{1,0},{2,3},{3,2},{4,5},{5,4},{6,7},{7,6},{8,9},{9,8},{10,11... | collective-permute-start | bytes 626696 | tf_op jit(solution)/shard_map/ppermute | solution.py:23
  146.7 1.1 collective-permute-done.2.other_ref
  147.8 7.5 %factors.1 = (f32[32,128]{1,0:T(8,128)}, f32[128,128]{1,0:T(8,128)}) custom-call(s32[1]{0:T(128)} %bitcast.core_ref, f32[408,128]{1,0:T(8,128)S(1)} %grams.1.own_ref, f32[408,128]{1,0:T(8,128)S(1)} %collective-permute-done.2.other_ref), custom_call_target="tpu_custom_call" | custom-call | tf_op jit(solution)/shard_map/factors/pallas_call | solution.py:27
  (1 shorter events, 0.0 us)
Async XLA Ops:
  0.6 1.0 copy-start
  1.7 1.0 copy-start.1
  3.8 13.1 %copy-start.2 = (f32[128,128]{1,0:T(8,128)S(1)}, f32[128,128]{1,0:T(8,128)}, u32[]{:S(2)}) copy-start(f32[128,128]{1,0:T(8,128)} %own_ref.1) | copy-start | bytes 196612
  3.8 41.7 %all-to-all-start = ((f32[64,32,128]{2,1,0:T(8,128)}), f32[64,32,128]{2,1,0:T(8,128)S(1)}, u32[]{:S(2)}, u32[]{:S(2)}) async-start(f32[64,32,128]{2,1,0:T(8,128)} %bitcast.2), calls=%async_computation | async-start | bytes 2097152 | tf_op jit(solution)/shard_map/all_to_all | solution.py:19
  16.9 1.4 collective-permute-start
  87.8 4.8 %collective-permute-start.1 = (f32[264,128]{1,0:T(8,128)S(1)}, f32[264,128]{1,0:T(8,128)S(1)}, u32[]{:S(2)}, u32[]{:S(2)}) collective-permute-start(f32[264,128]{1,0:T(8,128)S(1)} %across.1.own_ref), channel_id=1, source_target_pairs={{0,1},{1,0},{2,3},{3,2},{4,5},{5,4},{6,7},{7,6},{8,9},{9,8},{10,11... | collective-permute-start | bytes 405512 | tf_op jit(solution)/shard_map/ppermute | solution.py:23
  117.2 24.1 %all-to-all-start.4 = ((f32[128,8,128]{2,1,0:T(8,128)}), f32[128,8,128]{2,1,0:T(8,128)S(1)}, u32[]{:S(2)}, u32[]{:S(2)}) async-start(f32[128,8,128]{2,1,0:T(8,128)} %bitcast.10), calls=%async_computation.4 | async-start | bytes 1048576 | tf_op jit(solution)/shard_map/all_to_all | solution.py:19
  142.3 5.5 %collective-permute-start.2 = (f32[408,128]{1,0:T(8,128)S(1)}, f32[408,128]{1,0:T(8,128)S(1)}, u32[]{:S(2)}, u32[]{:S(2)}) collective-permute-start(f32[408,128]{1,0:T(8,128)S(1)} %grams.1.own_ref), channel_id=1, source_target_pairs={{0,1},{1,0},{2,3},{3,2},{4,5},{5,4},{6,7},{7,6},{8,9},{9,8},{10,11... | collective-permute-start | bytes 626696 | tf_op jit(solution)/shard_map/ppermute | solution.py:23

commit v3 on v2

--- a/solution.py
+++ b/solution.py
@@ -10,7 +10,7 @@
 
 ROWS = ("x", "z")
 COLS = ("y", "core")
-CHIPS = ("x", "z", "y")
+PLANE = ("x", "y")
 CHANGE = ("x", "z", "core")
 SUB, LANE = 8, 128
 
@@ -80,14 +80,12 @@
 
 
 def sum_kernel(in_ref, out_ref, *, rows):
-    tiles = [in_ref[SUB * i : SUB * (i + 1), :] for i in range(in_ref.shape[0] // SUB)]
-    while len(tiles) > 1:
-        tiles = [a + b for a, b in zip(tiles[::2], tiles[1::2])]
-    total = tiles[0]
-    if rows < SUB:
-        total = total + pltpu.roll(total, rows, 0)
-    for i in range(out_ref.shape[0] // SUB):
-        out_ref[SUB * i : SUB * (i + 1), :] = total
+    for at in range(0, rows, SUB):
+        tiles = [in_ref[i + at : i + at + SUB, :] for i in range(0, in_ref.shape[0], rows)]
+        while len(tiles) > 1:
+            tiles = [a + b for a, b in zip(tiles[::2], tiles[1::2])]
+        for i in range(0, out_ref.shape[0], rows):
+            out_ref[i + at : i + at + SUB, :] = tiles[0]
 
 
 def across_kernel(ht_ref, c_ref, out_ref):
@@ -198,14 +196,18 @@
     operator_ref[...] = dot(dot(lower, cross), lower_w, 1, 1) * lax.rsqrt(top)
 
 
-def summed_over_chips(part):
-    chips = lax.axis_size(CHIPS)
-    rows = part.shape[0] // chips
-    blocks = exchanged(part.reshape(chips, rows, LANE), CHIPS).reshape(part.shape)
-    (copies,) = call(
-        functools.partial(sum_kernel, rows=rows), f"sum_{rows}", [part.shape], [], [blocks]
-    )
-    return exchanged(copies.reshape(chips, rows, LANE), CHIPS).reshape(part.shape)
+def exchanged_rows(values, axis):
+    count = lax.axis_size(axis)
+    return exchanged(values.reshape(count, -1, LANE), axis).reshape(values.shape)
+
+
+def summed_over_chips(part, name):
+    rows = part.shape[0] // lax.axis_size(PLANE)
+    kernel = functools.partial(sum_kernel, rows=rows)
+    line = (lax.axis_size("z") * rows, LANE)
+    (copies,) = call(kernel, name + "_plane", [line], [], [exchanged_rows(part, PLANE)])
+    (copies,) = call(kernel, name + "_line", [part.shape], [], [exchanged_rows(copies, "z")])
+    return exchanged_rows(copies, PLANE)
 
 
 def on_device(hankel, shifted, start_basis):
@@ -221,11 +223,11 @@
     (c_part,) = call(
         columns_kernel, "columns", [(rows, LANE)], [core], [ht, start_basis, other_start]
     )
-    c = summed_over_chips(c_part)
+    c = summed_over_chips(c_part, "columns")
     (x_part,) = call(across_kernel, "across", [(2 * LANE + SUB, LANE)], [], [ht, c])
     x_other = from_other_core(x_part)
     (yz_part,) = call(image_kernel, "image", [(2 * rows, LANE)], [], [ht, x_part, x_other])
-    yz = summed_over_chips(yz_part)
+    yz = summed_over_chips(yz_part, "image")
     (grams,) = call(
         functools.partial(gram_kernel, half=half),
         "grams",

time: 156 us -> 142 us (0.910)
  waiting for transfers between devices: 46 us -> 39 us
  starting transfers between devices: 30 us -> 26.6 us
  blocking collectives: 63.8 us -> 60.8 us
    all_to_all x2, waiting for transfers between devices: 43 us -> 36 us  [exchanged(): return lax.all_to_all(blocks, axis, 0, 0, tiled=True)]
    all_to_all x2, starting transfers between devices: 21.3 us -> 17.7 us  [exchanged(): return lax.all_to_all(blocks, axis, 0, 0, tiled=True)]
    all_to_all x3 -> x5, blocking collectives: 63.8 us -> 60.8 us  [exchanged(): return lax.all_to_all(blocks, axis, 0, 0, tiled=True)]
    pallas_call x8 -> x10, Pallas kernels: 12.6 us -> 12.7 us  [call(): pl.pallas_call(kernel, name=name, out_shape=[jax.ShapeDtypeStruct(shape,...]
where the time goes in v3:
time: 142 us
  blocking collectives  60.8 us (43%)
  waiting for transfers between devices  39 us (27%)
  starting transfers between devices  26.6 us (19%)
  Pallas kernels  12.7 us (9%)
  local copies, waits for them, and re-layouts  2.08 us (1%)
    all_to_all x5, blocking collectives, exchanged(): return lax.all_to_all(blocks, axis, 0, 0, tiled=True)  60.8 us
    all_to_all x2, waiting for transfers between devices, exchanged(): return lax.all_to_all(blocks, axis, 0, 0, tiled=True)  36 us
    all_to_all x2, starting transfers between devices, exchanged(): return lax.all_to_all(blocks, axis, 0, 0, tiled=True)  17.7 us
    pallas_call x10, Pallas kernels, call(): pl.pallas_call(kernel, name=name, out_shape=[jax.ShapeDtypeStruct(shape,...  12.7 us
    ppermute x3, starting transfers between devices, from_other_core(): return lax.ppermute(value, 'core', [(0, 1), (1, 0)])  8.86 us
    ppermute x3, waiting for transfers between devices, from_other_core(): return lax.ppermute(value, 'core', [(0, 1), (1, 0)])  2.98 us
  transfers between devices with their start and end apart: 5, of which 5 were waited for; matrix products, arithmetic and copies ran while one was open for 0% of the time, Pallas kernels for 0%

profile of v3, /device:TPU:1, one launch (start us, length us, event | category | flops | bytes accessed | tf_op | source)
XLA Modules:
  0.0 141.9 jit_solution(9866677606597888319)
XLA Ops:
  0.6 0.0 copy-start
  0.6 1.0 copy-done
  1.7 0.0 copy-start.1
  1.7 1.0 copy-done.1
  2.7 1.0 split.1
  3.8 0.0 copy-start.2
  3.8 13.1 %all-to-all-start = ((f32[64,32,128]{2,1,0:T(8,128)}), f32[64,32,128]{2,1,0:T(8,128)S(1)}, u32[]{:S(2)}, u32[]{:S(2)}) async-start(f32[64,32,128]{2,1,0:T(8,128)} %bitcast.2), calls=%async_computation | async-start | bytes 2097152 | tf_op jit(solution)/shard_map/all_to_all | solution.py:19
  16.9 0.0 copy-done.2
  16.9 0.5 collective-permute-start
  17.4 0.9 collective-permute-done.other_ref
  18.3 27.1 %all-to-all-done = f32[64,32,128]{2,1,0:T(8,128)S(1)} async-done(((f32[64,32,128]{2,1,0:T(8,128)}), f32[64,32,128]{2,1,0:T(8,128)S(1)}, u32[]{:S(2)}, u32[]{:S(2)}) %all-to-all-start) | async-done | bytes 1048608 | tf_op jit(solution)/shard_map/all_to_all | solution.py:19
  45.4 0.6 columns.1
  46.0 14.8 %all_to_all.35 = f32[16,32,128]{2,1,0:T(8,128)S(1)} all-to-all(f32[16,32,128]{2,1,0:T(8,128)S(1)} %bitcast.28), channel_id=1, replica_groups=mesh['x'=4,'z'=8,'y'=4,'core'=2] {'x','y'}, dimensions={0} | all-to-all | bytes 524288 | tf_op jit(solution)/shard_map/all_to_all | solution.py:19
  60.8 10.3 %all_to_all.36 = f32[8,32,128]{2,1,0:T(8,128)S(1)} all-to-all(f32[8,32,128]{2,1,0:T(8,128)S(1)} %bitcast.29), channel_id=1, replica_groups=mesh['x'=4,'z'=8,'y'=4,'core'=2] {'z'}, dimensions={0} | all-to-all | bytes 262144 | tf_op jit(solution)/shard_map/all_to_all | solution.py:19
  71.2 10.5 %all_to_all.37 = f32[16,32,128]{2,1,0:T(8,128)S(1)} all-to-all(f32[16,32,128]{2,1,0:T(8,128)S(1)} %bitcast.27), channel_id=1, replica_groups=mesh['x'=4,'z'=8,'y'=4,'core'=2] {'x','y'}, dimensions={0} | all-to-all | bytes 524288 | tf_op jit(solution)/shard_map/all_to_all | solution.py:19
  81.7 0.7 across.1.own_ref
  82.4 3.9 %collective-permute-start.1 = (f32[264,128]{1,0:T(8,128)S(1)}, f32[264,128]{1,0:T(8,128)S(1)}, u32[]{:S(2)}, u32[]{:S(2)}) collective-permute-start(f32[264,128]{1,0:T(8,128)S(1)} %across.1.own_ref), channel_id=1, source_target_pairs={{0,1},{1,0},{2,3},{3,2},{4,5},{5,4},{6,7},{7,6},{8,9},{9,8},{10,11... | collective-permute-start | bytes 405512 | tf_op jit(solution)/shard_map/ppermute | solution.py:23
  86.3 1.0 collective-permute-done.1.other_ref
  87.3 1.0 image.1
  88.3 13.6 %all_to_all.38 = f32[16,64,128]{2,1,0:T(8,128)S(1)} all-to-all(f32[16,64,128]{2,1,0:T(8,128)S(1)} %bitcast.21), channel_id=1, replica_groups=mesh['x'=4,'z'=8,'y'=4,'core'=2] {'x','y'}, dimensions={0} | all-to-all | bytes 1048576 | tf_op jit(solution)/shard_map/all_to_all | solution.py:19
  101.9 11.6 %all_to_all.39 = f32[8,64,128]{2,1,0:T(8,128)S(1)} all-to-all(f32[8,64,128]{2,1,0:T(8,128)S(1)} %bitcast.24), channel_id=1, replica_groups=mesh['x'=4,'z'=8,'y'=4,'core'=2] {'z'}, dimensions={0} | all-to-all | bytes 524288 | tf_op jit(solution)/shard_map/all_to_all | solution.py:19
  113.5 0.9 image_line.1
  114.4 4.6 %all-to-all-start.6 = ((f32[16,64,128]{2,1,0:T(8,128)}), f32[16,64,128]{2,1,0:T(8,128)S(1)}, u32[]{:S(2)}, u32[]{:S(2)}) async-start(f32[16,64,128]{2,1,0:T(8,128)} %bitcast.14), calls=%async_computation.6 | async-start | bytes 1048576 | tf_op jit(solution)/shard_map/all_to_all | solution.py:19
  119.0 8.9 %all-to-all-done.6 = f32[16,64,128]{2,1,0:T(8,128)S(1)} async-done(((f32[16,64,128]{2,1,0:T(8,128)}), f32[16,64,128]{2,1,0:T(8,128)S(1)}, u32[]{:S(2)}, u32[]{:S(2)}) %all-to-all-start.6) | async-done | bytes 524320 | tf_op jit(solution)/shard_map/all_to_all | solution.py:19
  127.9 0.9 grams.1.own_ref
  128.9 4.4 %collective-permute-start.2 = (f32[408,128]{1,0:T(8,128)S(1)}, f32[408,128]{1,0:T(8,128)S(1)}, u32[]{:S(2)}, u32[]{:S(2)}) collective-permute-start(f32[408,128]{1,0:T(8,128)S(1)} %grams.1.own_ref), channel_id=1, source_target_pairs={{0,1},{1,0},{2,3},{3,2},{4,5},{5,4},{6,7},{7,6},{8,9},{9,8},{10,11... | collective-permute-start | bytes 626696 | tf_op jit(solution)/shard_map/ppermute | solution.py:23
  133.3 1.1 collective-permute-done.2.other_ref
  134.4 7.5 %factors.1 = (f32[32,128]{1,0:T(8,128)}, f32[128,128]{1,0:T(8,128)}) custom-call(s32[1]{0:T(128)} %bitcast.core_ref, f32[408,128]{1,0:T(8,128)S(1)} %grams.1.own_ref, f32[408,128]{1,0:T(8,128)S(1)} %collective-permute-done.2.other_ref), custom_call_target="tpu_custom_call" | custom-call | tf_op jit(solution)/shard_map/factors/pallas_call | solution.py:27
  (3 shorter events, 0.1 us)
Async XLA Ops:
  0.6 1.0 copy-start
  1.7 1.0 copy-start.1
  3.8 13.1 %copy-start.2 = (f32[128,128]{1,0:T(8,128)S(1)}, f32[128,128]{1,0:T(8,128)}, u32[]{:S(2)}) copy-start(f32[128,128]{1,0:T(8,128)} %own_ref.1) | copy-start | bytes 196612
  3.8 41.7 %all-to-all-start = ((f32[64,32,128]{2,1,0:T(8,128)}), f32[64,32,128]{2,1,0:T(8,128)S(1)}, u32[]{:S(2)}, u32[]{:S(2)}) async-start(f32[64,32,128]{2,1,0:T(8,128)} %bitcast.2), calls=%async_computation | async-start | bytes 2097152 | tf_op jit(solution)/shard_map/all_to_all | solution.py:19
  16.9 1.4 %collective-permute-start = (f32[128,128]{1,0:T(8,128)S(1)}, f32[128,128]{1,0:T(8,128)S(1)}, u32[]{:S(2)}, u32[]{:S(2)}) collective-permute-start(f32[128,128]{1,0:T(8,128)S(1)} %copy-done.2), channel_id=1, source_target_pairs={{0,1},{1,0},{2,3},{3,2},{4,5},{5,4},{6,7},{7,6},{8,9},{9,8},{10,11... | collective-permute-start | bytes 196616 | tf_op jit(solution)/shard_map/ppermute | solution.py:23
  82.4 4.9 %collective-permute-start.1 = (f32[264,128]{1,0:T(8,128)S(1)}, f32[264,128]{1,0:T(8,128)S(1)}, u32[]{:S(2)}, u32[]{:S(2)}) collective-permute-start(f32[264,128]{1,0:T(8,128)S(1)} %across.1.own_ref), channel_id=1, source_target_pairs={{0,1},{1,0},{2,3},{3,2},{4,5},{5,4},{6,7},{7,6},{8,9},{9,8},{10,11... | collective-permute-start | bytes 405512 | tf_op jit(solution)/shard_map/ppermute | solution.py:23
  114.4 13.5 %all-to-all-start.6 = ((f32[16,64,128]{2,1,0:T(8,128)}), f32[16,64,128]{2,1,0:T(8,128)S(1)}, u32[]{:S(2)}, u32[]{:S(2)}) async-start(f32[16,64,128]{2,1,0:T(8,128)} %bitcast.14), calls=%async_computation.6 | async-start | bytes 1048576 | tf_op jit(solution)/shard_map/all_to_all | solution.py:19
  128.9 5.5 %collective-permute-start.2 = (f32[408,128]{1,0:T(8,128)S(1)}, f32[408,128]{1,0:T(8,128)S(1)}, u32[]{:S(2)}, u32[]{:S(2)}) collective-permute-start(f32[408,128]{1,0:T(8,128)S(1)} %grams.1.own_ref), channel_id=1, source_target_pairs={{0,1},{1,0},{2,3},{3,2},{4,5},{5,4},{6,7},{7,6},{8,9},{9,8},{10,11... | collective-permute-start | bytes 626696 | tf_op jit(solution)/shard_map/ppermute | solution.py:23

commit v4 on v3

--- a/solution.py
+++ b/solution.py
@@ -13,6 +13,7 @@
 PLANE = ("x", "y")
 CHANGE = ("x", "z", "core")
 SUB, LANE = 8, 128
+PIECES = 4
 
 
 def exchanged(blocks, axis):
@@ -23,16 +24,16 @@
     return lax.ppermute(value, "core", [(0, 1), (1, 0)])
 
 
-def call(kernel, name, shapes, scalars, arrays):
+def call(kernel, name, shapes, arrays, scratch=(), space=pltpu.VMEM):
     return pl.pallas_call(
         kernel,
         name=name,
         out_shape=[jax.ShapeDtypeStruct(shape, jnp.float32) for shape in shapes],
-        in_specs=[pl.BlockSpec(memory_space=pltpu.SMEM)] * len(scalars)
-        + [pl.BlockSpec(memory_space=pltpu.VMEM)] * len(arrays),
-        out_specs=[pl.BlockSpec(memory_space=pltpu.VMEM)] * len(shapes),
-        compiler_params=pltpu.CompilerParams(vmem_limit_bytes=24 << 20),
-    )(*scalars, *arrays)
+        in_specs=[pl.BlockSpec(memory_space=space)] * len(arrays),
+        out_specs=[pl.BlockSpec(memory_space=space)] * len(shapes),
+        scratch_shapes=scratch,
+        compiler_params=pltpu.CompilerParams(vmem_limit_bytes=(24 if space is pltpu.VMEM else 60) << 20),
+    )(*arrays)
 
 
 def dot(left, right, left_dim=1, right_dim=0):
@@ -53,15 +54,30 @@
     return jnp.max(jnp.max(jnp.abs(value), axis=0, keepdims=True), axis=1, keepdims=True)
 
 
-def split_kernel(h_ref, t_ref, out_ref):
-    groups, _, half2, lanes = out_ref.shape
-    half = half2 // 2
-    for at, ref in ((0, h_ref), (half, t_ref)):
-        for g in range(groups):
-            for part in range(2):
-                out_ref[g, part, at : at + half, :] = ref[
-                    part * half : (part + 1) * half, g * lanes : (g + 1) * lanes
-                ]
+def split_kernel(h_ref, t_ref, out_ref, h, t, out, in_sem, out_sem):
+    groups, _, half2, lanes = out.shape
+    half, some = half2 // 2, groups // PIECES
+    loads, stores = [], []
+    for i in range(PIECES):
+        at = slice(i * some * lanes, (i + 1) * some * lanes)
+        for j, (source, block) in enumerate(((h_ref, h), (t_ref, t))):
+            load = pltpu.make_async_copy(source.at[:, at], block.at[:, at], in_sem.at[2 * i + j])
+            load.start()
+            loads.append(load)
+    for i in range(PIECES):
+        for j, block in enumerate((h, t)):
+            loads[2 * i + j].wait()
+            for g in range(i * some, (i + 1) * some):
+                for part in range(2):
+                    out[g, part, j * half : (j + 1) * half, :] = block[
+                        part * half : (part + 1) * half, g * lanes : (g + 1) * lanes
+                    ]
+        at = slice(i * some, (i + 1) * some)
+        store = pltpu.make_async_copy(out.at[at], out_ref.at[at], out_sem.at[i])
+        store.start()
+        stores.append(store)
+    for store in stores:
+        store.wait()
 
 
 def block_of(ht_ref, part, which):
@@ -71,8 +87,8 @@
     return block.reshape(groups * half, lanes)
 
 
-def columns_kernel(core_ref, ht_ref, own_ref, other_ref, out_ref):
-    first = core_ref[0] == 0
+def columns_kernel(ht_ref, own_ref, other_ref, out_ref):
+    first = lax.axis_index("core") == 0
     own, other = own_ref[...], other_ref[...]
     out_ref[...] = dot(block_of(ht_ref, 0, 0), jnp.where(first, own, other)) + dot(
         block_of(ht_ref, 1, 0), jnp.where(first, other, own)
@@ -108,7 +124,7 @@
         ) + dot(block_of(ht_ref, 1, which), x[LANE:])
 
 
-def gram_kernel(at_ref, yz_ref, c_ref, own_ref, other_ref, out_ref, *, half):
+def gram_kernel(yz_ref, c_ref, own_ref, other_ref, out_ref, *, half):
     scale, scale_other = own_ref[2 * LANE : 2 * LANE + 1, :], other_ref[2 * LANE : 2 * LANE + 1, :]
     top = inverse_or_zero(jnp.maximum(scale, scale_other))
     c = c_ref[...]
@@ -121,7 +137,8 @@
     out_ref[:LANE, :] = dot(y, y, 0, 0)
     out_ref[LANE : 2 * LANE, :] = dot(y, yz_ref[rows:, :], 0, 0)
     out_ref[2 * LANE : 3 * LANE, :] = dot(c, y, 0, 0)
-    start = pl.multiple_of(at_ref[0] * half, half)
+    place = lax.axis_index("x") * lax.axis_size("z") + lax.axis_index("z")
+    start = pl.multiple_of(place * half, half)
     out_ref[3 * LANE : 3 * LANE + half, :] = yz_ref[pl.ds(start, half), :] * back
     out_ref[3 * LANE + half :, :] = jnp.broadcast_to(y_scale, (SUB, LANE))
 
@@ -178,7 +195,7 @@
     return [jnp.concatenate(mine, axis=0) for mine in work]
 
 
-def final_kernel(core_ref, own_ref, other_ref, basis_ref, operator_ref, *, half, total):
+def final_kernel(own_ref, other_ref, basis_ref, operator_ref, *, half, total):
     at = 3 * LANE + half
     scale, scale_other = own_ref[at : at + 1, :], other_ref[at : at + 1, :]
     top = jnp.maximum(scale, scale_other)
@@ -189,7 +206,7 @@
     gram_w = own_ref[2 * LANE : 3 * LANE, :] * f + other_ref[2 * LANE : 3 * LANE, :] * f_other
     lower, lower_w = inverse_factors([gram, gram_w])
     root = jnp.sqrt(jnp.float32(total))
-    core = core_ref[0]
+    core = lax.axis_index("core")
     for ref, factor, place in ((own_ref, f, core), (other_ref, f_other, 1 - core)):
         rows = ref[3 * LANE : at, :] * (factor * root)
         basis_ref[pl.ds(pl.multiple_of(place * half, half), half), :] = dot(rows, lower, 1, 1)
@@ -205,8 +222,8 @@
     rows = part.shape[0] // lax.axis_size(PLANE)
     kernel = functools.partial(sum_kernel, rows=rows)
     line = (lax.axis_size("z") * rows, LANE)
-    (copies,) = call(kernel, name + "_plane", [line], [], [exchanged_rows(part, PLANE)])
-    (copies,) = call(kernel, name + "_line", [part.shape], [], [exchanged_rows(copies, "z")])
+    (copies,) = call(kernel, name + "_plane", [line], [exchanged_rows(part, PLANE)])
+    (copies,) = call(kernel, name + "_line", [part.shape], [exchanged_rows(copies, "z")])
     return exchanged_rows(copies, PLANE)
 
 
@@ -214,32 +231,34 @@
     rows_dev = hankel.shape[0]
     groups, half = lax.axis_size(ROWS), rows_dev // 2
     rows = groups * half
-    core = lax.axis_index("core").astype(jnp.int32).reshape(1)
-    place = lax.axis_index(ROWS).astype(jnp.int32).reshape(1)
     other_start = from_other_core(start_basis)
-    (pieces,) = call(split_kernel, "split", [(groups, 2, rows_dev, LANE)], [], [hankel, shifted])
+    out_shape = (groups, 2, rows_dev, LANE)
+    scratch = [
+        pltpu.VMEM(hankel.shape, jnp.float32),
+        pltpu.VMEM(hankel.shape, jnp.float32),
+        pltpu.VMEM(out_shape, jnp.float32),
+        pltpu.SemaphoreType.DMA((2 * PIECES,)),
+        pltpu.SemaphoreType.DMA((PIECES,)),
+    ]
+    (pieces,) = call(split_kernel, "split", [out_shape], [hankel, shifted], scratch, pl.ANY)
     pieces = exchanged(pieces.reshape(2 * groups, rows_dev, LANE), CHANGE)
     ht = pieces.reshape(groups, 2, rows_dev, LANE)
-    (c_part,) = call(
-        columns_kernel, "columns", [(rows, LANE)], [core], [ht, start_basis, other_start]
-    )
+    (c_part,) = call(columns_kernel, "columns", [(rows, LANE)], [ht, start_basis, other_start])
     c = summed_over_chips(c_part, "columns")
-    (x_part,) = call(across_kernel, "across", [(2 * LANE + SUB, LANE)], [], [ht, c])
+    (x_part,) = call(across_kernel, "across", [(2 * LANE + SUB, LANE)], [ht, c])
     x_other = from_other_core(x_part)
-    (yz_part,) = call(image_kernel, "image", [(2 * rows, LANE)], [], [ht, x_part, x_other])
+    (yz_part,) = call(image_kernel, "image", [(2 * rows, LANE)], [ht, x_part, x_other])
     yz = summed_over_chips(yz_part, "image")
     (grams,) = call(
         functools.partial(gram_kernel, half=half),
         "grams",
         [(3 * LANE + half + SUB, LANE)],
-        [place],
         [yz, c, x_part, x_other],
     )
     return call(
         functools.partial(final_kernel, half=half, total=rows_dev * groups),
         "factors",
         [(rows_dev, LANE), (LANE, LANE)],
-        [core],
         [grams, from_other_core(grams)],
     )
 

time: 142 us -> 140 us (0.986)
  blocking collectives: 60.8 us -> 74.1 us
  waiting for transfers between devices: 39 us -> 30.1 us
  starting transfers between devices: 26.6 us -> 22 us
  local copies, waits for them, and re-layouts: 2.08 us -> 0.01 us
    all_to_all x5 -> x6, blocking collectives: 60.8 us -> 74.1 us  [exchanged(): return lax.all_to_all(blocks, axis, 0, 0, tiled=True)]
    all_to_all x2 -> x1, waiting for transfers between devices: 36 us -> 27.1 us  [exchanged(): return lax.all_to_all(blocks, axis, 0, 0, tiled=True)]
    all_to_all x2 -> x1, starting transfers between devices: 17.7 us -> 13.1 us  [exchanged(): return lax.all_to_all(blocks, axis, 0, 0, tiled=True)]
    unnamed x6 -> x2, local copies, waits for them, and re-layouts: 2.08 us -> 0.01 us
  transfers between devices with their start and end apart: 5 -> 4, of which waited for: 5 -> 4; matrix products, arithmetic and copies ran while one was open for 0% -> 0% of each run, Pallas kernels for 0% -> 0%
where the time goes in v4:
time: 140 us
  blocking collectives  74.1 us (53%)
  waiting for transfers between devices  30.1 us (22%)
  starting transfers between devices  22 us (16%)
  Pallas kernels  12.9 us (9%)
    all_to_all x6, blocking collectives, exchanged(): return lax.all_to_all(blocks, axis, 0, 0, tiled=True)  74.1 us
    all_to_all x1, waiting for transfers between devices, exchanged(): return lax.all_to_all(blocks, axis, 0, 0, tiled=True)  27.1 us
    all_to_all x1, starting transfers between devices, exchanged(): return lax.all_to_all(blocks, axis, 0, 0, tiled=True)  13.1 us
    pallas_call x10, Pallas kernels, call(): pl.pallas_call(kernel, name=name, out_shape=[jax.ShapeDtypeStruct(shape,...  12.9 us
    ppermute x3, starting transfers between devices, from_other_core(): return lax.ppermute(value, 'core', [(0, 1), (1, 0)])  8.86 us
    ppermute x3, waiting for transfers between devices, from_other_core(): return lax.ppermute(value, 'core', [(0, 1), (1, 0)])  2.98 us
  transfers between devices with their start and end apart: 4, of which 4 were waited for; matrix products, arithmetic and copies ran while one was open for 0% of the time, Pallas kernels for 0%

profile of v4, /device:TPU:1, one launch (start us, length us, event | category | flops | bytes accessed | tf_op | source)
XLA Modules:
  0.0 139.9 jit_solution(3342487122194999784)
XLA Ops:
  0.6 2.1 %split.1 = f32[32,2,32,128]{3,2,1,0:T(8,128)} custom-call(f32[32,4096]{1,0:T(8,128)} %h_ref.1, f32[32,4096]{1,0:T(8,128)} %t_ref.1), custom_call_target="tpu_custom_call" | custom-call | tf_op jit(solution)/shard_map/split/pallas_call | solution.py:28
  2.7 0.0 copy-start
  2.8 13.1 %all-to-all-start = ((f32[64,32,128]{2,1,0:T(8,128)}), f32[64,32,128]{2,1,0:T(8,128)S(1)}, u32[]{:S(2)}, u32[]{:S(2)}) async-start(f32[64,32,128]{2,1,0:T(8,128)} %bitcast.30), calls=%async_computation | async-start | bytes 2097152 | tf_op jit(solution)/shard_map/all_to_all | solution.py:20
  15.9 0.0 copy-done
  15.9 0.5 collective-permute-start
  16.4 0.9 collective-permute-done.other_ref
  17.4 27.1 %all-to-all-done = f32[64,32,128]{2,1,0:T(8,128)S(1)} async-done(((f32[64,32,128]{2,1,0:T(8,128)}), f32[64,32,128]{2,1,0:T(8,128)S(1)}, u32[]{:S(2)}, u32[]{:S(2)}) %all-to-all-start) | async-done | bytes 1048608 | tf_op jit(solution)/shard_map/all_to_all | solution.py:20
  44.5 0.6 columns.1
  45.1 14.8 %all_to_all.35 = f32[16,32,128]{2,1,0:T(8,128)S(1)} all-to-all(f32[16,32,128]{2,1,0:T(8,128)S(1)} %bitcast.27), channel_id=1, replica_groups=mesh['x'=4,'z'=8,'y'=4,'core'=2] {'x','y'}, dimensions={0} | all-to-all | bytes 524288 | tf_op jit(solution)/shard_map/all_to_all | solution.py:20
  59.8 10.3 %all_to_all.36 = f32[8,32,128]{2,1,0:T(8,128)S(1)} all-to-all(f32[8,32,128]{2,1,0:T(8,128)S(1)} %bitcast.28), channel_id=1, replica_groups=mesh['x'=4,'z'=8,'y'=4,'core'=2] {'z'}, dimensions={0} | all-to-all | bytes 262144 | tf_op jit(solution)/shard_map/all_to_all | solution.py:20
  70.2 10.5 %all_to_all.37 = f32[16,32,128]{2,1,0:T(8,128)S(1)} all-to-all(f32[16,32,128]{2,1,0:T(8,128)S(1)} %bitcast.26), channel_id=1, replica_groups=mesh['x'=4,'z'=8,'y'=4,'core'=2] {'x','y'}, dimensions={0} | all-to-all | bytes 524288 | tf_op jit(solution)/shard_map/all_to_all | solution.py:20
  80.7 0.7 across.1.own_ref
  81.4 3.9 %collective-permute-start.1 = (f32[264,128]{1,0:T(8,128)S(1)}, f32[264,128]{1,0:T(8,128)S(1)}, u32[]{:S(2)}, u32[]{:S(2)}) collective-permute-start(f32[264,128]{1,0:T(8,128)S(1)} %across.1.own_ref), channel_id=1, source_target_pairs={{0,1},{1,0},{2,3},{3,2},{4,5},{5,4},{6,7},{7,6},{8,9},{9,8},{10,11... | collective-permute-start | bytes 405512 | tf_op jit(solution)/shard_map/ppermute | solution.py:24
  85.3 1.0 collective-permute-done.1.other_ref
  86.3 1.0 image.1
  87.3 13.6 %all_to_all.38 = f32[16,64,128]{2,1,0:T(8,128)S(1)} all-to-all(f32[16,64,128]{2,1,0:T(8,128)S(1)} %bitcast.19), channel_id=1, replica_groups=mesh['x'=4,'z'=8,'y'=4,'core'=2] {'x','y'}, dimensions={0} | all-to-all | bytes 1048576 | tf_op jit(solution)/shard_map/all_to_all | solution.py:20
  100.9 11.6 %all_to_all.39 = f32[8,64,128]{2,1,0:T(8,128)S(1)} all-to-all(f32[8,64,128]{2,1,0:T(8,128)S(1)} %bitcast.23), channel_id=1, replica_groups=mesh['x'=4,'z'=8,'y'=4,'core'=2] {'z'}, dimensions={0} | all-to-all | bytes 524288 | tf_op jit(solution)/shard_map/all_to_all | solution.py:20
  112.6 13.3 %all_to_all.40 = f32[16,64,128]{2,1,0:T(8,128)S(1)} all-to-all(f32[16,64,128]{2,1,0:T(8,128)S(1)} %bitcast.22), channel_id=1, replica_groups=mesh['x'=4,'z'=8,'y'=4,'core'=2] {'x','y'}, dimensions={0} | all-to-all | bytes 1048576 | tf_op jit(solution)/shard_map/all_to_all | solution.py:20
  125.9 1.0 grams.1.own_ref
  126.9 4.4 %collective-permute-start.2 = (f32[408,128]{1,0:T(8,128)S(1)}, f32[408,128]{1,0:T(8,128)S(1)}, u32[]{:S(2)}, u32[]{:S(2)}) collective-permute-start(f32[408,128]{1,0:T(8,128)S(1)} %grams.1.own_ref), channel_id=1, source_target_pairs={{0,1},{1,0},{2,3},{3,2},{4,5},{5,4},{6,7},{7,6},{8,9},{9,8},{10,11... | collective-permute-start | bytes 626696 | tf_op jit(solution)/shard_map/ppermute | solution.py:24
  131.3 1.1 collective-permute-done.2.other_ref
  132.4 7.5 %factors.1 = (f32[32,128]{1,0:T(8,128)}, f32[128,128]{1,0:T(8,128)}) custom-call(f32[408,128]{1,0:T(8,128)S(1)} %grams.1.own_ref, f32[408,128]{1,0:T(8,128)S(1)} %collective-permute-done.2.other_ref), custom_call_target="tpu_custom_call" | custom-call | tf_op jit(solution)/shard_map/factors/pallas_call | solution.py:28
  (4 shorter events, 0.1 us)
Async XLA Ops:
  2.7 13.2 %copy-start = (f32[128,128]{1,0:T(8,128)S(1)}, f32[128,128]{1,0:T(8,128)}, u32[]{:S(2)}) copy-start(f32[128,128]{1,0:T(8,128)} %own_ref.1) | copy-start | bytes 196612
  2.8 41.7 %all-to-all-start = ((f32[64,32,128]{2,1,0:T(8,128)}), f32[64,32,128]{2,1,0:T(8,128)S(1)}, u32[]{:S(2)}, u32[]{:S(2)}) async-start(f32[64,32,128]{2,1,0:T(8,128)} %bitcast.30), calls=%async_computation | async-start | bytes 2097152 | tf_op jit(solution)/shard_map/all_to_all | solution.py:20
  15.9 1.4 %collective-permute-start = (f32[128,128]{1,0:T(8,128)S(1)}, f32[128,128]{1,0:T(8,128)S(1)}, u32[]{:S(2)}, u32[]{:S(2)}) collective-permute-start(f32[128,128]{1,0:T(8,128)S(1)} %copy-done), channel_id=1, source_target_pairs={{0,1},{1,0},{2,3},{3,2},{4,5},{5,4},{6,7},{7,6},{8,9},{9,8},{10,11... | collective-permute-start | bytes 196616 | tf_op jit(solution)/shard_map/ppermute | solution.py:24
  81.4 4.9 %collective-permute-start.1 = (f32[264,128]{1,0:T(8,128)S(1)}, f32[264,128]{1,0:T(8,128)S(1)}, u32[]{:S(2)}, u32[]{:S(2)}) collective-permute-start(f32[264,128]{1,0:T(8,128)S(1)} %across.1.own_ref), channel_id=1, source_target_pairs={{0,1},{1,0},{2,3},{3,2},{4,5},{5,4},{6,7},{7,6},{8,9},{9,8},{10,11... | collective-permute-start | bytes 405512 | tf_op jit(solution)/shard_map/ppermute | solution.py:24
  126.9 5.5 %collective-permute-start.2 = (f32[408,128]{1,0:T(8,128)S(1)}, f32[408,128]{1,0:T(8,128)S(1)}, u32[]{:S(2)}, u32[]{:S(2)}) collective-permute-start(f32[408,128]{1,0:T(8,128)S(1)} %grams.1.own_ref), channel_id=1, source_target_pairs={{0,1},{1,0},{2,3},{3,2},{4,5},{5,4},{6,7},{7,6},{8,9},{9,8},{10,11... | collective-permute-start | bytes 626696 | tf_op jit(solution)/shard_map/ppermute | solution.py:24

commit v5 on v4

--- a/solution.py
+++ b/solution.py
@@ -30,7 +30,7 @@
         name=name,
         out_shape=[jax.ShapeDtypeStruct(shape, jnp.float32) for shape in shapes],
         in_specs=[pl.BlockSpec(memory_space=space)] * len(arrays),
-        out_specs=[pl.BlockSpec(memory_space=space)] * len(shapes),
+        out_specs=[pl.BlockSpec(memory_space=pltpu.VMEM)] * len(shapes),
         scratch_shapes=scratch,
         compiler_params=pltpu.CompilerParams(vmem_limit_bytes=(24 if space is pltpu.VMEM else 60) << 20),
     )(*arrays)
@@ -54,14 +54,14 @@
     return jnp.max(jnp.max(jnp.abs(value), axis=0, keepdims=True), axis=1, keepdims=True)
 
 
-def split_kernel(h_ref, t_ref, out_ref, h, t, out, in_sem, out_sem):
-    groups, _, half2, lanes = out.shape
+def split_kernel(h_ref, t_ref, out_ref, h, t, sem):
+    groups, _, half2, lanes = out_ref.shape
     half, some = half2 // 2, groups // PIECES
-    loads, stores = [], []
+    loads = []
     for i in range(PIECES):
         at = slice(i * some * lanes, (i + 1) * some * lanes)
         for j, (source, block) in enumerate(((h_ref, h), (t_ref, t))):
-            load = pltpu.make_async_copy(source.at[:, at], block.at[:, at], in_sem.at[2 * i + j])
+            load = pltpu.make_async_copy(source.at[:, at], block.at[:, at], sem.at[2 * i + j])
             load.start()
             loads.append(load)
     for i in range(PIECES):
@@ -69,15 +69,9 @@
             loads[2 * i + j].wait()
             for g in range(i * some, (i + 1) * some):
                 for part in range(2):
-                    out[g, part, j * half : (j + 1) * half, :] = block[
+                    out_ref[g, part, j * half : (j + 1) * half, :] = block[
                         part * half : (part + 1) * half, g * lanes : (g + 1) * lanes
                     ]
-        at = slice(i * some, (i + 1) * some)
-        store = pltpu.make_async_copy(out.at[at], out_ref.at[at], out_sem.at[i])
-        store.start()
-        stores.append(store)
-    for store in stores:
-        store.wait()
 
 
 def block_of(ht_ref, part, which):
@@ -206,10 +200,13 @@
     gram_w = own_ref[2 * LANE : 3 * LANE, :] * f + other_ref[2 * LANE : 3 * LANE, :] * f_other
     lower, lower_w = inverse_factors([gram, gram_w])
     root = jnp.sqrt(jnp.float32(total))
+    rows = jnp.concatenate(
+        [own_ref[3 * LANE : at, :] * (f * root), other_ref[3 * LANE : at, :] * (f_other * root)]
+    )
+    basis = dot(rows, lower, 1, 1)
     core = lax.axis_index("core")
-    for ref, factor, place in ((own_ref, f, core), (other_ref, f_other, 1 - core)):
-        rows = ref[3 * LANE : at, :] * (factor * root)
-        basis_ref[pl.ds(pl.multiple_of(place * half, half), half), :] = dot(rows, lower, 1, 1)
+    for block, place in ((basis[:half], core), (basis[half:], 1 - core)):
+        basis_ref[pl.ds(pl.multiple_of(place * half, half), half), :] = block
     operator_ref[...] = dot(dot(lower, cross), lower_w, 1, 1) * lax.rsqrt(top)
 
 
@@ -236,11 +233,10 @@
     scratch = [
         pltpu.VMEM(hankel.shape, jnp.float32),
         pltpu.VMEM(hankel.shape, jnp.float32),
-        pltpu.VMEM(out_shape, jnp.float32),
         pltpu.SemaphoreType.DMA((2 * PIECES,)),
-        pltpu.SemaphoreType.DMA((PIECES,)),
     ]
     (pieces,) = call(split_kernel, "split", [out_shape], [hankel, shifted], scratch, pl.ANY)
+    pieces, other_start = lax.optimization_barrier((pieces, other_start))
     pieces = exchanged(pieces.reshape(2 * groups, rows_dev, LANE), CHANGE)
     ht = pieces.reshape(groups, 2, rows_dev, LANE)
     (c_part,) = call(columns_kernel, "columns", [(rows, LANE)], [ht, start_basis, other_start])

time: 140 us -> 140 us (level)
  blocking collectives: 74.1 us -> 113 us
  waiting for transfers between devices: 30.1 us -> 2.08 us
  starting transfers between devices: 22 us -> 11.6 us
    all_to_all x6 -> x7, blocking collectives: 74.1 us -> 113 us  [exchanged(): return lax.all_to_all(blocks, axis, 0, 0, tiled=True)]
    all_to_all x1 -> x0, waiting for transfers between devices: 27.1 us -> none  [exchanged(): return lax.all_to_all(blocks, axis, 0, 0, tiled=True)]
    all_to_all x1 -> x0, starting transfers between devices: 13.1 us -> none  [exchanged(): return lax.all_to_all(blocks, axis, 0, 0, tiled=True)]
    ppermute x3, starting transfers between devices: 8.86 us -> 11.6 us  [from_other_core(): return lax.ppermute(value, 'core', [(0, 1), (1, 0)])]
  transfers between devices with their start and end apart: 4 -> 3, of which waited for: 4 -> 2; matrix products, arithmetic and copies ran while one was open for 0% -> 0% of each run, Pallas kernels for 0% -> 2%
where the time goes in v5:
time: 140 us
  blocking collectives  113 us (81%)
  Pallas kernels  12.8 us (9%)
  starting transfers between devices  11.6 us (8%)
  waiting for transfers between devices  2.08 us (1%)
    all_to_all x7, blocking collectives, exchanged(): return lax.all_to_all(blocks, axis, 0, 0, tiled=True)  113 us
    pallas_call x10, Pallas kernels, call(): pl.pallas_call(kernel, name=name, out_shape=[jax.ShapeDtypeStruct(shape,...  12.8 us
    ppermute x3, starting transfers between devices, from_other_core(): return lax.ppermute(value, 'core', [(0, 1), (1, 0)])  11.6 us
  transfers between devices with their start and end apart: 3, of which 2 were waited for; matrix products, arithmetic and copies ran while one was open for 0% of the time, Pallas kernels for 2%

profile of v5, /device:TPU:1, one launch (start us, length us, event | category | flops | bytes accessed | tf_op | source)
XLA Modules:
  0.0 139.9 jit_solution(17104912747538648156)
XLA Ops:
  0.6 3.3 %collective-permute-start = (f32[128,128]{1,0:T(8,128)}, f32[128,128]{1,0:T(8,128)S(1)}, u32[]{:S(2)}, u32[]{:S(2)}) collective-permute-start(f32[128,128]{1,0:T(8,128)} %own_ref.1), channel_id=1, source_target_pairs={{0,1},{1,0},{2,3},{3,2},{4,5},{5,4},{6,7},{7,6},{8,9},{9,8},{10,11... | collective-permute-start | bytes 196616 | tf_op jit(solution)/shard_map/ppermute | solution.py:24
  4.0 2.3 %split.1 = f32[32,2,32,128]{3,2,1,0:T(8,128)} custom-call(f32[32,4096]{1,0:T(8,128)} %h_ref.1, f32[32,4096]{1,0:T(8,128)} %t_ref.1), custom_call_target="tpu_custom_call" | custom-call | tf_op jit(solution)/shard_map/split/pallas_call | solution.py:28
  6.3 0.0 collective-permute-done.other_ref
  6.3 0.0 copy-start
  6.3 38.6 %all_to_all.35 = f32[64,32,128]{2,1,0:T(8,128)S(1)} all-to-all(f32[64,32,128]{2,1,0:T(8,128)} %bitcast.30), channel_id=1, replica_groups=mesh['x'=4,'z'=8,'y'=4,'core'=2] {'x','z','core'}, dimensions={0} | all-to-all | bytes 2097152 | tf_op jit(solution)/shard_map/all_to_all | solution.py:20
  44.9 0.0 copy-done
  44.9 0.6 columns.1
  45.5 14.8 %all_to_all.36 = f32[16,32,128]{2,1,0:T(8,128)S(1)} all-to-all(f32[16,32,128]{2,1,0:T(8,128)S(1)} %bitcast.27), channel_id=1, replica_groups=mesh['x'=4,'z'=8,'y'=4,'core'=2] {'x','y'}, dimensions={0} | all-to-all | bytes 524288 | tf_op jit(solution)/shard_map/all_to_all | solution.py:20
  60.3 10.3 %all_to_all.37 = f32[8,32,128]{2,1,0:T(8,128)S(1)} all-to-all(f32[8,32,128]{2,1,0:T(8,128)S(1)} %bitcast.28), channel_id=1, replica_groups=mesh['x'=4,'z'=8,'y'=4,'core'=2] {'z'}, dimensions={0} | all-to-all | bytes 262144 | tf_op jit(solution)/shard_map/all_to_all | solution.py:20
  70.6 10.5 %all_to_all.38 = f32[16,32,128]{2,1,0:T(8,128)S(1)} all-to-all(f32[16,32,128]{2,1,0:T(8,128)S(1)} %bitcast.26), channel_id=1, replica_groups=mesh['x'=4,'z'=8,'y'=4,'core'=2] {'x','y'}, dimensions={0} | all-to-all | bytes 524288 | tf_op jit(solution)/shard_map/all_to_all | solution.py:20
  81.1 0.7 across.1.own_ref
  81.8 3.9 %collective-permute-start.1 = (f32[264,128]{1,0:T(8,128)S(1)}, f32[264,128]{1,0:T(8,128)S(1)}, u32[]{:S(2)}, u32[]{:S(2)}) collective-permute-start(f32[264,128]{1,0:T(8,128)S(1)} %across.1.own_ref), channel_id=1, source_target_pairs={{0,1},{1,0},{2,3},{3,2},{4,5},{5,4},{6,7},{7,6},{8,9},{9,8},{10,11... | collective-permute-start | bytes 405512 | tf_op jit(solution)/shard_map/ppermute | solution.py:24
  85.7 1.0 collective-permute-done.1.other_ref
  86.7 1.0 image.1
  87.7 13.6 %all_to_all.39 = f32[16,64,128]{2,1,0:T(8,128)S(1)} all-to-all(f32[16,64,128]{2,1,0:T(8,128)S(1)} %bitcast.19), channel_id=1, replica_groups=mesh['x'=4,'z'=8,'y'=4,'core'=2] {'x','y'}, dimensions={0} | all-to-all | bytes 1048576 | tf_op jit(solution)/shard_map/all_to_all | solution.py:20
  101.3 11.6 %all_to_all.40 = f32[8,64,128]{2,1,0:T(8,128)S(1)} all-to-all(f32[8,64,128]{2,1,0:T(8,128)S(1)} %bitcast.23), channel_id=1, replica_groups=mesh['x'=4,'z'=8,'y'=4,'core'=2] {'z'}, dimensions={0} | all-to-all | bytes 524288 | tf_op jit(solution)/shard_map/all_to_all | solution.py:20
  113.0 13.3 %all_to_all.41 = f32[16,64,128]{2,1,0:T(8,128)S(1)} all-to-all(f32[16,64,128]{2,1,0:T(8,128)S(1)} %bitcast.22), channel_id=1, replica_groups=mesh['x'=4,'z'=8,'y'=4,'core'=2] {'x','y'}, dimensions={0} | all-to-all | bytes 1048576 | tf_op jit(solution)/shard_map/all_to_all | solution.py:20
  126.4 1.0 grams.1.own_ref
  127.3 4.4 %collective-permute-start.2 = (f32[408,128]{1,0:T(8,128)S(1)}, f32[408,128]{1,0:T(8,128)S(1)}, u32[]{:S(2)}, u32[]{:S(2)}) collective-permute-start(f32[408,128]{1,0:T(8,128)S(1)} %grams.1.own_ref), channel_id=1, source_target_pairs={{0,1},{1,0},{2,3},{3,2},{4,5},{5,4},{6,7},{7,6},{8,9},{9,8},{10,11... | collective-permute-start | bytes 626696 | tf_op jit(solution)/shard_map/ppermute | solution.py:24
  131.8 1.1 collective-permute-done.2.other_ref
  132.9 7.0 %factors.1 = (f32[32,128]{1,0:T(8,128)}, f32[128,128]{1,0:T(8,128)}) custom-call(f32[408,128]{1,0:T(8,128)S(1)} %grams.1.own_ref, f32[408,128]{1,0:T(8,128)S(1)} %collective-permute-done.2.other_ref), custom_call_target="tpu_custom_call" | custom-call | tf_op jit(solution)/shard_map/factors/pallas_call | solution.py:28
  (4 shorter events, 0.1 us)
Async XLA Ops:
  0.6 5.7 %collective-permute-start = (f32[128,128]{1,0:T(8,128)}, f32[128,128]{1,0:T(8,128)S(1)}, u32[]{:S(2)}, u32[]{:S(2)}) collective-permute-start(f32[128,128]{1,0:T(8,128)} %own_ref.1), channel_id=1, source_target_pairs={{0,1},{1,0},{2,3},{3,2},{4,5},{5,4},{6,7},{7,6},{8,9},{9,8},{10,11... | collective-permute-start | bytes 196616 | tf_op jit(solution)/shard_map/ppermute | solution.py:24
  6.3 38.6 %copy-start = (f32[128,128]{1,0:T(8,128)S(1)}, f32[128,128]{1,0:T(8,128)}, u32[]{:S(2)}) copy-start(f32[128,128]{1,0:T(8,128)} %own_ref.1) | copy-start | bytes 196612
  81.8 4.9 %collective-permute-start.1 = (f32[264,128]{1,0:T(8,128)S(1)}, f32[264,128]{1,0:T(8,128)S(1)}, u32[]{:S(2)}, u32[]{:S(2)}) collective-permute-start(f32[264,128]{1,0:T(8,128)S(1)} %across.1.own_ref), channel_id=1, source_target_pairs={{0,1},{1,0},{2,3},{3,2},{4,5},{5,4},{6,7},{7,6},{8,9},{9,8},{10,11... | collective-permute-start | bytes 405512 | tf_op jit(solution)/shard_map/ppermute | solution.py:24
  127.3 5.5 %collective-permute-start.2 = (f32[408,128]{1,0:T(8,128)S(1)}, f32[408,128]{1,0:T(8,128)S(1)}, u32[]{:S(2)}, u32[]{:S(2)}) collective-permute-start(f32[408,128]{1,0:T(8,128)S(1)} %grams.1.own_ref), channel_id=1, source_target_pairs={{0,1},{1,0},{2,3},{3,2},{4,5},{5,4},{6,7},{7,6},{8,9},{9,8},{10,11... | collective-permute-start | bytes 626696 | tf_op jit(solution)/shard_map/ppermute | solution.py:24

commit v6 on v4

v6 whole, which is shorter than its diff:
```python
import functools

import jax
import jax.numpy as jnp
from jax import lax
from jax.experimental import pallas as pl
from jax.experimental.pallas import tpu as pltpu
from jax.sharding import Mesh
from jax.sharding import PartitionSpec as P

ROWS = ("x", "z")
COLS = ("y", "core")
PLANE = ("x", "y")
SUB, LANE = 8, 128
PIECES = 4


def exchanged(blocks, axis):
    return lax.all_to_all(blocks, axis, 0, 0, tiled=True)


def from_other_core(value):
    return lax.ppermute(value, "core", [(0, 1), (1, 0)])


def to_second(value):
    return lax.ppermute(value, "core", [(0, 1)])


def call(kernel, name, shapes, arrays, scratch=(), space=pltpu.VMEM):
    return pl.pallas_call(
        kernel,
        name=name,
        out_shape=[jax.ShapeDtypeStruct(shape, jnp.float32) for shape in shapes],
        in_specs=[pl.BlockSpec(memory_space=space)] * len(arrays),
        out_specs=[pl.BlockSpec(memory_space=space)] * len(shapes),
        scratch_shapes=scratch,
        compiler_params=pltpu.CompilerParams(vmem_limit_bytes=(24 if space is pltpu.VMEM else 60) << 20),
    )(*arrays)


def dot(left, right, left_dim=1, right_dim=0):
    return lax.dot_general(
        left,
        right,
        (((left_dim,), (right_dim,)), ((), ())),
        precision=lax.Precision.HIGHEST,
        preferred_element_type=jnp.float32,
    )


def inverse_or_zero(scale):
    return jnp.where(scale > 0, 1.0 / jnp.where(scale > 0, scale, 1.0), 0.0)


def largest(value):
    return jnp.max(jnp.max(jnp.abs(value), axis=0, keepdims=True), axis=1, keepdims=True)


def split_kernel(*refs):
    count = (len(refs) - 4) // 2
    sources, out_ref = refs[:count], refs[count]
    blocks, out, in_sem, out_sem = refs[count + 1 : 2 * count + 1], *refs[2 * count + 1 :]
    groups, _, lanes = out.shape
    some, rows = groups // PIECES, out.shape[1] // count
    loads, stores = [], []
    for i in range(PIECES):
        at = slice(i * some * lanes, (i + 1) * some * lanes)
        for j in range(count):
            load = pltpu.make_async_copy(
                sources[j].at[:, at], blocks[j].at[:, at], in_sem.at[count * i + j]
            )
            load.start()
            loads.append(load)
    for i in range(PIECES):
        for j in range(count):
            loads[count * i + j].wait()
            for g in range(i * some, (i + 1) * some):
                out[g, j * rows : (j + 1) * rows, :] = blocks[j][:, g * lanes : (g + 1) * lanes]
        at = slice(i * some, (i + 1) * some)
        store = pltpu.make_async_copy(out.at[at], out_ref.at[at], out_sem.at[i])
        store.start()
        stores.append(store)
    for store in stores:
        store.wait()


def columns_kernel(own_ref, other_ref, start_ref, start_other_ref, out_ref):
    out_ref[...] = dot(own_ref[...], start_ref[...]) + dot(other_ref[...], start_other_ref[...])


def sum_kernel(in_ref, out_ref, *, rows):
    for at in range(0, rows, SUB):
        tiles = [in_ref[i + at : i + at + SUB, :] for i in range(0, in_ref.shape[0], rows)]
        while len(tiles) > 1:
            tiles = [a + b for a, b in zip(tiles[::2], tiles[1::2])]
        for i in range(0, out_ref.shape[0], rows):
            out_ref[i + at : i + at + SUB, :] = tiles[0]


def across_kernel(own_ref, other_ref, c_ref, x_ref, out_ref, unused_ref):
    c = c_ref[...]
    c = c * inverse_or_zero(largest(c))
    x_ref[:LANE, :] = dot(own_ref[...], c, 0, 0)
    x_ref[LANE:, :] = dot(other_ref[...], c, 0, 0)
    out_ref[...] = c


def image_kernel(own_ref, other_ref, t_ref, x_ref, x_other_ref, out_ref):
    core = lax.axis_index("core")

    @pl.when(core == 0)
    def _():
        x = x_ref[...]
        out_ref[...] = dot(own_ref[...], x[:LANE]) + dot(other_ref[...], x[LANE:])

    @pl.when(core == 1)
    def _():
        x = x_other_ref[...]
        rows = t_ref.shape[1] // 2
        first = t_ref[:, :rows, :].reshape(out_ref.shape)
        second = t_ref[:, rows:, :].reshape(out_ref.shape)
        out_ref[...] = dot(first, x[:LANE]) + dot(second, x[LANE:])


def inverse_factors(matrices):
    size = matrices[0].shape[0]
    blocks = size // SUB
    lane = lax.broadcasted_iota(jnp.int32, (SUB, size), 1)
    sub = lax.broadcasted_iota(jnp.int32, (SUB, size), 0)
    work = [[m[SUB * i : SUB * (i + 1), :] for i in range(blocks)] for m in matrices]

    def columns(rows, low):
        return [
            jnp.broadcast_to(rows[:, low + j : low + j + 1], (SUB, size)) for j in range(SUB)
        ]

    def row(values, j):
        return jnp.broadcast_to(values[j : j + 1, :], (SUB, size))

    for k in range(blocks):
        low = SUB * k
        inside = (lane >= low) & (lane < low + SUB)
        done = []
        for mine in work:
            column = columns(mine[k], low)
            w = jnp.where(inside, (lane == sub + low).astype(jnp.float32), mine[k])
            steps, pivots = [], jnp.ones((SUB, size), jnp.float32)
            for j in range(SUB):
                pivot = row(column[j], j)
                inverse = 1.0 / pivot
                pivots = jnp.where(sub == j, pivot, pivots)
                factor = jnp.where(sub > j, column[j] * inverse, 0.0)
                ahead = {}
                for i in range(j + 1, SUB):
                    ahead[i] = row(column[i], j)
                    column[i] = column[i] - factor * ahead[i]
                reduced = row(w, j)
                w = w - factor * reduced
                steps.append((inverse, ahead, reduced))
            root = lax.rsqrt(pivots)
            root = root * (1.5 - 0.5 * pivots * root * root)
            mine[k] = jnp.where(lane <= sub + low, w * root, 0.0)
            done.append(steps)
        for mine, steps in zip(work, done):
            for i in range(k + 1, blocks):
                column = columns(mine[i], low)
                w = jnp.where(inside, 0.0, mine[i])
                for j, (inverse, ahead, reduced) in enumerate(steps):
                    factor = column[j] * inverse
                    for n in range(j + 1, SUB):
                        column[n] = column[n] - factor * ahead[n]
                    w = w - factor * reduced
                mine[i] = w
    return [jnp.concatenate(mine, axis=0) for mine in work]


def final_kernel(own_ref, other_ref, c_ref, c_other_ref, basis_ref, operator_ref, y_ref):
    first = lax.axis_index("core") == 0
    y = jnp.where(first, own_ref[...], other_ref[...])
    z = jnp.where(first, other_ref[...], own_ref[...])
    c = jnp.where(first, c_ref[...], c_other_ref[...])
    scale = largest(y)
    y = y * inverse_or_zero(scale)
    y_ref[...] = y
    lower, lower_w = inverse_factors([dot(y, y, 0, 0), dot(c, y, 0, 0)])
    cross = dot(y, z, 0, 0)
    rows, total = basis_ref.shape[0], y_ref.shape[0]
    place = lax.axis_index("x") * lax.axis_size("z") + lax.axis_index("z")
    mine = y_ref[pl.ds(pl.multiple_of(place * rows, rows), rows), :]
    basis_ref[...] = dot(mine * jnp.sqrt(jnp.float32(total)), lower, 1, 1)
    operator_ref[...] = dot(dot(lower, cross), lower_w, 1, 1) * lax.rsqrt(scale)


def exchanged_rows(values, axis):
    count = lax.axis_size(axis)
    return exchanged(values.reshape(count, -1, LANE), axis).reshape(values.shape)


def summed_over_chips(part, name):
    rows = part.shape[0] // lax.axis_size(PLANE)
    kernel = functools.partial(sum_kernel, rows=rows)
    line = (lax.axis_size("z") * rows, LANE)
    (copies,) = call(kernel, name + "_plane", [line], [exchanged_rows(part, PLANE)])
    (copies,) = call(kernel, name + "_line", [part.shape], [exchanged_rows(copies, "z")])
    return exchanged_rows(copies, PLANE)


def split(name, *sources):
    rows, cols = sources[0].shape
    shape = (lax.axis_size(ROWS), len(sources) * rows, LANE)
    scratch = [pltpu.VMEM((rows, cols), jnp.float32)] * len(sources) + [
        pltpu.VMEM(shape, jnp.float32),
        pltpu.SemaphoreType.DMA((len(sources) * PIECES,)),
        pltpu.SemaphoreType.DMA((PIECES,)),
    ]
    return call(split_kernel, name, [shape], sources, scratch, pl.ANY)[0]


def on_device(hankel, shifted, start_basis):
    groups, rows_dev = lax.axis_size(ROWS), hankel.shape[0]
    rows = groups * rows_dev
    start_other = from_other_core(start_basis)
    shifted_other = to_second(shifted)
    own = exchanged(split("split", hankel), ROWS).reshape(rows, LANE)
    other = lax.ppermute(own, "core", [(1, 0)])
    both = (groups, 2 * rows_dev, LANE)

    def project(own, other, start_basis, start_other, shifted, shifted_other):
        (c_part,) = call(
            columns_kernel, "columns", [(rows, LANE)], [own, other, start_basis, start_other]
        )
        c = summed_over_chips(c_part, "columns")
        shapes = [(2 * LANE, LANE), (rows, LANE), both]
        return tuple(call(across_kernel, "across", shapes, [own, other, c]))

    def relay(own, other, start_basis, start_other, shifted, shifted_other):
        t = exchanged(split("split_shifted", shifted_other, shifted), ROWS)
        return jnp.zeros((2 * LANE, LANE), jnp.float32), jnp.zeros((rows, LANE), jnp.float32), t

    x, c, t = lax.cond(
        lax.axis_index("core") == 0, project, relay,
        own, other, start_basis, start_other, shifted, shifted_other,
    )
    x_other, c_other = to_second(x), to_second(c)
    (part,) = call(image_kernel, "image", [(rows, LANE)], [own, other, t, x, x_other])
    part = summed_over_chips(part, "image")
    return call(
        final_kernel,
        "factors",
        [(rows_dev, LANE), (LANE, LANE)],
        [part, from_other_core(part), c, c_other],
        [pltpu.VMEM((rows, LANE), jnp.float32)],
    )


def solution(mesh):
    finer = Mesh(mesh.devices.reshape(4, 8, 4, 2), ("x", "z", "y", "core"))
    placed = (P(ROWS, COLS), P(ROWS, COLS), P((*COLS, *ROWS), None))

    def whole(*blocks):
        return tuple(on_device(*blocks))

    return jax.shard_map(
        whole, mesh=finer, in_specs=placed, out_specs=(P(ROWS, None), P()), check_vma=False
    )
```

time: 140 us -> 141 us (level)
  blocking collectives: 74.1 us -> 47.4 us
  waiting for transfers between devices: 30.1 us -> 48.4 us
  starting transfers between devices: 22 us -> 30.3 us
    all_to_all x6 -> x3, blocking collectives: 74.1 us -> 47.4 us  [exchanged(): return lax.all_to_all(blocks, axis, 0, 0, tiled=True)]
    ppermute x0 -> x4, waiting for transfers between devices: none -> 24.7 us  [the longest x3 24.7 us: to_second(): return lax.ppermute(value, 'core', [(0, 1)])]
    ppermute x0 -> x4, starting transfers between devices: none -> 9.31 us  [the longest x1 5.43 us: on_device(): other = lax.ppermute(own, 'core', [(1, 0)])]
    all_to_all x1 -> x2, waiting for transfers between devices: 27.1 us -> 20.7 us  [exchanged(): return lax.all_to_all(blocks, axis, 0, 0, tiled=True)]
    ppermute x3 -> x2, starting transfers between devices: 8.86 us -> 4.24 us  [from_other_core(): return lax.ppermute(value, 'core', [(0, 1), (1, 0)])]
    all_to_all x1 -> x2, starting transfers between devices: 13.1 us -> 16.8 us  [exchanged(): return lax.all_to_all(blocks, axis, 0, 0, tiled=True)]
    pallas_call x10 -> x6, Pallas kernels: 12.9 us -> 13.5 us  [call(): pl.pallas_call(kernel, name=name, out_shape=[jax.ShapeDtypeStruct(shape,...]
    ppermute x3 -> x2, waiting for transfers between devices: 2.98 us -> 2.99 us  [from_other_core(): return lax.ppermute(value, 'core', [(0, 1), (1, 0)])]
  transfers between devices with their start and end apart: 4 -> 8, of which waited for: 4 -> 5; matrix products, arithmetic and copies ran while one was open for 0% -> 0% of each run, Pallas kernels for 0% -> 0%
where the time goes in v6:
time: 141 us; the launch traced here: 140 us
  waiting for transfers between devices  48.4 us (34%)
  blocking collectives  47.4 us (34%)
  starting transfers between devices  30.3 us (21%)
  Pallas kernels  13.5 us (10%)
    all_to_all x3, blocking collectives, exchanged(): return lax.all_to_all(blocks, axis, 0, 0, tiled=True)  47.4 us
    ppermute x3, waiting for transfers between devices, to_second(): return lax.ppermute(value, 'core', [(0, 1)])  24.7 us
    all_to_all x2, waiting for transfers between devices, exchanged(): return lax.all_to_all(blocks, axis, 0, 0, tiled=True)  20.7 us
    all_to_all x2, starting transfers between devices, exchanged(): return lax.all_to_all(blocks, axis, 0, 0, tiled=True)  16.8 us
    pallas_call x6, Pallas kernels, call(): pl.pallas_call(kernel, name=name, out_shape=[jax.ShapeDtypeStruct(shape,...  13.5 us
    ppermute x1, starting transfers between devices, on_device(): other = lax.ppermute(own, 'core', [(1, 0)])  5.43 us
    ppermute x2, starting transfers between devices, from_other_core(): return lax.ppermute(value, 'core', [(0, 1), (1, 0)])  4.24 us
    ppermute x3, starting transfers between devices, to_second(): return lax.ppermute(value, 'core', [(0, 1)])  3.88 us
  transfers between devices with their start and end apart: 8, of which 5 were waited for; matrix products, arithmetic and copies ran while one was open for 0% of the time, Pallas kernels for 0%

profile of v6, /device:TPU:1, one launch (start us, length us, event | category | flops | bytes accessed | tf_op | source)
XLA Modules:
  0.0 140.4 jit_solution(16308508038176245821)
XLA Ops:
  0.6 1.8 %split.1 = f32[32,32,128]{2,1,0:T(8,128)} custom-call(f32[32,4096]{1,0:T(8,128)} %refs_0_.1), custom_call_target="tpu_custom_call" | custom-call | tf_op jit(solution)/shard_map/split/pallas_call | solution.py:31
  2.4 0.0 copy-start
  2.5 0.0 copy-start.1
  2.5 12.0 %all-to-all-start.4 = ((f32[32,32,128]{2,1,0:T(8,128)}), f32[32,32,128]{2,1,0:T(8,128)S(1)}, u32[]{:S(2)}, u32[]{:S(2)}) async-start(f32[32,32,128]{2,1,0:T(8,128)} %split.1), calls=%async_computation.4 | async-start | bytes 1048576 | tf_op jit(solution)/shard_map/all_to_all | solution.py:19
  14.5 0.0 copy-done
  14.5 1.3 collective-permute-start.1
  15.8 13.0 %all-to-all-done.4 = f32[32,32,128]{2,1,0:T(8,128)S(1)} async-done(((f32[32,32,128]{2,1,0:T(8,128)}), f32[32,32,128]{2,1,0:T(8,128)S(1)}, u32[]{:S(2)}, u32[]{:S(2)}) %all-to-all-start.4) | async-done | bytes 524320 | tf_op jit(solution)/shard_map/all_to_all | solution.py:19
  28.8 5.4 %collective-permute-start = (f32[1024,128]{1,0:T(8,128)S(1)}, f32[1024,128]{1,0:T(8,128)S(1)}, u32[]{:S(2)}, u32[]{:S(2)}) collective-permute-start(f32[1024,128]{1,0:T(8,128)S(1)} %bitcast.25), channel_id=1, source_target_pairs={{1,0},{3,2},{5,4},{7,6},{9,8},{11,10},{13,12},{15,14},{17,16},{19,... | collective-permute-start | bytes 1572872 | tf_op jit(solution)/shard_map/ppermute | solution.py:226
  34.2 0.0 copy-done.1
  34.3 0.1 collective-permute-start.2
  34.4 0.0 collective-permute-done.1
  34.4 1.5 %collective-permute-done.2 = f32[128,128]{1,0:T(8,128)S(1)} collective-permute-done((f32[128,128]{1,0:T(8,128)S(1)}, f32[128,128]{1,0:T(8,128)S(1)}, u32[]{:S(2)}, u32[]{:S(2)}) %collective-permute-start.2) | collective-permute-done | bytes 65568 | tf_op jit(solution)/shard_map/ppermute | solution.py:23
  35.8 0.0 collective-permute-done.other_ref
  35.8 23.8 %conditional.1 = ((f32[256,128]{1,0:T(8,128)S(1)}, f32[1024,128]{1,0:T(8,128)S(1)}, f32[32,64,128]{2,1,0:T(8,128)S(1)})) conditional(s32[]{:T(128)} %convert_element_type.3, (f32[32,4096]{1,0:T(8,128)S(1)}, f32[32,4096]{1,0:T(8,128)S(1)}) %tuple.21, (f32[1024,128]{1,0:T(8,128)S(1)}, f32[1024,128]{1,0:T(8,128)S(1)}, f32[128,128]{1,0:T(8,128)S(1)}, ...), branch_computations={%region_0.0_spmd, %region_1.0_spmd} | conditional | bytes 2752552 | solution.py:241
  35.8 1.4 %split_shifted.1 = f32[32,64,128]{2,1,0:T(8,128)} custom-call(f32[32,4096]{1,0:T(8,128)S(1)} %get-tuple-element.12.refs_0_, f32[32,4096]{1,0:T(8,128)S(1)} %get-tuple-element.13.refs_1_), custom_call_target="tpu_custom_call" | custom-call | tf_op jit(solution)/shard_map/cond/branch_0_fun/split_shifted/pallas_call | solution.py:31
  37.3 22.3 %all_to_all.36 = f32[32,64,128]{2,1,0:T(8,128)S(1)} all-to-all(f32[32,64,128]{2,1,0:T(8,128)} %split_shifted.1), channel_id=1, replica_groups=mesh['x'=4,'z'=8,'y'=4,'core'=2] {'x','z'}, dimensions={0} | all-to-all | bytes 2097152 | tf_op jit(solution)/shard_map/cond/branch_0_fun/all_to_all | solution.py:19
  59.7 1.3 collective-permute-start.3
  61.0 24.7 %collective-permute-done.3.x_other_ref = f32[256,128]{1,0:T(8,128)S(1)} collective-permute-done((f32[256,128]{1,0:T(8,128)S(1)}, f32[256,128]{1,0:T(8,128)S(1)}, u32[]{:S(2)}, u32[]{:S(2)}) %collective-permute-start.3) | collective-permute-done | bytes 131104 | tf_op jit(solution)/shard_map/ppermute | solution.py:27
  85.7 1.0 image.1
  86.7 13.2 %all_to_all.40 = f32[16,64,128]{2,1,0:T(8,128)S(1)} all-to-all(f32[16,64,128]{2,1,0:T(8,128)S(1)} %bitcast.20), channel_id=1, replica_groups=mesh['x'=4,'z'=8,'y'=4,'core'=2] {'x','y'}, dimensions={0} | all-to-all | bytes 1048576 | tf_op jit(solution)/shard_map/all_to_all | solution.py:19
  99.9 11.9 %all_to_all.41 = f32[8,64,128]{2,1,0:T(8,128)S(1)} all-to-all(f32[8,64,128]{2,1,0:T(8,128)S(1)} %bitcast.23), channel_id=1, replica_groups=mesh['x'=4,'z'=8,'y'=4,'core'=2] {'z'}, dimensions={0} | all-to-all | bytes 524288 | tf_op jit(solution)/shard_map/all_to_all | solution.py:19
  111.8 0.8 image_line.1
  112.6 4.8 %all-to-all-start.7 = ((f32[16,64,128]{2,1,0:T(8,128)}), f32[16,64,128]{2,1,0:T(8,128)S(1)}, u32[]{:S(2)}, u32[]{:S(2)}) async-start(f32[16,64,128]{2,1,0:T(8,128)} %bitcast.11), calls=%async_computation.7 | async-start | bytes 1048576 | tf_op jit(solution)/shard_map/all_to_all | solution.py:19
  117.4 1.3 collective-permute-start.5
  118.7 7.6 %all-to-all-done.7 = f32[16,64,128]{2,1,0:T(8,128)S(1)} async-done(((f32[16,64,128]{2,1,0:T(8,128)}), f32[16,64,128]{2,1,0:T(8,128)S(1)}, u32[]{:S(2)}, u32[]{:S(2)}) %all-to-all-start.7) | async-done | bytes 524320 | tf_op jit(solution)/shard_map/all_to_all | solution.py:19
  126.4 4.2 %collective-permute-start.4 = (f32[1024,128]{1,0:T(8,128)S(1)}, f32[1024,128]{1,0:T(8,128)S(1)}, u32[]{:S(2)}, u32[]{:S(2)}) collective-permute-start(f32[1024,128]{1,0:T(8,128)S(1)} %bitcast.18), channel_id=1, source_target_pairs={{0,1},{1,0},{2,3},{3,2},{4,5},{5,4},{6,7},{7,6},{8,9},{9,8},{10,11... | collective-permute-start | bytes 1572872 | tf_op jit(solution)/shard_map/ppermute | solution.py:23
  130.5 0.0 collective-permute-done.5.c_other_ref
  130.5 1.5 %collective-permute-done.4.other_ref = f32[1024,128]{1,0:T(8,128)S(1)} collective-permute-done((f32[1024,128]{1,0:T(8,128)S(1)}, f32[1024,128]{1,0:T(8,128)S(1)}, u32[]{:S(2)}, u32[]{:S(2)}) %collective-permute-start.4) | collective-permute-done | bytes 524320 | tf_op jit(solution)/shard_map/ppermute | solution.py:23
  132.1 8.4 %factors.1 = (f32[32,128]{1,0:T(8,128)}, f32[128,128]{1,0:T(8,128)}) custom-call(f32[1024,128]{1,0:T(8,128)S(1)} %bitcast.19, f32[1024,128]{1,0:T(8,128)S(1)} %collective-permute-done.4.other_ref, f32[1024,128]{1,0:T(8,128)S(1)} %get-tuple-element.25.c_ref, f32[1024,128]{1,0:T(8,128)S(1)} %collective-permute-done.5.c_other_ref), custom_call_target="tpu_custom_call" | custom-call | tf_op jit(solution)/shard_map/factors/pallas_call | solution.py:31
  (3 shorter events, 0.1 us)
Async XLA Ops:
  2.4 12.0 %copy-start = (f32[32,4096]{1,0:T(8,128)S(1)}, f32[32,4096]{1,0:T(8,128)}, u32[]{:S(2)}) copy-start(f32[32,4096]{1,0:T(8,128)} %param.6) | copy-start | bytes 1572868
  2.5 31.8 %copy-start.1 = (f32[128,128]{1,0:T(8,128)S(1)}, f32[128,128]{1,0:T(8,128)}, u32[]{:S(2)}) copy-start(f32[128,128]{1,0:T(8,128)} %param.7) | copy-start | bytes 196612
  2.5 26.3 %all-to-all-start.4 = ((f32[32,32,128]{2,1,0:T(8,128)}), f32[32,32,128]{2,1,0:T(8,128)S(1)}, u32[]{:S(2)}, u32[]{:S(2)}) async-start(f32[32,32,128]{2,1,0:T(8,128)} %split.1), calls=%async_computation.4 | async-start | bytes 1048576 | tf_op jit(solution)/shard_map/all_to_all | solution.py:19
  14.5 19.9 %collective-permute-start.1 = (f32[32,4096]{1,0:T(8,128)S(1)}, f32[32,4096]{1,0:T(8,128)S(1)}, u32[]{:S(2)}, u32[]{:S(2)}) collective-permute-start(f32[32,4096]{1,0:T(8,128)S(1)} %copy-done), channel_id=1, source_target_pairs={{0,1},{2,3},{4,5},{6,7},{8,9},{10,11},{12,13},{14,15},{16,17},{18,... | collective-permute-start | bytes 1572872 | tf_op jit(solution)/shard_map/ppermute | solution.py:27
  28.8 7.0 %collective-permute-start = (f32[1024,128]{1,0:T(8,128)S(1)}, f32[1024,128]{1,0:T(8,128)S(1)}, u32[]{:S(2)}, u32[]{:S(2)}) collective-permute-start(f32[1024,128]{1,0:T(8,128)S(1)} %bitcast.25), channel_id=1, source_target_pairs={{1,0},{3,2},{5,4},{7,6},{9,8},{11,10},{13,12},{15,14},{17,16},{19,... | collective-permute-start | bytes 1572872 | tf_op jit(solution)/shard_map/ppermute | solution.py:226
  34.3 1.6 %collective-permute-start.2 = (f32[128,128]{1,0:T(8,128)S(1)}, f32[128,128]{1,0:T(8,128)S(1)}, u32[]{:S(2)}, u32[]{:S(2)}) collective-permute-start(f32[128,128]{1,0:T(8,128)S(1)} %copy-done.1), channel_id=1, source_target_pairs={{0,1},{1,0},{2,3},{3,2},{4,5},{5,4},{6,7},{7,6},{8,9},{9,8},{10,11... | collective-permute-start | bytes 196616 | tf_op jit(solution)/shard_map/ppermute | solution.py:23
  59.7 26.0 %collective-permute-start.3 = (f32[256,128]{1,0:T(8,128)S(1)}, f32[256,128]{1,0:T(8,128)S(1)}, u32[]{:S(2)}, u32[]{:S(2)}) collective-permute-start(f32[256,128]{1,0:T(8,128)S(1)} %get-tuple-element.24.x_ref), channel_id=1, source_target_pairs={{0,1},{2,3},{4,5},{6,7},{8,9},{10,11},{12,13},{14,15},{16,17},{18,... | collective-permute-start | bytes 393224 | tf_op jit(solution)/shard_map/ppermute | solution.py:27
  112.6 13.7 %all-to-all-start.7 = ((f32[16,64,128]{2,1,0:T(8,128)}), f32[16,64,128]{2,1,0:T(8,128)S(1)}, u32[]{:S(2)}, u32[]{:S(2)}) async-start(f32[16,64,128]{2,1,0:T(8,128)} %bitcast.11), calls=%async_computation.7 | async-start | bytes 1048576 | tf_op jit(solution)/shard_map/all_to_all | solution.py:19
  117.4 13.1 %collective-permute-start.5 = (f32[1024,128]{1,0:T(8,128)S(1)}, f32[1024,128]{1,0:T(8,128)S(1)}, u32[]{:S(2)}, u32[]{:S(2)}) collective-permute-start(f32[1024,128]{1,0:T(8,128)S(1)} %get-tuple-element.25.c_ref), channel_id=1, source_target_pairs={{0,1},{2,3},{4,5},{6,7},{8,9},{10,11},{12,13},{14,15},{16,17},{18,... | collective-permute-start | bytes 1572872 | tf_op jit(solution)/shard_map/ppermute | solution.py:27
  126.4 5.7 %collective-permute-start.4 = (f32[1024,128]{1,0:T(8,128)S(1)}, f32[1024,128]{1,0:T(8,128)S(1)}, u32[]{:S(2)}, u32[]{:S(2)}) collective-permute-start(f32[1024,128]{1,0:T(8,128)S(1)} %bitcast.18), channel_id=1, source_target_pairs={{0,1},{1,0},{2,3},{3,2},{4,5},{5,4},{6,7},{7,6},{8,9},{9,8},{10,11... | collective-permute-start | bytes 1572872 | tf_op jit(solution)/shard_map/ppermute | solution.py:23

commit v7 on v6

--- a/solution.py
+++ b/solution.py
@@ -222,8 +222,9 @@
     rows = groups * rows_dev
     start_other = from_other_core(start_basis)
     shifted_other = to_second(shifted)
-    own = exchanged(split("split", hankel), ROWS).reshape(rows, LANE)
-    other = lax.ppermute(own, "core", [(1, 0)])
+    pieces, start_other = lax.optimization_barrier((split("split", hankel), start_other))
+    own = exchanged(pieces, ROWS).reshape(rows, LANE)
+    other = from_other_core(own)
     both = (groups, 2 * rows_dev, LANE)
 
     def project(own, other, start_basis, start_other, shifted, shifted_other):
@@ -242,7 +243,7 @@
         lax.axis_index("core") == 0, project, relay,
         own, other, start_basis, start_other, shifted, shifted_other,
     )
-    x_other, c_other = to_second(x), to_second(c)
+    x_other, c_other = from_other_core(x), to_second(c)
     (part,) = call(image_kernel, "image", [(rows, LANE)], [own, other, t, x, x_other])
     part = summed_over_chips(part, "image")
     return call(

time: 141 us -> 139 us (0.986)
  waiting for transfers between devices: 48.4 us -> 25.3 us
  starting transfers between devices: 30.3 us -> 51.5 us
    ppermute x2 -> x4, starting transfers between devices: 4.24 us -> 34.9 us  [from_other_core(): return lax.ppermute(value, 'core', [(0, 1), (1, 0)])]
    ppermute x3 -> x2, waiting for transfers between devices: 24.7 us -> 0.01 us  [to_second(): return lax.ppermute(value, 'core', [(0, 1)])]
    ppermute x1 -> x0, starting transfers between devices: 5.43 us -> none  [on_device(): other = lax.ppermute(own, 'core', [(1, 0)])]
    all_to_all x2, starting transfers between devices: 16.8 us -> 14 us  [exchanged(): return lax.all_to_all(blocks, axis, 0, 0, tiled=True)]
    ppermute x3 -> x2, starting transfers between devices: 3.88 us -> 2.58 us  [to_second(): return lax.ppermute(value, 'core', [(0, 1)])]
    ppermute x2 -> x4, waiting for transfers between devices: 2.99 us -> 4.06 us  [from_other_core(): return lax.ppermute(value, 'core', [(0, 1), (1, 0)])]
  transfers between devices with their start and end apart: 8 -> 8, of which waited for: 5 -> 5; matrix products, arithmetic and copies ran while one was open for 0% -> 0% of each run, Pallas kernels for 0% -> 1%
where the time goes in v7:
time: 139 us
  starting transfers between devices  51.5 us (37%)
  blocking collectives  47.4 us (34%)
  waiting for transfers between devices  25.3 us (18%)
  Pallas kernels  13.5 us (10%)
    all_to_all x3, blocking collectives, exchanged(): return lax.all_to_all(blocks, axis, 0, 0, tiled=True)  47.4 us
    ppermute x4, starting transfers between devices, from_other_core(): return lax.ppermute(value, 'core', [(0, 1), (1, 0)])  34.9 us
    all_to_all x2, waiting for transfers between devices, exchanged(): return lax.all_to_all(blocks, axis, 0, 0, tiled=True)  21.2 us
    all_to_all x2, starting transfers between devices, exchanged(): return lax.all_to_all(blocks, axis, 0, 0, tiled=True)  14 us
    pallas_call x6, Pallas kernels, call(): pl.pallas_call(kernel, name=name, out_shape=[jax.ShapeDtypeStruct(shape,...  13.5 us
    ppermute x4, waiting for transfers between devices, from_other_core(): return lax.ppermute(value, 'core', [(0, 1), (1, 0)])  4.06 us
  transfers between devices with their start and end apart: 8, of which 5 were waited for; matrix products, arithmetic and copies ran while one was open for 0% of the time, Pallas kernels for 1%

profile of v7, /device:TPU:1, one launch (start us, length us, event | category | flops | bytes accessed | tf_op | source)
XLA Modules:
  0.0 138.5 jit_solution(6445533930262585860)
XLA Ops:
  0.6 3.3 %collective-permute-start = (f32[128,128]{1,0:T(8,128)}, f32[128,128]{1,0:T(8,128)S(1)}, u32[]{:S(2)}, u32[]{:S(2)}) collective-permute-start(f32[128,128]{1,0:T(8,128)} %param.7), channel_id=1, source_target_pairs={{0,1},{1,0},{2,3},{3,2},{4,5},{5,4},{6,7},{7,6},{8,9},{9,8},{10,11... | collective-permute-start | bytes 196616 | tf_op jit(solution)/shard_map/ppermute | solution.py:23
  4.0 1.8 %split.1 = f32[32,32,128]{2,1,0:T(8,128)} custom-call(f32[32,4096]{1,0:T(8,128)} %refs_0_.1), custom_call_target="tpu_custom_call" | custom-call | tf_op jit(solution)/shard_map/split/pallas_call | solution.py:31
  5.8 0.0 copy-start
  5.8 0.0 copy-start.1
  5.8 0.0 collective-permute-done
  5.8 9.4 %all-to-all-start.4 = ((f32[32,32,128]{2,1,0:T(8,128)}), f32[32,32,128]{2,1,0:T(8,128)S(1)}, u32[]{:S(2)}, u32[]{:S(2)}) async-start(f32[32,32,128]{2,1,0:T(8,128)} %split.1), calls=%async_computation.4 | async-start | bytes 1048576 | tf_op jit(solution)/shard_map/all_to_all | solution.py:19
  15.3 0.0 copy-done
  15.3 1.3 collective-permute-start.2
  16.6 13.6 %all-to-all-done.4 = f32[32,32,128]{2,1,0:T(8,128)S(1)} async-done(((f32[32,32,128]{2,1,0:T(8,128)}), f32[32,32,128]{2,1,0:T(8,128)S(1)}, u32[]{:S(2)}, u32[]{:S(2)}) %all-to-all-start.4) | async-done | bytes 524320 | tf_op jit(solution)/shard_map/all_to_all | solution.py:19
  30.1 2.8 %collective-permute-start.1 = (f32[1024,128]{1,0:T(8,128)S(1)}, f32[1024,128]{1,0:T(8,128)S(1)}, u32[]{:S(2)}, u32[]{:S(2)}) collective-permute-start(f32[1024,128]{1,0:T(8,128)S(1)} %bitcast.25), channel_id=1, source_target_pairs={{0,1},{1,0},{2,3},{3,2},{4,5},{5,4},{6,7},{7,6},{8,9},{9,8},{10,11... | collective-permute-start | bytes 1572872 | tf_op jit(solution)/shard_map/ppermute | solution.py:23
  33.0 0.0 collective-permute-done.2
  33.0 1.5 %collective-permute-done.1.other_ref = f32[1024,128]{1,0:T(8,128)S(1)} collective-permute-done((f32[1024,128]{1,0:T(8,128)S(1)}, f32[1024,128]{1,0:T(8,128)S(1)}, u32[]{:S(2)}, u32[]{:S(2)}) %collective-permute-start.1) | collective-permute-done | bytes 524320 | tf_op jit(solution)/shard_map/ppermute | solution.py:23
  34.5 0.0 copy-done.1
  34.5 23.9 %conditional.1 = ((f32[256,128]{1,0:T(8,128)S(1)}, f32[1024,128]{1,0:T(8,128)S(1)}, f32[32,64,128]{2,1,0:T(8,128)S(1)})) conditional(s32[]{:T(128)} %convert_element_type.3, (f32[32,4096]{1,0:T(8,128)S(1)}, f32[32,4096]{1,0:T(8,128)S(1)}) %tuple.23, (f32[1024,128]{1,0:T(8,128)S(1)}, f32[1024,128]{1,0:T(8,128)S(1)}, f32[128,128]{1,0:T(8,128)S(1)}, ...), branch_computations={%region_0.0_spmd, %region_1.0_spmd} | conditional | bytes 2752552 | solution.py:242
  34.5 1.4 %split_shifted.1 = f32[32,64,128]{2,1,0:T(8,128)} custom-call(f32[32,4096]{1,0:T(8,128)S(1)} %get-tuple-element.12.refs_0_, f32[32,4096]{1,0:T(8,128)S(1)} %get-tuple-element.13.refs_1_), custom_call_target="tpu_custom_call" | custom-call | tf_op jit(solution)/shard_map/cond/branch_0_fun/split_shifted/pallas_call | solution.py:31
  35.9 22.4 %all_to_all.36 = f32[32,64,128]{2,1,0:T(8,128)S(1)} all-to-all(f32[32,64,128]{2,1,0:T(8,128)} %split_shifted.1), channel_id=1, replica_groups=mesh['x'=4,'z'=8,'y'=4,'core'=2] {'x','z'}, dimensions={0} | all-to-all | bytes 2097152 | tf_op jit(solution)/shard_map/cond/branch_0_fun/all_to_all | solution.py:19
  58.4 24.6 %collective-permute-start.3 = (f32[256,128]{1,0:T(8,128)S(1)}, f32[256,128]{1,0:T(8,128)S(1)}, u32[]{:S(2)}, u32[]{:S(2)}) collective-permute-start(f32[256,128]{1,0:T(8,128)S(1)} %get-tuple-element.28.x_ref), channel_id=1, source_target_pairs={{0,1},{1,0},{2,3},{3,2},{4,5},{5,4},{6,7},{7,6},{8,9},{9,8},{10,11... | collective-permute-start | bytes 393224 | tf_op jit(solution)/shard_map/ppermute | solution.py:23
  83.0 1.0 collective-permute-done.3.x_other_ref
  84.0 1.0 image.1
  85.0 13.3 %all_to_all.40 = f32[16,64,128]{2,1,0:T(8,128)S(1)} all-to-all(f32[16,64,128]{2,1,0:T(8,128)S(1)} %bitcast.20), channel_id=1, replica_groups=mesh['x'=4,'z'=8,'y'=4,'core'=2] {'x','y'}, dimensions={0} | all-to-all | bytes 1048576 | tf_op jit(solution)/shard_map/all_to_all | solution.py:19
  98.4 11.6 %all_to_all.41 = f32[8,64,128]{2,1,0:T(8,128)S(1)} all-to-all(f32[8,64,128]{2,1,0:T(8,128)S(1)} %bitcast.23), channel_id=1, replica_groups=mesh['x'=4,'z'=8,'y'=4,'core'=2] {'z'}, dimensions={0} | all-to-all | bytes 524288 | tf_op jit(solution)/shard_map/all_to_all | solution.py:19
  110.1 0.8 image_line.1
  110.9 4.6 %all-to-all-start.7 = ((f32[16,64,128]{2,1,0:T(8,128)}), f32[16,64,128]{2,1,0:T(8,128)S(1)}, u32[]{:S(2)}, u32[]{:S(2)}) async-start(f32[16,64,128]{2,1,0:T(8,128)} %bitcast.11), calls=%async_computation.7 | async-start | bytes 1048576 | tf_op jit(solution)/shard_map/all_to_all | solution.py:19
  115.5 1.3 collective-permute-start.5
  116.8 7.6 %all-to-all-done.7 = f32[16,64,128]{2,1,0:T(8,128)S(1)} async-done(((f32[16,64,128]{2,1,0:T(8,128)}), f32[16,64,128]{2,1,0:T(8,128)S(1)}, u32[]{:S(2)}, u32[]{:S(2)}) %all-to-all-start.7) | async-done | bytes 524320 | tf_op jit(solution)/shard_map/all_to_all | solution.py:19
  124.5 4.2 %collective-permute-start.4 = (f32[1024,128]{1,0:T(8,128)S(1)}, f32[1024,128]{1,0:T(8,128)S(1)}, u32[]{:S(2)}, u32[]{:S(2)}) collective-permute-start(f32[1024,128]{1,0:T(8,128)S(1)} %bitcast.18), channel_id=1, source_target_pairs={{0,1},{1,0},{2,3},{3,2},{4,5},{5,4},{6,7},{7,6},{8,9},{9,8},{10,11... | collective-permute-start | bytes 1572872 | tf_op jit(solution)/shard_map/ppermute | solution.py:23
  128.6 0.0 collective-permute-done.5.c_other_ref
  128.6 1.5 %collective-permute-done.4.other_ref = f32[1024,128]{1,0:T(8,128)S(1)} collective-permute-done((f32[1024,128]{1,0:T(8,128)S(1)}, f32[1024,128]{1,0:T(8,128)S(1)}, u32[]{:S(2)}, u32[]{:S(2)}) %collective-permute-start.4) | collective-permute-done | bytes 524320 | tf_op jit(solution)/shard_map/ppermute | solution.py:23
  130.2 8.4 %factors.1 = (f32[32,128]{1,0:T(8,128)}, f32[128,128]{1,0:T(8,128)}) custom-call(f32[1024,128]{1,0:T(8,128)S(1)} %bitcast.19, f32[1024,128]{1,0:T(8,128)S(1)} %collective-permute-done.4.other_ref, f32[1024,128]{1,0:T(8,128)S(1)} %get-tuple-element.29.c_ref, f32[1024,128]{1,0:T(8,128)S(1)} %collective-permute-done.5.c_other_ref), custom_call_target="tpu_custom_call" | custom-call | tf_op jit(solution)/shard_map/factors/pallas_call | solution.py:31
  (3 shorter events, 0.1 us)
Async XLA Ops:
  0.6 5.2 %collective-permute-start = (f32[128,128]{1,0:T(8,128)}, f32[128,128]{1,0:T(8,128)S(1)}, u32[]{:S(2)}, u32[]{:S(2)}) collective-permute-start(f32[128,128]{1,0:T(8,128)} %param.7), channel_id=1, source_target_pairs={{0,1},{1,0},{2,3},{3,2},{4,5},{5,4},{6,7},{7,6},{8,9},{9,8},{10,11... | collective-permute-start | bytes 196616 | tf_op jit(solution)/shard_map/ppermute | solution.py:23
  5.8 9.5 %copy-start = (f32[32,4096]{1,0:T(8,128)S(1)}, f32[32,4096]{1,0:T(8,128)}, u32[]{:S(2)}) copy-start(f32[32,4096]{1,0:T(8,128)} %param.6) | copy-start | bytes 1572868
  5.8 28.7 %copy-start.1 = (f32[128,128]{1,0:T(8,128)S(1)}, f32[128,128]{1,0:T(8,128)}, u32[]{:S(2)}) copy-start(f32[128,128]{1,0:T(8,128)} %param.7) | copy-start | bytes 196612
  5.8 24.3 %all-to-all-start.4 = ((f32[32,32,128]{2,1,0:T(8,128)}), f32[32,32,128]{2,1,0:T(8,128)S(1)}, u32[]{:S(2)}, u32[]{:S(2)}) async-start(f32[32,32,128]{2,1,0:T(8,128)} %split.1), calls=%async_computation.4 | async-start | bytes 1048576 | tf_op jit(solution)/shard_map/all_to_all | solution.py:19
  15.3 17.7 %collective-permute-start.2 = (f32[32,4096]{1,0:T(8,128)S(1)}, f32[32,4096]{1,0:T(8,128)S(1)}, u32[]{:S(2)}, u32[]{:S(2)}) collective-permute-start(f32[32,4096]{1,0:T(8,128)S(1)} %copy-done), channel_id=1, source_target_pairs={{0,1},{2,3},{4,5},{6,7},{8,9},{10,11},{12,13},{14,15},{16,17},{18,... | collective-permute-start | bytes 1572872 | tf_op jit(solution)/shard_map/ppermute | solution.py:27
  30.1 4.3 %collective-permute-start.1 = (f32[1024,128]{1,0:T(8,128)S(1)}, f32[1024,128]{1,0:T(8,128)S(1)}, u32[]{:S(2)}, u32[]{:S(2)}) collective-permute-start(f32[1024,128]{1,0:T(8,128)S(1)} %bitcast.25), channel_id=1, source_target_pairs={{0,1},{1,0},{2,3},{3,2},{4,5},{5,4},{6,7},{7,6},{8,9},{9,8},{10,11... | collective-permute-start | bytes 1572872 | tf_op jit(solution)/shard_map/ppermute | solution.py:23
  58.4 25.6 %collective-permute-start.3 = (f32[256,128]{1,0:T(8,128)S(1)}, f32[256,128]{1,0:T(8,128)S(1)}, u32[]{:S(2)}, u32[]{:S(2)}) collective-permute-start(f32[256,128]{1,0:T(8,128)S(1)} %get-tuple-element.28.x_ref), channel_id=1, source_target_pairs={{0,1},{1,0},{2,3},{3,2},{4,5},{5,4},{6,7},{7,6},{8,9},{9,8},{10,11... | collective-permute-start | bytes 393224 | tf_op jit(solution)/shard_map/ppermute | solution.py:23
  110.9 13.5 %all-to-all-start.7 = ((f32[16,64,128]{2,1,0:T(8,128)}), f32[16,64,128]{2,1,0:T(8,128)S(1)}, u32[]{:S(2)}, u32[]{:S(2)}) async-start(f32[16,64,128]{2,1,0:T(8,128)} %bitcast.11), calls=%async_computation.7 | async-start | bytes 1048576 | tf_op jit(solution)/shard_map/all_to_all | solution.py:19
  115.5 13.1 %collective-permute-start.5 = (f32[1024,128]{1,0:T(8,128)S(1)}, f32[1024,128]{1,0:T(8,128)S(1)}, u32[]{:S(2)}, u32[]{:S(2)}) collective-permute-start(f32[1024,128]{1,0:T(8,128)S(1)} %get-tuple-element.29.c_ref), channel_id=1, source_target_pairs={{0,1},{2,3},{4,5},{6,7},{8,9},{10,11},{12,13},{14,15},{16,17},{18,... | collective-permute-start | bytes 1572872 | tf_op jit(solution)/shard_map/ppermute | solution.py:27
  124.5 5.7 %collective-permute-start.4 = (f32[1024,128]{1,0:T(8,128)S(1)}, f32[1024,128]{1,0:T(8,128)S(1)}, u32[]{:S(2)}, u32[]{:S(2)}) collective-permute-start(f32[1024,128]{1,0:T(8,128)S(1)} %bitcast.18), channel_id=1, source_target_pairs={{0,1},{1,0},{2,3},{3,2},{4,5},{5,4},{6,7},{7,6},{8,9},{9,8},{10,11... | collective-permute-start | bytes 1572872 | tf_op jit(solution)/shard_map/ppermute | solution.py:23

commit v8 on v7

--- a/solution.py
+++ b/solution.py
@@ -106,17 +106,23 @@
     out_ref[...] = c
 
 
-def image_kernel(own_ref, other_ref, t_ref, x_ref, x_other_ref, out_ref):
-    core = lax.axis_index("core")
-
-    @pl.when(core == 0)
+def image_kernel(own_ref, other_ref, x_ref, out_ref):
+    @pl.when(lax.axis_index("core") == 0)
     def _():
         x = x_ref[...]
         out_ref[...] = dot(own_ref[...], x[:LANE]) + dot(other_ref[...], x[LANE:])
 
+
+def second_image_kernel(t_ref, x_ref, image_ref, out_ref):
+    core = lax.axis_index("core")
+
+    @pl.when(core == 0)
+    def _():
+        out_ref[...] = image_ref[...]
+
     @pl.when(core == 1)
     def _():
-        x = x_other_ref[...]
+        x = x_ref[...]
         rows = t_ref.shape[1] // 2
         first = t_ref[:, :rows, :].reshape(out_ref.shape)
         second = t_ref[:, rows:, :].reshape(out_ref.shape)
@@ -175,21 +181,36 @@
     return [jnp.concatenate(mine, axis=0) for mine in work]
 
 
-def final_kernel(own_ref, other_ref, c_ref, c_other_ref, basis_ref, operator_ref, y_ref):
+def factor_kernel(y_ref, c_ref, out_ref):
+    @pl.when(lax.axis_index("core") == 0)
+    def _():
+        y = y_ref[...]
+        scale = largest(y)
+        y = y * inverse_or_zero(scale)
+        lower, lower_w = inverse_factors([dot(y, y, 0, 0), dot(c_ref[...], y, 0, 0)])
+        out_ref[:LANE, :] = lower
+        out_ref[LANE : 2 * LANE, :] = lower_w
+        out_ref[2 * LANE :, :] = jnp.broadcast_to(scale, (SUB, LANE))
+
+
+def cross_kernel(own_ref, other_ref, after_ref, out_ref):
     first = lax.axis_index("core") == 0
     y = jnp.where(first, own_ref[...], other_ref[...])
     z = jnp.where(first, other_ref[...], own_ref[...])
-    c = jnp.where(first, c_ref[...], c_other_ref[...])
-    scale = largest(y)
-    y = y * inverse_or_zero(scale)
-    y_ref[...] = y
-    lower, lower_w = inverse_factors([dot(y, y, 0, 0), dot(c, y, 0, 0)])
-    cross = dot(y, z, 0, 0)
-    rows, total = basis_ref.shape[0], y_ref.shape[0]
+    out_ref[...] = dot(y * inverse_or_zero(largest(y)), z, 0, 0)
+
+
+def final_kernel(own_ref, other_ref, l_ref, l_other_ref, cross_ref, basis_ref, operator_ref):
+    first = lax.axis_index("core") == 0
+    factors = jnp.where(first, l_ref[...], l_other_ref[...])
+    lower, lower_w = factors[:LANE], factors[LANE : 2 * LANE]
+    scale = factors[2 * LANE : 2 * LANE + 1]
+    rows, total = basis_ref.shape[0], own_ref.shape[0]
     place = lax.axis_index("x") * lax.axis_size("z") + lax.axis_index("z")
-    mine = y_ref[pl.ds(pl.multiple_of(place * rows, rows), rows), :]
+    at = pl.ds(pl.multiple_of(place * rows, rows), rows)
+    mine = jnp.where(first, own_ref[at, :], other_ref[at, :]) * inverse_or_zero(scale)
     basis_ref[...] = dot(mine * jnp.sqrt(jnp.float32(total)), lower, 1, 1)
-    operator_ref[...] = dot(dot(lower, cross), lower_w, 1, 1) * lax.rsqrt(scale)
+    operator_ref[...] = dot(dot(lower, cross_ref[...]), lower_w, 1, 1) * lax.rsqrt(scale)
 
 
 def exchanged_rows(values, axis):
@@ -243,15 +264,18 @@
         lax.axis_index("core") == 0, project, relay,
         own, other, start_basis, start_other, shifted, shifted_other,
     )
-    x_other, c_other = from_other_core(x), to_second(c)
-    (part,) = call(image_kernel, "image", [(rows, LANE)], [own, other, t, x, x_other])
+    x_other = from_other_core(x)
+    (part,) = call(image_kernel, "image", [(rows, LANE)], [own, other, x])
+    (part,) = call(second_image_kernel, "second_image", [(rows, LANE)], [t, x_other, part])
     part = summed_over_chips(part, "image")
+    part_other = from_other_core(part)
+    (factors,) = call(factor_kernel, "factors", [(2 * LANE + SUB, LANE)], [part, c])
+    (cross,) = call(cross_kernel, "cross", [(LANE, LANE)], [part, part_other, factors])
     return call(
         final_kernel,
-        "factors",
+        "results",
         [(rows_dev, LANE), (LANE, LANE)],
-        [part, from_other_core(part), c, c_other],
-        [pltpu.VMEM((rows, LANE), jnp.float32)],
+        [part, part_other, factors, from_other_core(factors), cross],
     )
 
 

time: 139 us -> 139 us (level)
  blocking collectives: 47.4 us -> 63.6 us
  waiting for transfers between devices: 25.3 us -> 16.3 us
  Pallas kernels: 13.5 us -> 6.4 us
    all_to_all x3 -> x4, blocking collectives: 47.4 us -> 63.6 us  [exchanged(): return lax.all_to_all(blocks, axis, 0, 0, tiled=True)]
    all_to_all x2 -> x1, waiting for transfers between devices: 21.2 us -> 13.6 us  [exchanged(): return lax.all_to_all(blocks, axis, 0, 0, tiled=True)]
    pallas_call x6 -> x9, Pallas kernels: 13.5 us -> 6.4 us  [call(): pl.pallas_call(kernel, name=name, out_shape=[jax.ShapeDtypeStruct(shape,...]
    ppermute x4 -> x5, starting transfers between devices: 34.9 us -> 40.4 us  [from_other_core(): return lax.ppermute(value, 'core', [(0, 1), (1, 0)])]
    all_to_all x2 -> x1, starting transfers between devices: 14 us -> 9.44 us  [exchanged(): return lax.all_to_all(blocks, axis, 0, 0, tiled=True)]
    ppermute x4 -> x5, waiting for transfers between devices: 4.06 us -> 2.71 us  [from_other_core(): return lax.ppermute(value, 'core', [(0, 1), (1, 0)])]
  transfers between devices with their start and end apart: 8 -> 7, of which waited for: 5 -> 4; matrix products, arithmetic and copies ran while one was open for 0% -> 0% of each run, Pallas kernels for 1% -> 2%
where the time goes in v8:
time: 139 us; the launch traced here: 138 us
  blocking collectives  63.6 us (46%)
  starting transfers between devices  51.2 us (37%)
  waiting for transfers between devices  16.3 us (12%)
  Pallas kernels  6.4 us (5%)
    all_to_all x4, blocking collectives, exchanged(): return lax.all_to_all(blocks, axis, 0, 0, tiled=True)  63.6 us
    ppermute x5, starting transfers between devices, from_other_core(): return lax.ppermute(value, 'core', [(0, 1), (1, 0)])  40.4 us
    all_to_all x1, waiting for transfers between devices, exchanged(): return lax.all_to_all(blocks, axis, 0, 0, tiled=True)  13.6 us
    all_to_all x1, starting transfers between devices, exchanged(): return lax.all_to_all(blocks, axis, 0, 0, tiled=True)  9.44 us
    pallas_call x9, Pallas kernels, call(): pl.pallas_call(kernel, name=name, out_shape=[jax.ShapeDtypeStruct(shape,...  6.4 us
  transfers between devices with their start and end apart: 7, of which 4 were waited for; matrix products, arithmetic and copies ran while one was open for 0% of the time, Pallas kernels for 2%

profile of v8, /device:TPU:1, one launch (start us, length us, event | category | flops | bytes accessed | tf_op | source)
XLA Modules:
  0.0 138.3 jit_solution(3185376233141684417)
XLA Ops:
  0.6 3.3 %collective-permute-start.1 = (f32[128,128]{1,0:T(8,128)}, f32[128,128]{1,0:T(8,128)S(1)}, u32[]{:S(2)}, u32[]{:S(2)}) collective-permute-start(f32[128,128]{1,0:T(8,128)} %param.7), channel_id=1, source_target_pairs={{0,1},{1,0},{2,3},{3,2},{4,5},{5,4},{6,7},{7,6},{8,9},{9,8},{10,11... | collective-permute-start | bytes 196616 | tf_op jit(solution)/shard_map/ppermute | solution.py:23
  4.0 1.8 %split.1 = f32[32,32,128]{2,1,0:T(8,128)} custom-call(f32[32,4096]{1,0:T(8,128)} %refs_0_.1), custom_call_target="tpu_custom_call" | custom-call | tf_op jit(solution)/shard_map/split/pallas_call | solution.py:31
  5.8 0.0 copy-start
  5.8 0.0 copy-start.1
  5.8 0.0 collective-permute-done.1
  5.8 9.4 %all-to-all-start.4 = ((f32[32,32,128]{2,1,0:T(8,128)}), f32[32,32,128]{2,1,0:T(8,128)S(1)}, u32[]{:S(2)}, u32[]{:S(2)}) async-start(f32[32,32,128]{2,1,0:T(8,128)} %split.1), calls=%async_computation.4 | async-start | bytes 1048576 | tf_op jit(solution)/shard_map/all_to_all | solution.py:19
  15.3 0.0 copy-done
  15.3 1.3 collective-permute-start
  16.6 13.6 %all-to-all-done.4 = f32[32,32,128]{2,1,0:T(8,128)S(1)} async-done(((f32[32,32,128]{2,1,0:T(8,128)}), f32[32,32,128]{2,1,0:T(8,128)S(1)}, u32[]{:S(2)}, u32[]{:S(2)}) %all-to-all-start.4) | async-done | bytes 524320 | tf_op jit(solution)/shard_map/all_to_all | solution.py:19
  30.2 2.8 %collective-permute-start.2 = (f32[1024,128]{1,0:T(8,128)S(1)}, f32[1024,128]{1,0:T(8,128)S(1)}, u32[]{:S(2)}, u32[]{:S(2)}) collective-permute-start(f32[1024,128]{1,0:T(8,128)S(1)} %bitcast.28), channel_id=1, source_target_pairs={{0,1},{1,0},{2,3},{3,2},{4,5},{5,4},{6,7},{7,6},{8,9},{9,8},{10,11... | collective-permute-start | bytes 1572872 | tf_op jit(solution)/shard_map/ppermute | solution.py:23
  33.0 0.0 collective-permute-done
  33.0 1.5 %collective-permute-done.2.other_ref = f32[1024,128]{1,0:T(8,128)S(1)} collective-permute-done((f32[1024,128]{1,0:T(8,128)S(1)}, f32[1024,128]{1,0:T(8,128)S(1)}, u32[]{:S(2)}, u32[]{:S(2)}) %collective-permute-start.2) | collective-permute-done | bytes 524320 | tf_op jit(solution)/shard_map/ppermute | solution.py:23
  34.5 0.0 copy-done.1
  34.5 23.9 %conditional.1 = ((f32[256,128]{1,0:T(8,128)S(1)}, f32[1024,128]{1,0:T(8,128)S(1)}, f32[32,64,128]{2,1,0:T(8,128)S(1)})) conditional(s32[]{:T(128)} %convert_element_type.3, (f32[32,4096]{1,0:T(8,128)S(1)}, f32[32,4096]{1,0:T(8,128)S(1)}) %tuple.23, (f32[1024,128]{1,0:T(8,128)S(1)}, f32[1024,128]{1,0:T(8,128)S(1)}, f32[128,128]{1,0:T(8,128)S(1)}, ...), branch_computations={%region_0.0_spmd, %region_1.0_spmd} | conditional | bytes 2752552 | solution.py:263
  34.5 1.4 %split_shifted.1 = f32[32,64,128]{2,1,0:T(8,128)} custom-call(f32[32,4096]{1,0:T(8,128)S(1)} %get-tuple-element.12.refs_0_, f32[32,4096]{1,0:T(8,128)S(1)} %get-tuple-element.13.refs_1_), custom_call_target="tpu_custom_call" | custom-call | tf_op jit(solution)/shard_map/cond/branch_0_fun/split_shifted/pallas_call | solution.py:31
  35.9 22.4 %all_to_all.36 = f32[32,64,128]{2,1,0:T(8,128)S(1)} all-to-all(f32[32,64,128]{2,1,0:T(8,128)} %split_shifted.1), channel_id=1, replica_groups=mesh['x'=4,'z'=8,'y'=4,'core'=2] {'x','z'}, dimensions={0} | all-to-all | bytes 2097152 | tf_op jit(solution)/shard_map/cond/branch_0_fun/all_to_all | solution.py:19
  58.4 24.6 %collective-permute-start.3 = (f32[256,128]{1,0:T(8,128)S(1)}, f32[256,128]{1,0:T(8,128)S(1)}, u32[]{:S(2)}, u32[]{:S(2)}) collective-permute-start(f32[256,128]{1,0:T(8,128)S(1)} %get-tuple-element.28.x_ref), channel_id=1, source_target_pairs={{0,1},{1,0},{2,3},{3,2},{4,5},{5,4},{6,7},{7,6},{8,9},{9,8},{10,11... | collective-permute-start | bytes 393224 | tf_op jit(solution)/shard_map/ppermute | solution.py:23
  83.0 1.0 collective-permute-done.3.x_ref
  84.0 1.0 second_image.1
  85.0 14.9 %all_to_all.40 = f32[16,64,128]{2,1,0:T(8,128)S(1)} all-to-all(f32[16,64,128]{2,1,0:T(8,128)S(1)} %bitcast.18), channel_id=1, replica_groups=mesh['x'=4,'z'=8,'y'=4,'core'=2] {'x','y'}, dimensions={0} | all-to-all | bytes 1048576 | tf_op jit(solution)/shard_map/all_to_all | solution.py:19
  100.0 14.2 %all_to_all.41 = f32[8,64,128]{2,1,0:T(8,128)S(1)} all-to-all(f32[8,64,128]{2,1,0:T(8,128)S(1)} %bitcast.26), channel_id=1, replica_groups=mesh['x'=4,'z'=8,'y'=4,'core'=2] {'z'}, dimensions={0} | all-to-all | bytes 524288 | tf_op jit(solution)/shard_map/all_to_all | solution.py:19
  114.3 12.1 %all_to_all.42 = f32[16,64,128]{2,1,0:T(8,128)S(1)} all-to-all(f32[16,64,128]{2,1,0:T(8,128)S(1)} %bitcast.22), channel_id=1, replica_groups=mesh['x'=4,'z'=8,'y'=4,'core'=2] {'x','y'}, dimensions={0} | all-to-all | bytes 1048576 | tf_op jit(solution)/shard_map/all_to_all | solution.py:19
  126.4 3.4 %collective-permute-start.4 = (f32[1024,128]{1,0:T(8,128)S(1)}, f32[1024,128]{1,0:T(8,128)S(1)}, u32[]{:S(2)}, u32[]{:S(2)}) collective-permute-start(f32[1024,128]{1,0:T(8,128)S(1)} %bitcast.13), channel_id=1, source_target_pairs={{0,1},{1,0},{2,3},{3,2},{4,5},{5,4},{6,7},{7,6},{8,9},{9,8},{10,11... | collective-permute-start | bytes 1572872 | tf_op jit(solution)/shard_map/ppermute | solution.py:23
  129.8 6.3 %collective-permute-start.5 = (f32[264,128]{1,0:T(8,128)S(1)}, f32[264,128]{1,0:T(8,128)S(1)}, u32[]{:S(2)}, u32[]{:S(2)}) collective-permute-start(f32[264,128]{1,0:T(8,128)S(1)} %factors.1.after_ref.l_ref), channel_id=1, source_target_pairs={{0,1},{1,0},{2,3},{3,2},{4,5},{5,4},{6,7},{7,6},{8,9},{9,8},{10,11... | collective-permute-start | bytes 405512 | tf_op jit(solution)/shard_map/ppermute | solution.py:23
  136.1 0.0 collective-permute-done.4.other_ref
  136.1 0.8 cross.1.cross_ref
  136.9 0.2 collective-permute-done.5.l_other_ref
  137.1 1.3 results.1
  (6 shorter events, 0.1 us)
Async XLA Ops:
  0.6 5.2 %collective-permute-start.1 = (f32[128,128]{1,0:T(8,128)}, f32[128,128]{1,0:T(8,128)S(1)}, u32[]{:S(2)}, u32[]{:S(2)}) collective-permute-start(f32[128,128]{1,0:T(8,128)} %param.7), channel_id=1, source_target_pairs={{0,1},{1,0},{2,3},{3,2},{4,5},{5,4},{6,7},{7,6},{8,9},{9,8},{10,11... | collective-permute-start | bytes 196616 | tf_op jit(solution)/shard_map/ppermute | solution.py:23
  5.8 9.5 %copy-start = (f32[32,4096]{1,0:T(8,128)S(1)}, f32[32,4096]{1,0:T(8,128)}, u32[]{:S(2)}) copy-start(f32[32,4096]{1,0:T(8,128)} %param.6) | copy-start | bytes 1572868
  5.8 28.7 %copy-start.1 = (f32[128,128]{1,0:T(8,128)S(1)}, f32[128,128]{1,0:T(8,128)}, u32[]{:S(2)}) copy-start(f32[128,128]{1,0:T(8,128)} %param.7) | copy-start | bytes 196612
  5.8 24.3 %all-to-all-start.4 = ((f32[32,32,128]{2,1,0:T(8,128)}), f32[32,32,128]{2,1,0:T(8,128)S(1)}, u32[]{:S(2)}, u32[]{:S(2)}) async-start(f32[32,32,128]{2,1,0:T(8,128)} %split.1), calls=%async_computation.4 | async-start | bytes 1048576 | tf_op jit(solution)/shard_map/all_to_all | solution.py:19
  15.3 17.7 %collective-permute-start = (f32[32,4096]{1,0:T(8,128)S(1)}, f32[32,4096]{1,0:T(8,128)S(1)}, u32[]{:S(2)}, u32[]{:S(2)}) collective-permute-start(f32[32,4096]{1,0:T(8,128)S(1)} %copy-done), channel_id=1, source_target_pairs={{0,1},{2,3},{4,5},{6,7},{8,9},{10,11},{12,13},{14,15},{16,17},{18,... | collective-permute-start | bytes 1572872 | tf_op jit(solution)/shard_map/ppermute | solution.py:27
  30.2 4.3 %collective-permute-start.2 = (f32[1024,128]{1,0:T(8,128)S(1)}, f32[1024,128]{1,0:T(8,128)S(1)}, u32[]{:S(2)}, u32[]{:S(2)}) collective-permute-start(f32[1024,128]{1,0:T(8,128)S(1)} %bitcast.28), channel_id=1, source_target_pairs={{0,1},{1,0},{2,3},{3,2},{4,5},{5,4},{6,7},{7,6},{8,9},{9,8},{10,11... | collective-permute-start | bytes 1572872 | tf_op jit(solution)/shard_map/ppermute | solution.py:23
  58.4 25.6 %collective-permute-start.3 = (f32[256,128]{1,0:T(8,128)S(1)}, f32[256,128]{1,0:T(8,128)S(1)}, u32[]{:S(2)}, u32[]{:S(2)}) collective-permute-start(f32[256,128]{1,0:T(8,128)S(1)} %get-tuple-element.28.x_ref), channel_id=1, source_target_pairs={{0,1},{1,0},{2,3},{3,2},{4,5},{5,4},{6,7},{7,6},{8,9},{9,8},{10,11... | collective-permute-start | bytes 393224 | tf_op jit(solution)/shard_map/ppermute | solution.py:23
  126.4 9.7 %collective-permute-start.4 = (f32[1024,128]{1,0:T(8,128)S(1)}, f32[1024,128]{1,0:T(8,128)S(1)}, u32[]{:S(2)}, u32[]{:S(2)}) collective-permute-start(f32[1024,128]{1,0:T(8,128)S(1)} %bitcast.13), channel_id=1, source_target_pairs={{0,1},{1,0},{2,3},{3,2},{4,5},{5,4},{6,7},{7,6},{8,9},{9,8},{10,11... | collective-permute-start | bytes 1572872 | tf_op jit(solution)/shard_map/ppermute | solution.py:23
  129.8 7.3 %collective-permute-start.5 = (f32[264,128]{1,0:T(8,128)S(1)}, f32[264,128]{1,0:T(8,128)S(1)}, u32[]{:S(2)}, u32[]{:S(2)}) collective-permute-start(f32[264,128]{1,0:T(8,128)S(1)} %factors.1.after_ref.l_ref), channel_id=1, source_target_pairs={{0,1},{1,0},{2,3},{3,2},{4,5},{5,4},{6,7},{7,6},{8,9},{9,8},{10,11... | collective-permute-start | bytes 405512 | tf_op jit(solution)/shard_map/ppermute | solution.py:23

commit v9 on v8

--- a/solution.py
+++ b/solution.py
@@ -85,8 +85,13 @@
         store.wait()
 
 
+def beside(left, right):
+    return jnp.concatenate([left, right], axis=1)
+
+
 def columns_kernel(own_ref, other_ref, start_ref, start_other_ref, out_ref):
-    out_ref[...] = dot(own_ref[...], start_ref[...]) + dot(other_ref[...], start_other_ref[...])
+    start = jnp.concatenate([start_ref[...], start_other_ref[...]])
+    out_ref[...] = dot(beside(own_ref[...], other_ref[...]), start)
 
 
 def sum_kernel(in_ref, out_ref, *, rows):
@@ -101,16 +106,14 @@
 def across_kernel(own_ref, other_ref, c_ref, x_ref, out_ref, unused_ref):
     c = c_ref[...]
     c = c * inverse_or_zero(largest(c))
-    x_ref[:LANE, :] = dot(own_ref[...], c, 0, 0)
-    x_ref[LANE:, :] = dot(other_ref[...], c, 0, 0)
+    x_ref[...] = dot(c, beside(own_ref[...], other_ref[...]), 0, 0)
     out_ref[...] = c
 
 
 def image_kernel(own_ref, other_ref, x_ref, out_ref):
     @pl.when(lax.axis_index("core") == 0)
     def _():
-        x = x_ref[...]
-        out_ref[...] = dot(own_ref[...], x[:LANE]) + dot(other_ref[...], x[LANE:])
+        out_ref[...] = dot(beside(own_ref[...], other_ref[...]), x_ref[...], 1, 1)
 
 
 def second_image_kernel(t_ref, x_ref, image_ref, out_ref):
@@ -122,11 +125,10 @@
 
     @pl.when(core == 1)
     def _():
-        x = x_ref[...]
         rows = t_ref.shape[1] // 2
         first = t_ref[:, :rows, :].reshape(out_ref.shape)
         second = t_ref[:, rows:, :].reshape(out_ref.shape)
-        out_ref[...] = dot(first, x[:LANE]) + dot(second, x[LANE:])
+        out_ref[...] = dot(beside(first, second), x_ref[...], 1, 1)
 
 
 def inverse_factors(matrices):
@@ -187,7 +189,8 @@
         y = y_ref[...]
         scale = largest(y)
         y = y * inverse_or_zero(scale)
-        lower, lower_w = inverse_factors([dot(y, y, 0, 0), dot(c_ref[...], y, 0, 0)])
+        grams = dot(y, beside(y, c_ref[...]), 0, 0)
+        lower, lower_w = inverse_factors([grams[:, :LANE], grams[:, LANE:]])
         out_ref[:LANE, :] = lower
         out_ref[LANE : 2 * LANE, :] = lower_w
         out_ref[2 * LANE :, :] = jnp.broadcast_to(scale, (SUB, LANE))
@@ -253,12 +256,12 @@
             columns_kernel, "columns", [(rows, LANE)], [own, other, start_basis, start_other]
         )
         c = summed_over_chips(c_part, "columns")
-        shapes = [(2 * LANE, LANE), (rows, LANE), both]
+        shapes = [(LANE, 2 * LANE), (rows, LANE), both]
         return tuple(call(across_kernel, "across", shapes, [own, other, c]))
 
     def relay(own, other, start_basis, start_other, shifted, shifted_other):
         t = exchanged(split("split_shifted", shifted_other, shifted), ROWS)
-        return jnp.zeros((2 * LANE, LANE), jnp.float32), jnp.zeros((rows, LANE), jnp.float32), t
+        return jnp.zeros((LANE, 2 * LANE), jnp.float32), jnp.zeros((rows, LANE), jnp.float32), t
 
     x, c, t = lax.cond(
         lax.axis_index("core") == 0, project, relay,

time: 139 us -> 138 us (level)
  no operation moved by 1% of the time
where the time goes in v9:
time: 138 us; the launch traced here: 137 us
  blocking collectives  63.5 us (46%)
  starting transfers between devices  50.2 us (36%)
  waiting for transfers between devices  16.3 us (12%)
  Pallas kernels  6.38 us (5%)
    all_to_all x4, blocking collectives, exchanged(): return lax.all_to_all(blocks, axis, 0, 0, tiled=True)  63.5 us
    ppermute x5, starting transfers between devices, from_other_core(): return lax.ppermute(value, 'core', [(0, 1), (1, 0)])  39.5 us
    all_to_all x1, waiting for transfers between devices, exchanged(): return lax.all_to_all(blocks, axis, 0, 0, tiled=True)  13.6 us
    all_to_all x1, starting transfers between devices, exchanged(): return lax.all_to_all(blocks, axis, 0, 0, tiled=True)  9.44 us
    pallas_call x9, Pallas kernels, call(): pl.pallas_call(kernel, name=name, out_shape=[jax.ShapeDtypeStruct(shape,...  6.38 us
  transfers between devices with their start and end apart: 7, of which 4 were waited for; matrix products, arithmetic and copies ran while one was open for 0% of the time, Pallas kernels for 2%

profile of v9, /device:TPU:1, one launch (start us, length us, event | category | flops | bytes accessed | tf_op | source)
XLA Modules:
  0.0 137.2 jit_solution(8676243751524364011)
XLA Ops:
  0.6 3.3 %collective-permute-start.1 = (f32[128,128]{1,0:T(8,128)}, f32[128,128]{1,0:T(8,128)S(1)}, u32[]{:S(2)}, u32[]{:S(2)}) collective-permute-start(f32[128,128]{1,0:T(8,128)} %param.7), channel_id=1, source_target_pairs={{0,1},{1,0},{2,3},{3,2},{4,5},{5,4},{6,7},{7,6},{8,9},{9,8},{10,11... | collective-permute-start | bytes 196616 | tf_op jit(solution)/shard_map/ppermute | solution.py:23
  4.0 1.8 %split.1 = f32[32,32,128]{2,1,0:T(8,128)} custom-call(f32[32,4096]{1,0:T(8,128)} %refs_0_.1), custom_call_target="tpu_custom_call" | custom-call | tf_op jit(solution)/shard_map/split/pallas_call | solution.py:31
  5.8 0.0 copy-start
  5.8 0.0 copy-start.1
  5.8 0.0 collective-permute-done.1
  5.8 9.4 %all-to-all-start.4 = ((f32[32,32,128]{2,1,0:T(8,128)}), f32[32,32,128]{2,1,0:T(8,128)S(1)}, u32[]{:S(2)}, u32[]{:S(2)}) async-start(f32[32,32,128]{2,1,0:T(8,128)} %split.1), calls=%async_computation.4 | async-start | bytes 1048576 | tf_op jit(solution)/shard_map/all_to_all | solution.py:19
  15.3 0.0 copy-done
  15.3 1.3 collective-permute-start
  16.6 13.6 %all-to-all-done.4 = f32[32,32,128]{2,1,0:T(8,128)S(1)} async-done(((f32[32,32,128]{2,1,0:T(8,128)}), f32[32,32,128]{2,1,0:T(8,128)S(1)}, u32[]{:S(2)}, u32[]{:S(2)}) %all-to-all-start.4) | async-done | bytes 524320 | tf_op jit(solution)/shard_map/all_to_all | solution.py:19
  30.2 2.8 %collective-permute-start.2 = (f32[1024,128]{1,0:T(8,128)S(1)}, f32[1024,128]{1,0:T(8,128)S(1)}, u32[]{:S(2)}, u32[]{:S(2)}) collective-permute-start(f32[1024,128]{1,0:T(8,128)S(1)} %bitcast.28), channel_id=1, source_target_pairs={{0,1},{1,0},{2,3},{3,2},{4,5},{5,4},{6,7},{7,6},{8,9},{9,8},{10,11... | collective-permute-start | bytes 1572872 | tf_op jit(solution)/shard_map/ppermute | solution.py:23
  33.0 0.0 collective-permute-done
  33.0 1.5 %collective-permute-done.2.other_ref = f32[1024,128]{1,0:T(8,128)S(1)} collective-permute-done((f32[1024,128]{1,0:T(8,128)S(1)}, f32[1024,128]{1,0:T(8,128)S(1)}, u32[]{:S(2)}, u32[]{:S(2)}) %collective-permute-start.2) | collective-permute-done | bytes 524320 | tf_op jit(solution)/shard_map/ppermute | solution.py:23
  34.5 0.0 copy-done.1
  34.5 23.9 %conditional.1 = ((f32[128,256]{1,0:T(8,128)S(1)}, f32[1024,128]{1,0:T(8,128)S(1)}, f32[32,64,128]{2,1,0:T(8,128)S(1)})) conditional(s32[]{:T(128)} %convert_element_type.3, (f32[32,4096]{1,0:T(8,128)S(1)}, f32[32,4096]{1,0:T(8,128)S(1)}) %tuple.23, (f32[1024,128]{1,0:T(8,128)S(1)}, f32[1024,128]{1,0:T(8,128)S(1)}, f32[128,128]{1,0:T(8,128)S(1)}, ...), branch_computations={%region_0.0_spmd, %region_1.0_spmd} | conditional | bytes 2752552 | solution.py:266
  34.5 1.4 %split_shifted.1 = f32[32,64,128]{2,1,0:T(8,128)} custom-call(f32[32,4096]{1,0:T(8,128)S(1)} %get-tuple-element.12.refs_0_, f32[32,4096]{1,0:T(8,128)S(1)} %get-tuple-element.13.refs_1_), custom_call_target="tpu_custom_call" | custom-call | tf_op jit(solution)/shard_map/cond/branch_0_fun/split_shifted/pallas_call | solution.py:31
  35.9 22.4 %all_to_all.36 = f32[32,64,128]{2,1,0:T(8,128)S(1)} all-to-all(f32[32,64,128]{2,1,0:T(8,128)} %split_shifted.1), channel_id=1, replica_groups=mesh['x'=4,'z'=8,'y'=4,'core'=2] {'x','z'}, dimensions={0} | all-to-all | bytes 2097152 | tf_op jit(solution)/shard_map/cond/branch_0_fun/all_to_all | solution.py:19
  58.4 23.8 %collective-permute-start.3 = (f32[128,256]{1,0:T(8,128)S(1)}, f32[128,256]{1,0:T(8,128)S(1)}, u32[]{:S(2)}, u32[]{:S(2)}) collective-permute-start(f32[128,256]{1,0:T(8,128)S(1)} %get-tuple-element.28.x_ref), channel_id=1, source_target_pairs={{0,1},{1,0},{2,3},{3,2},{4,5},{5,4},{6,7},{7,6},{8,9},{9,8},{10,11... | collective-permute-start | bytes 393224 | tf_op jit(solution)/shard_map/ppermute | solution.py:23
  82.2 1.0 collective-permute-done.3.x_ref
  83.2 1.0 second_image.1
  84.2 14.9 %all_to_all.40 = f32[16,64,128]{2,1,0:T(8,128)S(1)} all-to-all(f32[16,64,128]{2,1,0:T(8,128)S(1)} %bitcast.18), channel_id=1, replica_groups=mesh['x'=4,'z'=8,'y'=4,'core'=2] {'x','y'}, dimensions={0} | all-to-all | bytes 1048576 | tf_op jit(solution)/shard_map/all_to_all | solution.py:19
  99.1 14.2 %all_to_all.41 = f32[8,64,128]{2,1,0:T(8,128)S(1)} all-to-all(f32[8,64,128]{2,1,0:T(8,128)S(1)} %bitcast.26), channel_id=1, replica_groups=mesh['x'=4,'z'=8,'y'=4,'core'=2] {'z'}, dimensions={0} | all-to-all | bytes 524288 | tf_op jit(solution)/shard_map/all_to_all | solution.py:19
  113.3 12.0 %all_to_all.42 = f32[16,64,128]{2,1,0:T(8,128)S(1)} all-to-all(f32[16,64,128]{2,1,0:T(8,128)S(1)} %bitcast.22), channel_id=1, replica_groups=mesh['x'=4,'z'=8,'y'=4,'core'=2] {'x','y'}, dimensions={0} | all-to-all | bytes 1048576 | tf_op jit(solution)/shard_map/all_to_all | solution.py:19
  125.4 3.4 %collective-permute-start.4 = (f32[1024,128]{1,0:T(8,128)S(1)}, f32[1024,128]{1,0:T(8,128)S(1)}, u32[]{:S(2)}, u32[]{:S(2)}) collective-permute-start(f32[1024,128]{1,0:T(8,128)S(1)} %bitcast.13), channel_id=1, source_target_pairs={{0,1},{1,0},{2,3},{3,2},{4,5},{5,4},{6,7},{7,6},{8,9},{9,8},{10,11... | collective-permute-start | bytes 1572872 | tf_op jit(solution)/shard_map/ppermute | solution.py:23
  128.8 6.1 %collective-permute-start.5 = (f32[264,128]{1,0:T(8,128)S(1)}, f32[264,128]{1,0:T(8,128)S(1)}, u32[]{:S(2)}, u32[]{:S(2)}) collective-permute-start(f32[264,128]{1,0:T(8,128)S(1)} %factors.1.after_ref.l_ref), channel_id=1, source_target_pairs={{0,1},{1,0},{2,3},{3,2},{4,5},{5,4},{6,7},{7,6},{8,9},{9,8},{10,11... | collective-permute-start | bytes 405512 | tf_op jit(solution)/shard_map/ppermute | solution.py:23
  135.0 0.0 collective-permute-done.4.other_ref
  135.0 0.8 cross.1.cross_ref
  135.8 0.2 collective-permute-done.5.l_other_ref
  136.0 1.3 results.1
  (6 shorter events, 0.1 us)
Async XLA Ops:
  0.6 5.2 %collective-permute-start.1 = (f32[128,128]{1,0:T(8,128)}, f32[128,128]{1,0:T(8,128)S(1)}, u32[]{:S(2)}, u32[]{:S(2)}) collective-permute-start(f32[128,128]{1,0:T(8,128)} %param.7), channel_id=1, source_target_pairs={{0,1},{1,0},{2,3},{3,2},{4,5},{5,4},{6,7},{7,6},{8,9},{9,8},{10,11... | collective-permute-start | bytes 196616 | tf_op jit(solution)/shard_map/ppermute | solution.py:23
  5.8 9.5 %copy-start = (f32[32,4096]{1,0:T(8,128)S(1)}, f32[32,4096]{1,0:T(8,128)}, u32[]{:S(2)}) copy-start(f32[32,4096]{1,0:T(8,128)} %param.6) | copy-start | bytes 1572868
  5.8 28.7 %copy-start.1 = (f32[128,128]{1,0:T(8,128)S(1)}, f32[128,128]{1,0:T(8,128)}, u32[]{:S(2)}) copy-start(f32[128,128]{1,0:T(8,128)} %param.7) | copy-start | bytes 196612
  5.8 24.3 %all-to-all-start.4 = ((f32[32,32,128]{2,1,0:T(8,128)}), f32[32,32,128]{2,1,0:T(8,128)S(1)}, u32[]{:S(2)}, u32[]{:S(2)}) async-start(f32[32,32,128]{2,1,0:T(8,128)} %split.1), calls=%async_computation.4 | async-start | bytes 1048576 | tf_op jit(solution)/shard_map/all_to_all | solution.py:19
  15.3 17.7 %collective-permute-start = (f32[32,4096]{1,0:T(8,128)S(1)}, f32[32,4096]{1,0:T(8,128)S(1)}, u32[]{:S(2)}, u32[]{:S(2)}) collective-permute-start(f32[32,4096]{1,0:T(8,128)S(1)} %copy-done), channel_id=1, source_target_pairs={{0,1},{2,3},{4,5},{6,7},{8,9},{10,11},{12,13},{14,15},{16,17},{18,... | collective-permute-start | bytes 1572872 | tf_op jit(solution)/shard_map/ppermute | solution.py:27
  30.2 4.3 %collective-permute-start.2 = (f32[1024,128]{1,0:T(8,128)S(1)}, f32[1024,128]{1,0:T(8,128)S(1)}, u32[]{:S(2)}, u32[]{:S(2)}) collective-permute-start(f32[1024,128]{1,0:T(8,128)S(1)} %bitcast.28), channel_id=1, source_target_pairs={{0,1},{1,0},{2,3},{3,2},{4,5},{5,4},{6,7},{7,6},{8,9},{9,8},{10,11... | collective-permute-start | bytes 1572872 | tf_op jit(solution)/shard_map/ppermute | solution.py:23
  58.4 24.7 %collective-permute-start.3 = (f32[128,256]{1,0:T(8,128)S(1)}, f32[128,256]{1,0:T(8,128)S(1)}, u32[]{:S(2)}, u32[]{:S(2)}) collective-permute-start(f32[128,256]{1,0:T(8,128)S(1)} %get-tuple-element.28.x_ref), channel_id=1, source_target_pairs={{0,1},{1,0},{2,3},{3,2},{4,5},{5,4},{6,7},{7,6},{8,9},{9,8},{10,11... | collective-permute-start | bytes 393224 | tf_op jit(solution)/shard_map/ppermute | solution.py:23
  125.4 9.6 %collective-permute-start.4 = (f32[1024,128]{1,0:T(8,128)S(1)}, f32[1024,128]{1,0:T(8,128)S(1)}, u32[]{:S(2)}, u32[]{:S(2)}) collective-permute-start(f32[1024,128]{1,0:T(8,128)S(1)} %bitcast.13), channel_id=1, source_target_pairs={{0,1},{1,0},{2,3},{3,2},{4,5},{5,4},{6,7},{7,6},{8,9},{9,8},{10,11... | collective-permute-start | bytes 1572872 | tf_op jit(solution)/shard_map/ppermute | solution.py:23
  128.8 7.1 %collective-permute-start.5 = (f32[264,128]{1,0:T(8,128)S(1)}, f32[264,128]{1,0:T(8,128)S(1)}, u32[]{:S(2)}, u32[]{:S(2)}) collective-permute-start(f32[264,128]{1,0:T(8,128)S(1)} %factors.1.after_ref.l_ref), channel_id=1, source_target_pairs={{0,1},{1,0},{2,3},{3,2},{4,5},{5,4},{6,7},{7,6},{8,9},{9,8},{10,11... | collective-permute-start | bytes 405512 | tf_op jit(solution)/shard_map/ppermute | solution.py:23

commit v10 on v9

--- a/solution.py
+++ b/solution.py
@@ -89,9 +89,12 @@
     return jnp.concatenate([left, right], axis=1)
 
 
-def columns_kernel(own_ref, other_ref, start_ref, start_other_ref, out_ref):
-    start = jnp.concatenate([start_ref[...], start_other_ref[...]])
-    out_ref[...] = dot(beside(own_ref[...], other_ref[...]), start)
+def first_columns_kernel(own_ref, start_ref, out_ref):
+    out_ref[...] = dot(own_ref[...], start_ref[...])
+
+
+def columns_kernel(other_ref, start_ref, columns_ref, out_ref):
+    out_ref[...] = columns_ref[...] + dot(other_ref[...], start_ref[...])
 
 
 def sum_kernel(in_ref, out_ref, *, rows):
@@ -249,23 +252,22 @@
     pieces, start_other = lax.optimization_barrier((split("split", hankel), start_other))
     own = exchanged(pieces, ROWS).reshape(rows, LANE)
     other = from_other_core(own)
+    (c_part,) = call(first_columns_kernel, "first_columns", [(rows, LANE)], [own, start_basis])
     both = (groups, 2 * rows_dev, LANE)
 
-    def project(own, other, start_basis, start_other, shifted, shifted_other):
-        (c_part,) = call(
-            columns_kernel, "columns", [(rows, LANE)], [own, other, start_basis, start_other]
-        )
+    def project(own, other, c_part, start_other, shifted, shifted_other):
+        (c_part,) = call(columns_kernel, "columns", [(rows, LANE)], [other, start_other, c_part])
         c = summed_over_chips(c_part, "columns")
         shapes = [(LANE, 2 * LANE), (rows, LANE), both]
         return tuple(call(across_kernel, "across", shapes, [own, other, c]))
 
-    def relay(own, other, start_basis, start_other, shifted, shifted_other):
+    def relay(own, other, c_part, start_other, shifted, shifted_other):
         t = exchanged(split("split_shifted", shifted_other, shifted), ROWS)
         return jnp.zeros((LANE, 2 * LANE), jnp.float32), jnp.zeros((rows, LANE), jnp.float32), t
 
     x, c, t = lax.cond(
         lax.axis_index("core") == 0, project, relay,
-        own, other, start_basis, start_other, shifted, shifted_other,
+        own, other, c_part, start_other, shifted, shifted_other,
     )
     x_other = from_other_core(x)
     (part,) = call(image_kernel, "image", [(rows, LANE)], [own, other, x])

time: 138 us -> 137 us (level)
    pallas_call x9 -> x10, Pallas kernels: 6.38 us -> 6.94 us  [call(): pl.pallas_call(kernel, name=name, out_shape=[jax.ShapeDtypeStruct(shape,...]
where the time goes in v10:
time: 137 us
  blocking collectives  63.5 us (46%)
  starting transfers between devices  50 us (36%)
  waiting for transfers between devices  15.7 us (11%)
  Pallas kernels  6.94 us (5%)
    all_to_all x4, blocking collectives, exchanged(): return lax.all_to_all(blocks, axis, 0, 0, tiled=True)  63.5 us
    ppermute x5, starting transfers between devices, from_other_core(): return lax.ppermute(value, 'core', [(0, 1), (1, 0)])  39.2 us
    all_to_all x1, waiting for transfers between devices, exchanged(): return lax.all_to_all(blocks, axis, 0, 0, tiled=True)  13.6 us
    all_to_all x1, starting transfers between devices, exchanged(): return lax.all_to_all(blocks, axis, 0, 0, tiled=True)  9.44 us
    pallas_call x10, Pallas kernels, call(): pl.pallas_call(kernel, name=name, out_shape=[jax.ShapeDtypeStruct(shape,...  6.94 us
  transfers between devices with their start and end apart: 7, of which 4 were waited for; matrix products, arithmetic and copies ran while one was open for 0% of the time, Pallas kernels for 2%

profile of v10, /device:TPU:1, one launch (start us, length us, event | category | flops | bytes accessed | tf_op | source)
XLA Modules:
  0.0 137.0 jit_solution(13436615139617192104)
XLA Ops:
  0.6 3.3 %collective-permute-start.1 = (f32[128,128]{1,0:T(8,128)}, f32[128,128]{1,0:T(8,128)S(1)}, u32[]{:S(2)}, u32[]{:S(2)}) collective-permute-start(f32[128,128]{1,0:T(8,128)} %start_ref.1), channel_id=1, source_target_pairs={{0,1},{1,0},{2,3},{3,2},{4,5},{5,4},{6,7},{7,6},{8,9},{9,8},{10,11... | collective-permute-start | bytes 196616 | tf_op jit(solution)/shard_map/ppermute | solution.py:23
  4.0 1.8 %split.1 = f32[32,32,128]{2,1,0:T(8,128)} custom-call(f32[32,4096]{1,0:T(8,128)} %refs_0_.1), custom_call_target="tpu_custom_call" | custom-call | tf_op jit(solution)/shard_map/split/pallas_call | solution.py:31
  5.8 0.0 copy-start.1
  5.8 0.0 copy-start
  5.8 0.0 collective-permute-done.1
  5.8 9.4 %all-to-all-start.4 = ((f32[32,32,128]{2,1,0:T(8,128)}), f32[32,32,128]{2,1,0:T(8,128)S(1)}, u32[]{:S(2)}, u32[]{:S(2)}) async-start(f32[32,32,128]{2,1,0:T(8,128)} %split.1), calls=%async_computation.4 | async-start | bytes 1048576 | tf_op jit(solution)/shard_map/all_to_all | solution.py:19
  15.3 0.0 copy-done.1
  15.3 1.3 collective-permute-start
  16.6 13.6 %all-to-all-done.4 = f32[32,32,128]{2,1,0:T(8,128)S(1)} async-done(((f32[32,32,128]{2,1,0:T(8,128)}), f32[32,32,128]{2,1,0:T(8,128)S(1)}, u32[]{:S(2)}, u32[]{:S(2)}) %all-to-all-start.4) | async-done | bytes 524320 | tf_op jit(solution)/shard_map/all_to_all | solution.py:19
  30.2 2.8 %collective-permute-start.2 = (f32[1024,128]{1,0:T(8,128)S(1)}, f32[1024,128]{1,0:T(8,128)S(1)}, u32[]{:S(2)}, u32[]{:S(2)}) collective-permute-start(f32[1024,128]{1,0:T(8,128)S(1)} %bitcast.28), channel_id=1, source_target_pairs={{0,1},{1,0},{2,3},{3,2},{4,5},{5,4},{6,7},{7,6},{8,9},{9,8},{10,11... | collective-permute-start | bytes 1572872 | tf_op jit(solution)/shard_map/ppermute | solution.py:23
  33.0 0.0 collective-permute-done
  33.0 0.0 copy-done
  33.0 0.6 first_columns.1
  33.5 1.0 collective-permute-done.2.other_ref
  34.5 23.9 %conditional.1 = ((f32[128,256]{1,0:T(8,128)S(1)}, f32[1024,128]{1,0:T(8,128)S(1)}, f32[32,64,128]{2,1,0:T(8,128)S(1)})) conditional(s32[]{:T(128)} %convert_element_type.3, (f32[32,4096]{1,0:T(8,128)S(1)}, f32[32,4096]{1,0:T(8,128)S(1)}) %tuple.23, (f32[1024,128]{1,0:T(8,128)S(1)}, f32[128,128]{1,0:T(8,128)S(1)}, f32[1024,128]{1,0:T(8,128)S(1)}, ...), branch_computations={%region_0.0_spmd, %region_1.0_spmd} | conditional | bytes 2752552 | solution.py:268
  34.5 1.4 %split_shifted.1 = f32[32,64,128]{2,1,0:T(8,128)} custom-call(f32[32,4096]{1,0:T(8,128)S(1)} %get-tuple-element.12.refs_0_, f32[32,4096]{1,0:T(8,128)S(1)} %get-tuple-element.13.refs_1_), custom_call_target="tpu_custom_call" | custom-call | tf_op jit(solution)/shard_map/cond/branch_0_fun/split_shifted/pallas_call | solution.py:31
  35.9 22.4 %all_to_all.36 = f32[32,64,128]{2,1,0:T(8,128)S(1)} all-to-all(f32[32,64,128]{2,1,0:T(8,128)} %split_shifted.1), channel_id=1, replica_groups=mesh['x'=4,'z'=8,'y'=4,'core'=2] {'x','z'}, dimensions={0} | all-to-all | bytes 2097152 | tf_op jit(solution)/shard_map/cond/branch_0_fun/all_to_all | solution.py:19
  58.4 23.5 %collective-permute-start.3 = (f32[128,256]{1,0:T(8,128)S(1)}, f32[128,256]{1,0:T(8,128)S(1)}, u32[]{:S(2)}, u32[]{:S(2)}) collective-permute-start(f32[128,256]{1,0:T(8,128)S(1)} %get-tuple-element.28.x_ref), channel_id=1, source_target_pairs={{0,1},{1,0},{2,3},{3,2},{4,5},{5,4},{6,7},{7,6},{8,9},{9,8},{10,11... | collective-permute-start | bytes 393224 | tf_op jit(solution)/shard_map/ppermute | solution.py:23
  81.9 1.0 collective-permute-done.3.x_ref
  82.9 1.0 second_image.1
  83.9 14.9 %all_to_all.40 = f32[16,64,128]{2,1,0:T(8,128)S(1)} all-to-all(f32[16,64,128]{2,1,0:T(8,128)S(1)} %bitcast.18), channel_id=1, replica_groups=mesh['x'=4,'z'=8,'y'=4,'core'=2] {'x','y'}, dimensions={0} | all-to-all | bytes 1048576 | tf_op jit(solution)/shard_map/all_to_all | solution.py:19
  98.8 14.2 %all_to_all.41 = f32[8,64,128]{2,1,0:T(8,128)S(1)} all-to-all(f32[8,64,128]{2,1,0:T(8,128)S(1)} %bitcast.26), channel_id=1, replica_groups=mesh['x'=4,'z'=8,'y'=4,'core'=2] {'z'}, dimensions={0} | all-to-all | bytes 524288 | tf_op jit(solution)/shard_map/all_to_all | solution.py:19
  113.1 12.0 %all_to_all.42 = f32[16,64,128]{2,1,0:T(8,128)S(1)} all-to-all(f32[16,64,128]{2,1,0:T(8,128)S(1)} %bitcast.23), channel_id=1, replica_groups=mesh['x'=4,'z'=8,'y'=4,'core'=2] {'x','y'}, dimensions={0} | all-to-all | bytes 1048576 | tf_op jit(solution)/shard_map/all_to_all | solution.py:19
  125.1 3.4 %collective-permute-start.4 = (f32[1024,128]{1,0:T(8,128)S(1)}, f32[1024,128]{1,0:T(8,128)S(1)}, u32[]{:S(2)}, u32[]{:S(2)}) collective-permute-start(f32[1024,128]{1,0:T(8,128)S(1)} %bitcast.13), channel_id=1, source_target_pairs={{0,1},{1,0},{2,3},{3,2},{4,5},{5,4},{6,7},{7,6},{8,9},{9,8},{10,11... | collective-permute-start | bytes 1572872 | tf_op jit(solution)/shard_map/ppermute | solution.py:23
  128.6 6.1 %collective-permute-start.5 = (f32[264,128]{1,0:T(8,128)S(1)}, f32[264,128]{1,0:T(8,128)S(1)}, u32[]{:S(2)}, u32[]{:S(2)}) collective-permute-start(f32[264,128]{1,0:T(8,128)S(1)} %factors.1.after_ref.l_ref), channel_id=1, source_target_pairs={{0,1},{1,0},{2,3},{3,2},{4,5},{5,4},{6,7},{7,6},{8,9},{9,8},{10,11... | collective-permute-start | bytes 405512 | tf_op jit(solution)/shard_map/ppermute | solution.py:23
  134.7 0.0 collective-permute-done.4.other_ref
  134.7 0.8 cross.1.cross_ref
  135.5 0.2 collective-permute-done.5.l_other_ref
  135.7 1.3 results.1
  (6 shorter events, 0.1 us)
Async XLA Ops:
  0.6 5.2 %collective-permute-start.1 = (f32[128,128]{1,0:T(8,128)}, f32[128,128]{1,0:T(8,128)S(1)}, u32[]{:S(2)}, u32[]{:S(2)}) collective-permute-start(f32[128,128]{1,0:T(8,128)} %start_ref.1), channel_id=1, source_target_pairs={{0,1},{1,0},{2,3},{3,2},{4,5},{5,4},{6,7},{7,6},{8,9},{9,8},{10,11... | collective-permute-start | bytes 196616 | tf_op jit(solution)/shard_map/ppermute | solution.py:23
  5.8 9.5 %copy-start.1 = (f32[32,4096]{1,0:T(8,128)S(1)}, f32[32,4096]{1,0:T(8,128)}, u32[]{:S(2)}) copy-start(f32[32,4096]{1,0:T(8,128)} %param.6) | copy-start | bytes 1572868
  5.8 27.2 %copy-start = (f32[128,128]{1,0:T(8,128)S(1)}, f32[128,128]{1,0:T(8,128)}, u32[]{:S(2)}) copy-start(f32[128,128]{1,0:T(8,128)} %start_ref.1) | copy-start | bytes 196612
  5.8 24.3 %all-to-all-start.4 = ((f32[32,32,128]{2,1,0:T(8,128)}), f32[32,32,128]{2,1,0:T(8,128)S(1)}, u32[]{:S(2)}, u32[]{:S(2)}) async-start(f32[32,32,128]{2,1,0:T(8,128)} %split.1), calls=%async_computation.4 | async-start | bytes 1048576 | tf_op jit(solution)/shard_map/all_to_all | solution.py:19
  15.3 17.7 %collective-permute-start = (f32[32,4096]{1,0:T(8,128)S(1)}, f32[32,4096]{1,0:T(8,128)S(1)}, u32[]{:S(2)}, u32[]{:S(2)}) collective-permute-start(f32[32,4096]{1,0:T(8,128)S(1)} %copy-done.1), channel_id=1, source_target_pairs={{0,1},{2,3},{4,5},{6,7},{8,9},{10,11},{12,13},{14,15},{16,17},{18,... | collective-permute-start | bytes 1572872 | tf_op jit(solution)/shard_map/ppermute | solution.py:27
  30.2 4.3 %collective-permute-start.2 = (f32[1024,128]{1,0:T(8,128)S(1)}, f32[1024,128]{1,0:T(8,128)S(1)}, u32[]{:S(2)}, u32[]{:S(2)}) collective-permute-start(f32[1024,128]{1,0:T(8,128)S(1)} %bitcast.28), channel_id=1, source_target_pairs={{0,1},{1,0},{2,3},{3,2},{4,5},{5,4},{6,7},{7,6},{8,9},{9,8},{10,11... | collective-permute-start | bytes 1572872 | tf_op jit(solution)/shard_map/ppermute | solution.py:23
  58.4 24.5 %collective-permute-start.3 = (f32[128,256]{1,0:T(8,128)S(1)}, f32[128,256]{1,0:T(8,128)S(1)}, u32[]{:S(2)}, u32[]{:S(2)}) collective-permute-start(f32[128,256]{1,0:T(8,128)S(1)} %get-tuple-element.28.x_ref), channel_id=1, source_target_pairs={{0,1},{1,0},{2,3},{3,2},{4,5},{5,4},{6,7},{7,6},{8,9},{9,8},{10,11... | collective-permute-start | bytes 393224 | tf_op jit(solution)/shard_map/ppermute | solution.py:23
  125.1 9.6 %collective-permute-start.4 = (f32[1024,128]{1,0:T(8,128)S(1)}, f32[1024,128]{1,0:T(8,128)S(1)}, u32[]{:S(2)}, u32[]{:S(2)}) collective-permute-start(f32[1024,128]{1,0:T(8,128)S(1)} %bitcast.13), channel_id=1, source_target_pairs={{0,1},{1,0},{2,3},{3,2},{4,5},{5,4},{6,7},{7,6},{8,9},{9,8},{10,11... | collective-permute-start | bytes 1572872 | tf_op jit(solution)/shard_map/ppermute | solution.py:23
  128.6 7.1 %collective-permute-start.5 = (f32[264,128]{1,0:T(8,128)S(1)}, f32[264,128]{1,0:T(8,128)S(1)}, u32[]{:S(2)}, u32[]{:S(2)}) collective-permute-start(f32[264,128]{1,0:T(8,128)S(1)} %factors.1.after_ref.l_ref), channel_id=1, source_target_pairs={{0,1},{1,0},{2,3},{3,2},{4,5},{5,4},{6,7},{7,6},{8,9},{9,8},{10,11... | collective-permute-start | bytes 405512 | tf_op jit(solution)/shard_map/ppermute | solution.py:23

commit v11 on v10

--- a/solution.py
+++ b/solution.py
@@ -21,10 +21,6 @@
 
 def from_other_core(value):
     return lax.ppermute(value, "core", [(0, 1), (1, 0)])
-
-
-def to_second(value):
-    return lax.ppermute(value, "core", [(0, 1)])
 
 
 def call(kernel, name, shapes, arrays, scratch=(), space=pltpu.VMEM):
@@ -89,12 +85,23 @@
     return jnp.concatenate([left, right], axis=1)
 
 
-def first_columns_kernel(own_ref, start_ref, out_ref):
-    out_ref[...] = dot(own_ref[...], start_ref[...])
-
-
-def columns_kernel(other_ref, start_ref, columns_ref, out_ref):
-    out_ref[...] = columns_ref[...] + dot(other_ref[...], start_ref[...])
+def first_columns_kernel(own_ref, start_ref, keep_ref, send_ref):
+    first = lax.axis_index("core") == 0
+    columns = dot(own_ref[...], start_ref[...])
+    half = keep_ref.shape[0]
+    keep_ref[...] = jnp.where(first, columns[:half], columns[half:])
+    send_ref[...] = jnp.where(first, columns[half:], columns[:half])
+
+
+def columns_kernel(keep_ref, other_ref, out_ref):
+    out_ref[...] = keep_ref[...] + other_ref[...]
+
+
+def copies_kernel(own_ref, other_ref, out_ref):
+    rows = own_ref.shape[0]
+    for i in range(0, out_ref.shape[0], 2 * rows):
+        out_ref[i : i + rows, :] = own_ref[...]
+        out_ref[i + rows : i + 2 * rows, :] = other_ref[...]
 
 
 def sum_kernel(in_ref, out_ref, *, rows):
@@ -107,7 +114,8 @@
 
 
 def across_kernel(own_ref, other_ref, c_ref, x_ref, out_ref, unused_ref):
-    c = c_ref[...]
+    c = c_ref[...].reshape(lax.axis_size(PLANE), 2, -1, LANE)
+    c = jnp.concatenate([c[:, core].reshape(-1, LANE) for core in range(2)])
     c = c * inverse_or_zero(largest(c))
     x_ref[...] = dot(c, beside(own_ref[...], other_ref[...]), 0, 0)
     out_ref[...] = c
@@ -224,13 +232,13 @@
     return exchanged(values.reshape(count, -1, LANE), axis).reshape(values.shape)
 
 
-def summed_over_chips(part, name):
+def summed_pieces(part, name, pieces):
     rows = part.shape[0] // lax.axis_size(PLANE)
     kernel = functools.partial(sum_kernel, rows=rows)
     line = (lax.axis_size("z") * rows, LANE)
     (copies,) = call(kernel, name + "_plane", [line], [exchanged_rows(part, PLANE)])
-    (copies,) = call(kernel, name + "_line", [part.shape], [exchanged_rows(copies, "z")])
-    return exchanged_rows(copies, PLANE)
+    shapes = [(pieces * rows, LANE)]
+    return call(kernel, name + "_line", shapes, [exchanged_rows(copies, "z")])[0]
 
 
 def split(name, *sources):
@@ -247,32 +255,37 @@
 def on_device(hankel, shifted, start_basis):
     groups, rows_dev = lax.axis_size(ROWS), hankel.shape[0]
     rows = groups * rows_dev
-    start_other = from_other_core(start_basis)
-    shifted_other = to_second(shifted)
-    pieces, start_other = lax.optimization_barrier((split("split", hankel), start_other))
+    pieces, shifted_other = lax.optimization_barrier(
+        (split("split", hankel), from_other_core(shifted))
+    )
     own = exchanged(pieces, ROWS).reshape(rows, LANE)
+    halves = [(rows // 2, LANE)] * 2
+    keep, send = call(first_columns_kernel, "first_columns", halves, [own, start_basis])
+    received, own = lax.optimization_barrier((from_other_core(send), own))
     other = from_other_core(own)
-    (c_part,) = call(first_columns_kernel, "first_columns", [(rows, LANE)], [own, start_basis])
+    (c_part,) = call(columns_kernel, "columns", halves[:1], [keep, received])
+    piece = summed_pieces(c_part, "columns", 1)
+    piece_other = from_other_core(piece)
     both = (groups, 2 * rows_dev, LANE)
 
-    def project(own, other, c_part, start_other, shifted, shifted_other):
-        (c_part,) = call(columns_kernel, "columns", [(rows, LANE)], [other, start_other, c_part])
-        c = summed_over_chips(c_part, "columns")
+    def project(own, other, piece, piece_other, shifted, shifted_other):
+        (copies,) = call(copies_kernel, "copies", [(rows, LANE)], [piece, piece_other])
+        c = exchanged_rows(copies, PLANE)
         shapes = [(LANE, 2 * LANE), (rows, LANE), both]
         return tuple(call(across_kernel, "across", shapes, [own, other, c]))
 
-    def relay(own, other, c_part, start_other, shifted, shifted_other):
+    def relay(own, other, piece, piece_other, shifted, shifted_other):
         t = exchanged(split("split_shifted", shifted_other, shifted), ROWS)
         return jnp.zeros((LANE, 2 * LANE), jnp.float32), jnp.zeros((rows, LANE), jnp.float32), t
 
     x, c, t = lax.cond(
         lax.axis_index("core") == 0, project, relay,
-        own, other, c_part, start_other, shifted, shifted_other,
+        own, other, piece, piece_other, shifted, shifted_other,
     )
     x_other = from_other_core(x)
     (part,) = call(image_kernel, "image", [(rows, LANE)], [own, other, x])
     (part,) = call(second_image_kernel, "second_image", [(rows, LANE)], [t, x_other, part])
-    part = summed_over_chips(part, "image")
+    part = exchanged_rows(summed_pieces(part, "image", lax.axis_size(PLANE)), PLANE)
     part_other = from_other_core(part)
     (factors,) = call(factor_kernel, "factors", [(2 * LANE + SUB, LANE)], [part, c])
     (cross,) = call(cross_kernel, "cross", [(LANE, LANE)], [part, part_other, factors])

time: 137 us -> 143 us (1.044)
  blocking collectives: 63.5 us -> 112 us
  starting transfers between devices: 50 us -> 20.1 us
  waiting for transfers between devices: 15.7 us -> 3.5 us
    all_to_all x4 -> x7, blocking collectives: 63.5 us -> 112 us  [exchanged(): return lax.all_to_all(blocks, axis, 0, 0, tiled=True)]
    ppermute x5 -> x7, starting transfers between devices: 39.2 us -> 20.1 us  [from_other_core(): return lax.ppermute(value, 'core', [(0, 1), (1, 0)])]
    all_to_all x1 -> x0, waiting for transfers between devices: 13.6 us -> none  [exchanged(): return lax.all_to_all(blocks, axis, 0, 0, tiled=True)]
    all_to_all x1 -> x0, starting transfers between devices: 9.44 us -> none  [exchanged(): return lax.all_to_all(blocks, axis, 0, 0, tiled=True)]
    ppermute x5 -> x7, waiting for transfers between devices: 2.13 us -> 3.5 us  [from_other_core(): return lax.ppermute(value, 'core', [(0, 1), (1, 0)])]
    pallas_call x10 -> x13, Pallas kernels: 6.94 us -> 7.03 us  [call(): pl.pallas_call(kernel, name=name, out_shape=[jax.ShapeDtypeStruct(shape,...]
where the time goes in v11:
time: 143 us
  blocking collectives  112 us (78%)
  starting transfers between devices  20.1 us (14%)
  Pallas kernels  7.03 us (5%)
  waiting for transfers between devices  3.5 us (2%)
    all_to_all x7, blocking collectives, exchanged(): return lax.all_to_all(blocks, axis, 0, 0, tiled=True)  112 us
    ppermute x7, starting transfers between devices, from_other_core(): return lax.ppermute(value, 'core', [(0, 1), (1, 0)])  20.1 us
    pallas_call x13, Pallas kernels, call(): pl.pallas_call(kernel, name=name, out_shape=[jax.ShapeDtypeStruct(shape,...  7.03 us
    ppermute x7, waiting for transfers between devices, from_other_core(): return lax.ppermute(value, 'core', [(0, 1), (1, 0)])  3.5 us
  transfers between devices with their start and end apart: 7, of which 4 were waited for; matrix products, arithmetic and copies ran while one was open for 0% of the time, Pallas kernels for 2%

profile of v11, /device:TPU:1, one launch (start us, length us, event | category | flops | bytes accessed | tf_op | source)
XLA Modules:
  0.0 143.0 jit_solution(6826643888270388836)
XLA Ops:
  0.6 3.3 %collective-permute-start = (f32[32,4096]{1,0:T(8,128)}, f32[32,4096]{1,0:T(8,128)S(1)}, u32[]{:S(2)}, u32[]{:S(2)}) collective-permute-start(f32[32,4096]{1,0:T(8,128)} %param.6), channel_id=1, source_target_pairs={{0,1},{1,0},{2,3},{3,2},{4,5},{5,4},{6,7},{7,6},{8,9},{9,8},{10,11... | collective-permute-start | bytes 1572872 | tf_op jit(solution)/shard_map/ppermute | solution.py:23
  4.0 1.8 %split.1 = f32[32,32,128]{2,1,0:T(8,128)} custom-call(f32[32,4096]{1,0:T(8,128)} %refs_0_.1), custom_call_target="tpu_custom_call" | custom-call | tf_op jit(solution)/shard_map/split/pallas_call | solution.py:27
  5.8 0.0 copy-start
  5.8 0.0 collective-permute-done
  5.8 23.3 %all_to_all.40 = f32[32,32,128]{2,1,0:T(8,128)S(1)} all-to-all(f32[32,32,128]{2,1,0:T(8,128)} %split.1), channel_id=1, replica_groups=mesh['x'=4,'z'=8,'y'=4,'core'=2] {'x','z'}, dimensions={0} | all-to-all | bytes 1048576 | tf_op jit(solution)/shard_map/all_to_all | solution.py:19
  29.1 0.0 copy-done
  29.1 0.6 first_columns.1
  29.7 3.8 %collective-permute-start.1 = (f32[512,128]{1,0:T(8,128)S(1)}, f32[512,128]{1,0:T(8,128)S(1)}, u32[]{:S(2)}, u32[]{:S(2)}) collective-permute-start(f32[512,128]{1,0:T(8,128)S(1)} %get-tuple-element.32), channel_id=1, source_target_pairs={{0,1},{1,0},{2,3},{3,2},{4,5},{5,4},{6,7},{7,6},{8,9},{9,8},{10,11... | collective-permute-start | bytes 786440 | tf_op jit(solution)/shard_map/ppermute | solution.py:23
  33.5 1.2 collective-permute-done.1.other_ref
  34.6 0.4 collective-permute-start.3
  35.0 13.0 %all_to_all.41 = f32[16,32,128]{2,1,0:T(8,128)S(1)} all-to-all(f32[16,32,128]{2,1,0:T(8,128)S(1)} %bitcast.22), channel_id=1, replica_groups=mesh['x'=4,'z'=8,'y'=4,'core'=2] {'x','y'}, dimensions={0} | all-to-all | bytes 524288 | tf_op jit(solution)/shard_map/all_to_all | solution.py:19
  48.0 0.0 copy-start.1
  48.0 11.9 %all_to_all.42 = f32[8,32,128]{2,1,0:T(8,128)S(1)} all-to-all(f32[8,32,128]{2,1,0:T(8,128)S(1)} %bitcast.26), channel_id=1, replica_groups=mesh['x'=4,'z'=8,'y'=4,'core'=2] {'z'}, dimensions={0} | all-to-all | bytes 262144 | tf_op jit(solution)/shard_map/all_to_all | solution.py:19
  60.0 3.1 %collective-permute-start.2 = (f32[32,128]{1,0:T(8,128)S(1)}, f32[32,128]{1,0:T(8,128)S(1)}, u32[]{:S(2)}, u32[]{:S(2)}) collective-permute-start(f32[32,128]{1,0:T(8,128)S(1)} %columns_line.1), channel_id=1, source_target_pairs={{0,1},{1,0},{2,3},{3,2},{4,5},{5,4},{6,7},{7,6},{8,9},{9,8},{10,11... | collective-permute-start | bytes 49160 | tf_op jit(solution)/shard_map/ppermute | solution.py:23
  63.1 0.8 collective-permute-done.2
  63.9 0.0 collective-permute-done.3.other_ref
  63.9 0.0 copy-done.1
  63.9 22.4 %conditional.1 = ((f32[128,256]{1,0:T(8,128)S(1)}, f32[1024,128]{1,0:T(8,128)S(1)}, f32[32,64,128]{2,1,0:T(8,128)S(1)})) conditional(s32[]{:T(128)} %convert_element_type.3, (f32[32,4096]{1,0:T(8,128)S(1)}, f32[32,4096]{1,0:T(8,128)S(1)}) %tuple.25, (f32[32,128]{1,0:T(8,128)S(1)}, f32[32,128]{1,0:T(8,128)S(1)}, f32[1024,128]{1,0:T(8,128)S(1)}, ...), branch_computations={%region_0.0_spmd, %region_1.0_spmd} | conditional | bytes 2752552 | solution.py:281
  63.9 1.4 split_shifted.1
  65.4 20.9 %all_to_all.38 = f32[32,64,128]{2,1,0:T(8,128)S(1)} all-to-all(f32[32,64,128]{2,1,0:T(8,128)} %split_shifted.1), channel_id=1, replica_groups=mesh['x'=4,'z'=8,'y'=4,'core'=2] {'x','z'}, dimensions={0} | all-to-all | bytes 2097152 | tf_op jit(solution)/shard_map/cond/branch_0_fun/all_to_all | solution.py:19
  86.3 0.1 collective-permute-start.4
  86.5 1.3 collective-permute-done.4.x_ref
  87.8 1.0 second_image.1
  88.8 15.0 %all_to_all.43 = f32[16,64,128]{2,1,0:T(8,128)S(1)} all-to-all(f32[16,64,128]{2,1,0:T(8,128)S(1)} %bitcast.18), channel_id=1, replica_groups=mesh['x'=4,'z'=8,'y'=4,'core'=2] {'x','y'}, dimensions={0} | all-to-all | bytes 1048576 | tf_op jit(solution)/shard_map/all_to_all | solution.py:19
  103.8 15.2 %all_to_all.44 = f32[8,64,128]{2,1,0:T(8,128)S(1)} all-to-all(f32[8,64,128]{2,1,0:T(8,128)S(1)} %bitcast.23), channel_id=1, replica_groups=mesh['x'=4,'z'=8,'y'=4,'core'=2] {'z'}, dimensions={0} | all-to-all | bytes 524288 | tf_op jit(solution)/shard_map/all_to_all | solution.py:19
  119.1 12.3 %all_to_all.45 = f32[16,64,128]{2,1,0:T(8,128)S(1)} all-to-all(f32[16,64,128]{2,1,0:T(8,128)S(1)} %bitcast.20), channel_id=1, replica_groups=mesh['x'=4,'z'=8,'y'=4,'core'=2] {'x','y'}, dimensions={0} | all-to-all | bytes 1048576 | tf_op jit(solution)/shard_map/all_to_all | solution.py:19
  131.3 3.2 %collective-permute-start.5 = (f32[1024,128]{1,0:T(8,128)S(1)}, f32[1024,128]{1,0:T(8,128)S(1)}, u32[]{:S(2)}, u32[]{:S(2)}) collective-permute-start(f32[1024,128]{1,0:T(8,128)S(1)} %bitcast.13), channel_id=1, source_target_pairs={{0,1},{1,0},{2,3},{3,2},{4,5},{5,4},{6,7},{7,6},{8,9},{9,8},{10,11... | collective-permute-start | bytes 1572872 | tf_op jit(solution)/shard_map/ppermute | solution.py:23
  134.6 6.1 %collective-permute-start.6 = (f32[264,128]{1,0:T(8,128)S(1)}, f32[264,128]{1,0:T(8,128)S(1)}, u32[]{:S(2)}, u32[]{:S(2)}) collective-permute-start(f32[264,128]{1,0:T(8,128)S(1)} %factors.1.after_ref.l_ref), channel_id=1, source_target_pairs={{0,1},{1,0},{2,3},{3,2},{4,5},{5,4},{6,7},{7,6},{8,9},{9,8},{10,11... | collective-permute-start | bytes 405512 | tf_op jit(solution)/shard_map/ppermute | solution.py:23
  140.7 0.0 collective-permute-done.5.other_ref
  140.7 0.8 cross.1.cross_ref
  141.5 0.2 collective-permute-done.6.l_other_ref
  141.7 1.3 results.1
  (9 shorter events, 0.2 us)
Async XLA Ops:
  0.6 5.2 %collective-permute-start = (f32[32,4096]{1,0:T(8,128)}, f32[32,4096]{1,0:T(8,128)S(1)}, u32[]{:S(2)}, u32[]{:S(2)}) collective-permute-start(f32[32,4096]{1,0:T(8,128)} %param.6), channel_id=1, source_target_pairs={{0,1},{1,0},{2,3},{3,2},{4,5},{5,4},{6,7},{7,6},{8,9},{9,8},{10,11... | collective-permute-start | bytes 1572872 | tf_op jit(solution)/shard_map/ppermute | solution.py:23
  5.8 23.3 %copy-start = (f32[128,128]{1,0:T(8,128)S(1)}, f32[128,128]{1,0:T(8,128)}, u32[]{:S(2)}) copy-start(f32[128,128]{1,0:T(8,128)} %start_ref.1) | copy-start | bytes 196612
  29.7 5.0 %collective-permute-start.1 = (f32[512,128]{1,0:T(8,128)S(1)}, f32[512,128]{1,0:T(8,128)S(1)}, u32[]{:S(2)}, u32[]{:S(2)}) collective-permute-start(f32[512,128]{1,0:T(8,128)S(1)} %get-tuple-element.32), channel_id=1, source_target_pairs={{0,1},{1,0},{2,3},{3,2},{4,5},{5,4},{6,7},{7,6},{8,9},{9,8},{10,11... | collective-permute-start | bytes 786440 | tf_op jit(solution)/shard_map/ppermute | solution.py:23
  34.6 29.3 %collective-permute-start.3 = (f32[1024,128]{1,0:T(8,128)S(1)}, f32[1024,128]{1,0:T(8,128)S(1)}, u32[]{:S(2)}, u32[]{:S(2)}) collective-permute-start(f32[1024,128]{1,0:T(8,128)S(1)} %bitcast.29), channel_id=1, source_target_pairs={{0,1},{1,0},{2,3},{3,2},{4,5},{5,4},{6,7},{7,6},{8,9},{9,8},{10,11... | collective-permute-start | bytes 1572872 | tf_op jit(solution)/shard_map/ppermute | solution.py:23
  48.0 15.9 %copy-start.1 = (f32[32,4096]{1,0:T(8,128)S(1)}, f32[32,4096]{1,0:T(8,128)}, u32[]{:S(2)}) copy-start(f32[32,4096]{1,0:T(8,128)} %param.6) | copy-start | bytes 1572868
  60.0 3.9 %collective-permute-start.2 = (f32[32,128]{1,0:T(8,128)S(1)}, f32[32,128]{1,0:T(8,128)S(1)}, u32[]{:S(2)}, u32[]{:S(2)}) collective-permute-start(f32[32,128]{1,0:T(8,128)S(1)} %columns_line.1), channel_id=1, source_target_pairs={{0,1},{1,0},{2,3},{3,2},{4,5},{5,4},{6,7},{7,6},{8,9},{9,8},{10,11... | collective-permute-start | bytes 49160 | tf_op jit(solution)/shard_map/ppermute | solution.py:23
  86.3 1.4 %collective-permute-start.4 = (f32[128,256]{1,0:T(8,128)S(1)}, f32[128,256]{1,0:T(8,128)S(1)}, u32[]{:S(2)}, u32[]{:S(2)}) collective-permute-start(f32[128,256]{1,0:T(8,128)S(1)} %get-tuple-element.36.x_ref), channel_id=1, source_target_pairs={{0,1},{1,0},{2,3},{3,2},{4,5},{5,4},{6,7},{7,6},{8,9},{9,8},{10,11... | collective-permute-start | bytes 393224 | tf_op jit(solution)/shard_map/ppermute | solution.py:23
  131.3 9.4 %collective-permute-start.5 = (f32[1024,128]{1,0:T(8,128)S(1)}, f32[1024,128]{1,0:T(8,128)S(1)}, u32[]{:S(2)}, u32[]{:S(2)}) collective-permute-start(f32[1024,128]{1,0:T(8,128)S(1)} %bitcast.13), channel_id=1, source_target_pairs={{0,1},{1,0},{2,3},{3,2},{4,5},{5,4},{6,7},{7,6},{8,9},{9,8},{10,11... | collective-permute-start | bytes 1572872 | tf_op jit(solution)/shard_map/ppermute | solution.py:23
  134.6 7.1 %collective-permute-start.6 = (f32[264,128]{1,0:T(8,128)S(1)}, f32[264,128]{1,0:T(8,128)S(1)}, u32[]{:S(2)}, u32[]{:S(2)}) collective-permute-start(f32[264,128]{1,0:T(8,128)S(1)} %factors.1.after_ref.l_ref), channel_id=1, source_target_pairs={{0,1},{1,0},{2,3},{3,2},{4,5},{5,4},{6,7},{7,6},{8,9},{9,8},{10,11... | collective-permute-start | bytes 405512 | tf_op jit(solution)/shard_map/ppermute | solution.py:23

commit v12 on v10

--- a/solution.py
+++ b/solution.py
@@ -10,7 +10,7 @@
 
 ROWS = ("x", "z")
 COLS = ("y", "core")
-PLANE = ("x", "y")
+PLANE = ("y", "x")
 SUB, LANE = 8, 128
 PIECES = 4
 

time: 137 us -> 137 us (level)
  no operation moved by 1% of the time
where the time goes in v12:
time: 137 us
  blocking collectives  64.5 us (47%)
  starting transfers between devices  48.7 us (36%)
  waiting for transfers between devices  15.7 us (11%)
  Pallas kernels  6.94 us (5%)
    all_to_all x4, blocking collectives, exchanged(): return lax.all_to_all(blocks, axis, 0, 0, tiled=True)  64.5 us
    ppermute x5, starting transfers between devices, from_other_core(): return lax.ppermute(value, 'core', [(0, 1), (1, 0)])  37.9 us
    all_to_all x1, waiting for transfers between devices, exchanged(): return lax.all_to_all(blocks, axis, 0, 0, tiled=True)  13.6 us
    all_to_all x1, starting transfers between devices, exchanged(): return lax.all_to_all(blocks, axis, 0, 0, tiled=True)  9.44 us
    pallas_call x10, Pallas kernels, call(): pl.pallas_call(kernel, name=name, out_shape=[jax.ShapeDtypeStruct(shape,...  6.94 us
  transfers between devices with their start and end apart: 7, of which 4 were waited for; matrix products, arithmetic and copies ran while one was open for 0% of the time, Pallas kernels for 2%

profile of v12, /device:TPU:1, one launch (start us, length us, event | category | flops | bytes accessed | tf_op | source)
XLA Modules:
  0.0 136.6 jit_solution(14687188809093998779)
XLA Ops:
  0.6 3.3 %collective-permute-start.1 = (f32[128,128]{1,0:T(8,128)}, f32[128,128]{1,0:T(8,128)S(1)}, u32[]{:S(2)}, u32[]{:S(2)}) collective-permute-start(f32[128,128]{1,0:T(8,128)} %start_ref.1), channel_id=1, source_target_pairs={{0,1},{1,0},{2,3},{3,2},{4,5},{5,4},{6,7},{7,6},{8,9},{9,8},{10,11... | collective-permute-start | bytes 196616 | tf_op jit(solution)/shard_map/ppermute | solution.py:23
  4.0 1.8 %split.1 = f32[32,32,128]{2,1,0:T(8,128)} custom-call(f32[32,4096]{1,0:T(8,128)} %refs_0_.1), custom_call_target="tpu_custom_call" | custom-call | tf_op jit(solution)/shard_map/split/pallas_call | solution.py:31
  5.8 0.0 copy-start.1
  5.8 0.0 copy-start
  5.8 0.0 collective-permute-done.1
  5.8 9.4 %all-to-all-start.4 = ((f32[32,32,128]{2,1,0:T(8,128)}), f32[32,32,128]{2,1,0:T(8,128)S(1)}, u32[]{:S(2)}, u32[]{:S(2)}) async-start(f32[32,32,128]{2,1,0:T(8,128)} %split.1), calls=%async_computation.4 | async-start | bytes 1048576 | tf_op jit(solution)/shard_map/all_to_all | solution.py:19
  15.3 0.0 copy-done.1
  15.3 1.3 collective-permute-start
  16.6 13.6 %all-to-all-done.4 = f32[32,32,128]{2,1,0:T(8,128)S(1)} async-done(((f32[32,32,128]{2,1,0:T(8,128)}), f32[32,32,128]{2,1,0:T(8,128)S(1)}, u32[]{:S(2)}, u32[]{:S(2)}) %all-to-all-start.4) | async-done | bytes 524320 | tf_op jit(solution)/shard_map/all_to_all | solution.py:19
  30.2 2.8 %collective-permute-start.2 = (f32[1024,128]{1,0:T(8,128)S(1)}, f32[1024,128]{1,0:T(8,128)S(1)}, u32[]{:S(2)}, u32[]{:S(2)}) collective-permute-start(f32[1024,128]{1,0:T(8,128)S(1)} %bitcast.28), channel_id=1, source_target_pairs={{0,1},{1,0},{2,3},{3,2},{4,5},{5,4},{6,7},{7,6},{8,9},{9,8},{10,11... | collective-permute-start | bytes 1572872 | tf_op jit(solution)/shard_map/ppermute | solution.py:23
  33.0 0.0 collective-permute-done
  33.0 0.0 copy-done
  33.0 0.6 first_columns.1
  33.5 1.0 collective-permute-done.2.other_ref
  34.5 23.9 %conditional.1 = ((f32[128,256]{1,0:T(8,128)S(1)}, f32[1024,128]{1,0:T(8,128)S(1)}, f32[32,64,128]{2,1,0:T(8,128)S(1)})) conditional(s32[]{:T(128)} %convert_element_type.3, (f32[32,4096]{1,0:T(8,128)S(1)}, f32[32,4096]{1,0:T(8,128)S(1)}) %tuple.23, (f32[1024,128]{1,0:T(8,128)S(1)}, f32[128,128]{1,0:T(8,128)S(1)}, f32[1024,128]{1,0:T(8,128)S(1)}, ...), branch_computations={%region_0.0_spmd, %region_1.0_spmd} | conditional | bytes 2752552 | solution.py:268
  34.5 1.4 %split_shifted.1 = f32[32,64,128]{2,1,0:T(8,128)} custom-call(f32[32,4096]{1,0:T(8,128)S(1)} %get-tuple-element.12.refs_0_, f32[32,4096]{1,0:T(8,128)S(1)} %get-tuple-element.13.refs_1_), custom_call_target="tpu_custom_call" | custom-call | tf_op jit(solution)/shard_map/cond/branch_0_fun/split_shifted/pallas_call | solution.py:31
  35.9 22.4 %all_to_all.36 = f32[32,64,128]{2,1,0:T(8,128)S(1)} all-to-all(f32[32,64,128]{2,1,0:T(8,128)} %split_shifted.1), channel_id=1, replica_groups=mesh['x'=4,'z'=8,'y'=4,'core'=2] {'x','z'}, dimensions={0} | all-to-all | bytes 2097152 | tf_op jit(solution)/shard_map/cond/branch_0_fun/all_to_all | solution.py:19
  58.4 23.6 %collective-permute-start.3 = (f32[128,256]{1,0:T(8,128)S(1)}, f32[128,256]{1,0:T(8,128)S(1)}, u32[]{:S(2)}, u32[]{:S(2)}) collective-permute-start(f32[128,256]{1,0:T(8,128)S(1)} %get-tuple-element.28.x_ref), channel_id=1, source_target_pairs={{0,1},{1,0},{2,3},{3,2},{4,5},{5,4},{6,7},{7,6},{8,9},{9,8},{10,11... | collective-permute-start | bytes 393224 | tf_op jit(solution)/shard_map/ppermute | solution.py:23
  82.0 1.0 collective-permute-done.3.x_ref
  83.0 1.0 second_image.1
  84.0 14.8 %all_to_all.40 = f32[16,64,128]{2,1,0:T(8,128)S(1)} all-to-all(f32[16,64,128]{2,1,0:T(8,128)S(1)} %bitcast.18), channel_id=1, replica_groups=mesh['x'=4,'z'=8,'y'=4,'core'=2] {'y','x'}, dimensions={0} | all-to-all | bytes 1048576 | tf_op jit(solution)/shard_map/all_to_all | solution.py:19
  98.9 14.2 %all_to_all.41 = f32[8,64,128]{2,1,0:T(8,128)S(1)} all-to-all(f32[8,64,128]{2,1,0:T(8,128)S(1)} %bitcast.26), channel_id=1, replica_groups=mesh['x'=4,'z'=8,'y'=4,'core'=2] {'z'}, dimensions={0} | all-to-all | bytes 524288 | tf_op jit(solution)/shard_map/all_to_all | solution.py:19
  113.1 13.0 %all_to_all.42 = f32[16,64,128]{2,1,0:T(8,128)S(1)} all-to-all(f32[16,64,128]{2,1,0:T(8,128)S(1)} %bitcast.23), channel_id=1, replica_groups=mesh['x'=4,'z'=8,'y'=4,'core'=2] {'y','x'}, dimensions={0} | all-to-all | bytes 1048576 | tf_op jit(solution)/shard_map/all_to_all | solution.py:19
  126.1 2.1 %collective-permute-start.4 = (f32[1024,128]{1,0:T(8,128)S(1)}, f32[1024,128]{1,0:T(8,128)S(1)}, u32[]{:S(2)}, u32[]{:S(2)}) collective-permute-start(f32[1024,128]{1,0:T(8,128)S(1)} %bitcast.13), channel_id=1, source_target_pairs={{0,1},{1,0},{2,3},{3,2},{4,5},{5,4},{6,7},{7,6},{8,9},{9,8},{10,11... | collective-permute-start | bytes 1572872 | tf_op jit(solution)/shard_map/ppermute | solution.py:23
  128.2 6.1 %collective-permute-start.5 = (f32[264,128]{1,0:T(8,128)S(1)}, f32[264,128]{1,0:T(8,128)S(1)}, u32[]{:S(2)}, u32[]{:S(2)}) collective-permute-start(f32[264,128]{1,0:T(8,128)S(1)} %factors.1.after_ref.l_ref), channel_id=1, source_target_pairs={{0,1},{1,0},{2,3},{3,2},{4,5},{5,4},{6,7},{7,6},{8,9},{9,8},{10,11... | collective-permute-start | bytes 405512 | tf_op jit(solution)/shard_map/ppermute | solution.py:23
  134.4 0.0 collective-permute-done.4.other_ref
  134.4 0.8 cross.1.cross_ref
  135.2 0.2 collective-permute-done.5.l_other_ref
  135.3 1.3 results.1
  (6 shorter events, 0.1 us)
Async XLA Ops:
  0.6 5.2 %collective-permute-start.1 = (f32[128,128]{1,0:T(8,128)}, f32[128,128]{1,0:T(8,128)S(1)}, u32[]{:S(2)}, u32[]{:S(2)}) collective-permute-start(f32[128,128]{1,0:T(8,128)} %start_ref.1), channel_id=1, source_target_pairs={{0,1},{1,0},{2,3},{3,2},{4,5},{5,4},{6,7},{7,6},{8,9},{9,8},{10,11... | collective-permute-start | bytes 196616 | tf_op jit(solution)/shard_map/ppermute | solution.py:23
  5.8 9.5 %copy-start.1 = (f32[32,4096]{1,0:T(8,128)S(1)}, f32[32,4096]{1,0:T(8,128)}, u32[]{:S(2)}) copy-start(f32[32,4096]{1,0:T(8,128)} %param.6) | copy-start | bytes 1572868
  5.8 27.2 %copy-start = (f32[128,128]{1,0:T(8,128)S(1)}, f32[128,128]{1,0:T(8,128)}, u32[]{:S(2)}) copy-start(f32[128,128]{1,0:T(8,128)} %start_ref.1) | copy-start | bytes 196612
  5.8 24.3 %all-to-all-start.4 = ((f32[32,32,128]{2,1,0:T(8,128)}), f32[32,32,128]{2,1,0:T(8,128)S(1)}, u32[]{:S(2)}, u32[]{:S(2)}) async-start(f32[32,32,128]{2,1,0:T(8,128)} %split.1), calls=%async_computation.4 | async-start | bytes 1048576 | tf_op jit(solution)/shard_map/all_to_all | solution.py:19
  15.3 17.7 %collective-permute-start = (f32[32,4096]{1,0:T(8,128)S(1)}, f32[32,4096]{1,0:T(8,128)S(1)}, u32[]{:S(2)}, u32[]{:S(2)}) collective-permute-start(f32[32,4096]{1,0:T(8,128)S(1)} %copy-done.1), channel_id=1, source_target_pairs={{0,1},{2,3},{4,5},{6,7},{8,9},{10,11},{12,13},{14,15},{16,17},{18,... | collective-permute-start | bytes 1572872 | tf_op jit(solution)/shard_map/ppermute | solution.py:27
  30.2 4.3 %collective-permute-start.2 = (f32[1024,128]{1,0:T(8,128)S(1)}, f32[1024,128]{1,0:T(8,128)S(1)}, u32[]{:S(2)}, u32[]{:S(2)}) collective-permute-start(f32[1024,128]{1,0:T(8,128)S(1)} %bitcast.28), channel_id=1, source_target_pairs={{0,1},{1,0},{2,3},{3,2},{4,5},{5,4},{6,7},{7,6},{8,9},{9,8},{10,11... | collective-permute-start | bytes 1572872 | tf_op jit(solution)/shard_map/ppermute | solution.py:23
  58.4 24.5 %collective-permute-start.3 = (f32[128,256]{1,0:T(8,128)S(1)}, f32[128,256]{1,0:T(8,128)S(1)}, u32[]{:S(2)}, u32[]{:S(2)}) collective-permute-start(f32[128,256]{1,0:T(8,128)S(1)} %get-tuple-element.28.x_ref), channel_id=1, source_target_pairs={{0,1},{1,0},{2,3},{3,2},{4,5},{5,4},{6,7},{7,6},{8,9},{9,8},{10,11... | collective-permute-start | bytes 393224 | tf_op jit(solution)/shard_map/ppermute | solution.py:23
  126.1 8.3 %collective-permute-start.4 = (f32[1024,128]{1,0:T(8,128)S(1)}, f32[1024,128]{1,0:T(8,128)S(1)}, u32[]{:S(2)}, u32[]{:S(2)}) collective-permute-start(f32[1024,128]{1,0:T(8,128)S(1)} %bitcast.13), channel_id=1, source_target_pairs={{0,1},{1,0},{2,3},{3,2},{4,5},{5,4},{6,7},{7,6},{8,9},{9,8},{10,11... | collective-permute-start | bytes 1572872 | tf_op jit(solution)/shard_map/ppermute | solution.py:23
  128.2 7.1 %collective-permute-start.5 = (f32[264,128]{1,0:T(8,128)S(1)}, f32[264,128]{1,0:T(8,128)S(1)}, u32[]{:S(2)}, u32[]{:S(2)}) collective-permute-start(f32[264,128]{1,0:T(8,128)S(1)} %factors.1.after_ref.l_ref), channel_id=1, source_target_pairs={{0,1},{1,0},{2,3},{3,2},{4,5},{5,4},{6,7},{7,6},{8,9},{9,8},{10,11... | collective-permute-start | bytes 405512 | tf_op jit(solution)/shard_map/ppermute | solution.py:23

commit v13 on v10

--- a/solution.py
+++ b/solution.py
@@ -21,10 +21,6 @@
 
 def from_other_core(value):
     return lax.ppermute(value, "core", [(0, 1), (1, 0)])
-
-
-def to_second(value):
-    return lax.ppermute(value, "core", [(0, 1)])
 
 
 def call(kernel, name, shapes, arrays, scratch=(), space=pltpu.VMEM):
@@ -248,8 +244,10 @@
     groups, rows_dev = lax.axis_size(ROWS), hankel.shape[0]
     rows = groups * rows_dev
     start_other = from_other_core(start_basis)
-    shifted_other = to_second(shifted)
-    pieces, start_other = lax.optimization_barrier((split("split", hankel), start_other))
+    shifted_other = from_other_core(shifted)
+    pieces, start_other, shifted_other = lax.optimization_barrier(
+        (split("split", hankel), start_other, shifted_other)
+    )
     own = exchanged(pieces, ROWS).reshape(rows, LANE)
     other = from_other_core(own)
     (c_part,) = call(first_columns_kernel, "first_columns", [(rows, LANE)], [own, start_basis])

time: 137 us -> 137 us (level)
  blocking collectives: 63.5 us -> 87.1 us
  waiting for transfers between devices: 15.7 us -> 2.14 us
  starting transfers between devices: 50 us -> 39.6 us
    all_to_all x4 -> x5, blocking collectives: 63.5 us -> 87.1 us  [exchanged(): return lax.all_to_all(blocks, axis, 0, 0, tiled=True)]
    all_to_all x1 -> x0, waiting for transfers between devices: 13.6 us -> none  [exchanged(): return lax.all_to_all(blocks, axis, 0, 0, tiled=True)]
    all_to_all x1 -> x0, starting transfers between devices: 9.44 us -> none  [exchanged(): return lax.all_to_all(blocks, axis, 0, 0, tiled=True)]
    ppermute x5 -> x6, starting transfers between devices: 39.2 us -> 39.6 us  [from_other_core(): return lax.ppermute(value, 'core', [(0, 1), (1, 0)])]
  transfers between devices with their start and end apart: 7 -> 6, of which waited for: 4 -> 3; matrix products, arithmetic and copies ran while one was open for 0% -> 0% of each run, Pallas kernels for 2% -> 2%
where the time goes in v13:
time: 137 us
  blocking collectives  87.1 us (64%)
  starting transfers between devices  39.6 us (29%)
  Pallas kernels  6.93 us (5%)
  waiting for transfers between devices  2.14 us (2%)
    all_to_all x5, blocking collectives, exchanged(): return lax.all_to_all(blocks, axis, 0, 0, tiled=True)  87.1 us
    ppermute x6, starting transfers between devices, from_other_core(): return lax.ppermute(value, 'core', [(0, 1), (1, 0)])  39.6 us
    pallas_call x10, Pallas kernels, call(): pl.pallas_call(kernel, name=name, out_shape=[jax.ShapeDtypeStruct(shape,...  6.93 us
  transfers between devices with their start and end apart: 6, of which 3 were waited for; matrix products, arithmetic and copies ran while one was open for 0% of the time, Pallas kernels for 2%

profile of v13, /device:TPU:1, one launch (start us, length us, event | category | flops | bytes accessed | tf_op | source)
XLA Modules:
  0.0 136.6 jit_solution(2549572439685767499)
XLA Ops:
  0.6 3.3 %collective-permute-start.1 = (f32[32,4096]{1,0:T(8,128)}, f32[32,4096]{1,0:T(8,128)S(1)}, u32[]{:S(2)}, u32[]{:S(2)}) collective-permute-start(f32[32,4096]{1,0:T(8,128)} %param.6), channel_id=1, source_target_pairs={{0,1},{1,0},{2,3},{3,2},{4,5},{5,4},{6,7},{7,6},{8,9},{9,8},{10,11... | collective-permute-start | bytes 1572872 | tf_op jit(solution)/shard_map/ppermute | solution.py:23
  4.0 0.1 collective-permute-start
  4.1 1.8 %split.1 = f32[32,32,128]{2,1,0:T(8,128)} custom-call(f32[32,4096]{1,0:T(8,128)} %refs_0_.1), custom_call_target="tpu_custom_call" | custom-call | tf_op jit(solution)/shard_map/split/pallas_call | solution.py:27
  5.9 0.0 copy-start
  5.9 0.0 collective-permute-done
  5.9 0.0 collective-permute-done.1
  5.9 23.5 %all_to_all.40 = f32[32,32,128]{2,1,0:T(8,128)S(1)} all-to-all(f32[32,32,128]{2,1,0:T(8,128)} %split.1), channel_id=1, replica_groups=mesh['x'=4,'z'=8,'y'=4,'core'=2] {'x','z'}, dimensions={0} | all-to-all | bytes 1048576 | tf_op jit(solution)/shard_map/all_to_all | solution.py:19
  29.4 3.5 %collective-permute-start.2 = (f32[1024,128]{1,0:T(8,128)S(1)}, f32[1024,128]{1,0:T(8,128)S(1)}, u32[]{:S(2)}, u32[]{:S(2)}) collective-permute-start(f32[1024,128]{1,0:T(8,128)S(1)} %bitcast.28), channel_id=1, source_target_pairs={{0,1},{1,0},{2,3},{3,2},{4,5},{5,4},{6,7},{7,6},{8,9},{9,8},{10,11... | collective-permute-start | bytes 1572872 | tf_op jit(solution)/shard_map/ppermute | solution.py:23
  32.9 0.0 copy-done
  32.9 0.0 copy-start.1
  32.9 0.6 first_columns.1
  33.5 1.0 collective-permute-done.2.other_ref
  34.4 0.0 copy-done.1
  34.4 24.0 %conditional.1 = ((f32[128,256]{1,0:T(8,128)S(1)}, f32[1024,128]{1,0:T(8,128)S(1)}, f32[32,64,128]{2,1,0:T(8,128)S(1)})) conditional(s32[]{:T(128)} %convert_element_type.3, (f32[32,4096]{1,0:T(8,128)S(1)}, f32[32,4096]{1,0:T(8,128)S(1)}) %tuple.23, (f32[1024,128]{1,0:T(8,128)S(1)}, f32[128,128]{1,0:T(8,128)S(1)}, f32[1024,128]{1,0:T(8,128)S(1)}, ...), branch_computations={%region_0.0_spmd, %region_1.0_spmd} | conditional | bytes 2752552 | solution.py:266
  34.4 1.4 %split_shifted.1 = f32[32,64,128]{2,1,0:T(8,128)} custom-call(f32[32,4096]{1,0:T(8,128)S(1)} %get-tuple-element.12.refs_0_, f32[32,4096]{1,0:T(8,128)S(1)} %get-tuple-element.13.refs_1_), custom_call_target="tpu_custom_call" | custom-call | tf_op jit(solution)/shard_map/cond/branch_0_fun/split_shifted/pallas_call | solution.py:27
  35.8 22.5 %all_to_all.36 = f32[32,64,128]{2,1,0:T(8,128)S(1)} all-to-all(f32[32,64,128]{2,1,0:T(8,128)} %split_shifted.1), channel_id=1, replica_groups=mesh['x'=4,'z'=8,'y'=4,'core'=2] {'x','z'}, dimensions={0} | all-to-all | bytes 2097152 | tf_op jit(solution)/shard_map/cond/branch_0_fun/all_to_all | solution.py:19
  58.4 23.1 %collective-permute-start.3 = (f32[128,256]{1,0:T(8,128)S(1)}, f32[128,256]{1,0:T(8,128)S(1)}, u32[]{:S(2)}, u32[]{:S(2)}) collective-permute-start(f32[128,256]{1,0:T(8,128)S(1)} %get-tuple-element.30.x_ref), channel_id=1, source_target_pairs={{0,1},{1,0},{2,3},{3,2},{4,5},{5,4},{6,7},{7,6},{8,9},{9,8},{10,11... | collective-permute-start | bytes 393224 | tf_op jit(solution)/shard_map/ppermute | solution.py:23
  81.5 1.0 collective-permute-done.3.x_ref
  82.5 1.0 second_image.1
  83.5 14.9 %all_to_all.41 = f32[16,64,128]{2,1,0:T(8,128)S(1)} all-to-all(f32[16,64,128]{2,1,0:T(8,128)S(1)} %bitcast.18), channel_id=1, replica_groups=mesh['x'=4,'z'=8,'y'=4,'core'=2] {'x','y'}, dimensions={0} | all-to-all | bytes 1048576 | tf_op jit(solution)/shard_map/all_to_all | solution.py:19
  98.4 14.2 %all_to_all.42 = f32[8,64,128]{2,1,0:T(8,128)S(1)} all-to-all(f32[8,64,128]{2,1,0:T(8,128)S(1)} %bitcast.26), channel_id=1, replica_groups=mesh['x'=4,'z'=8,'y'=4,'core'=2] {'z'}, dimensions={0} | all-to-all | bytes 524288 | tf_op jit(solution)/shard_map/all_to_all | solution.py:19
  112.7 12.0 %all_to_all.43 = f32[16,64,128]{2,1,0:T(8,128)S(1)} all-to-all(f32[16,64,128]{2,1,0:T(8,128)S(1)} %bitcast.23), channel_id=1, replica_groups=mesh['x'=4,'z'=8,'y'=4,'core'=2] {'x','y'}, dimensions={0} | all-to-all | bytes 1048576 | tf_op jit(solution)/shard_map/all_to_all | solution.py:19
  124.7 3.4 %collective-permute-start.4 = (f32[1024,128]{1,0:T(8,128)S(1)}, f32[1024,128]{1,0:T(8,128)S(1)}, u32[]{:S(2)}, u32[]{:S(2)}) collective-permute-start(f32[1024,128]{1,0:T(8,128)S(1)} %bitcast.13), channel_id=1, source_target_pairs={{0,1},{1,0},{2,3},{3,2},{4,5},{5,4},{6,7},{7,6},{8,9},{9,8},{10,11... | collective-permute-start | bytes 1572872 | tf_op jit(solution)/shard_map/ppermute | solution.py:23
  128.2 6.1 %collective-permute-start.5 = (f32[264,128]{1,0:T(8,128)S(1)}, f32[264,128]{1,0:T(8,128)S(1)}, u32[]{:S(2)}, u32[]{:S(2)}) collective-permute-start(f32[264,128]{1,0:T(8,128)S(1)} %factors.1.after_ref.l_ref), channel_id=1, source_target_pairs={{0,1},{1,0},{2,3},{3,2},{4,5},{5,4},{6,7},{7,6},{8,9},{9,8},{10,11... | collective-permute-start | bytes 405512 | tf_op jit(solution)/shard_map/ppermute | solution.py:23
  134.3 0.0 collective-permute-done.4.other_ref
  134.3 0.8 cross.1.cross_ref
  135.1 0.2 collective-permute-done.5.l_other_ref
  135.3 1.3 results.1
  (6 shorter events, 0.1 us)
Async XLA Ops:
  0.6 5.3 %collective-permute-start.1 = (f32[32,4096]{1,0:T(8,128)}, f32[32,4096]{1,0:T(8,128)S(1)}, u32[]{:S(2)}, u32[]{:S(2)}) collective-permute-start(f32[32,4096]{1,0:T(8,128)} %param.6), channel_id=1, source_target_pairs={{0,1},{1,0},{2,3},{3,2},{4,5},{5,4},{6,7},{7,6},{8,9},{9,8},{10,11... | collective-permute-start | bytes 1572872 | tf_op jit(solution)/shard_map/ppermute | solution.py:23
  4.0 1.9 %collective-permute-start = (f32[128,128]{1,0:T(8,128)}, f32[128,128]{1,0:T(8,128)S(1)}, u32[]{:S(2)}, u32[]{:S(2)}) collective-permute-start(f32[128,128]{1,0:T(8,128)} %start_ref.1), channel_id=1, source_target_pairs={{0,1},{1,0},{2,3},{3,2},{4,5},{5,4},{6,7},{7,6},{8,9},{9,8},{10,11... | collective-permute-start | bytes 196616 | tf_op jit(solution)/shard_map/ppermute | solution.py:23
  5.9 27.0 %copy-start = (f32[128,128]{1,0:T(8,128)S(1)}, f32[128,128]{1,0:T(8,128)}, u32[]{:S(2)}) copy-start(f32[128,128]{1,0:T(8,128)} %start_ref.1) | copy-start | bytes 196612
  29.4 5.0 %collective-permute-start.2 = (f32[1024,128]{1,0:T(8,128)S(1)}, f32[1024,128]{1,0:T(8,128)S(1)}, u32[]{:S(2)}, u32[]{:S(2)}) collective-permute-start(f32[1024,128]{1,0:T(8,128)S(1)} %bitcast.28), channel_id=1, source_target_pairs={{0,1},{1,0},{2,3},{3,2},{4,5},{5,4},{6,7},{7,6},{8,9},{9,8},{10,11... | collective-permute-start | bytes 1572872 | tf_op jit(solution)/shard_map/ppermute | solution.py:23
  32.9 1.5 %copy-start.1 = (f32[32,4096]{1,0:T(8,128)S(1)}, f32[32,4096]{1,0:T(8,128)}, u32[]{:S(2)}) copy-start(f32[32,4096]{1,0:T(8,128)} %param.6) | copy-start | bytes 1572868
  58.4 24.1 %collective-permute-start.3 = (f32[128,256]{1,0:T(8,128)S(1)}, f32[128,256]{1,0:T(8,128)S(1)}, u32[]{:S(2)}, u32[]{:S(2)}) collective-permute-start(f32[128,256]{1,0:T(8,128)S(1)} %get-tuple-element.30.x_ref), channel_id=1, source_target_pairs={{0,1},{1,0},{2,3},{3,2},{4,5},{5,4},{6,7},{7,6},{8,9},{9,8},{10,11... | collective-permute-start | bytes 393224 | tf_op jit(solution)/shard_map/ppermute | solution.py:23
  124.7 9.6 %collective-permute-start.4 = (f32[1024,128]{1,0:T(8,128)S(1)}, f32[1024,128]{1,0:T(8,128)S(1)}, u32[]{:S(2)}, u32[]{:S(2)}) collective-permute-start(f32[1024,128]{1,0:T(8,128)S(1)} %bitcast.13), channel_id=1, source_target_pairs={{0,1},{1,0},{2,3},{3,2},{4,5},{5,4},{6,7},{7,6},{8,9},{9,8},{10,11... | collective-permute-start | bytes 1572872 | tf_op jit(solution)/shard_map/ppermute | solution.py:23
  128.2 7.1 %collective-permute-start.5 = (f32[264,128]{1,0:T(8,128)S(1)}, f32[264,128]{1,0:T(8,128)S(1)}, u32[]{:S(2)}, u32[]{:S(2)}) collective-permute-start(f32[264,128]{1,0:T(8,128)S(1)} %factors.1.after_ref.l_ref), channel_id=1, source_target_pairs={{0,1},{1,0},{2,3},{3,2},{4,5},{5,4},{6,7},{7,6},{8,9},{9,8},{10,11... | collective-permute-start | bytes 405512 | tf_op jit(solution)/shard_map/ppermute | solution.py:23

commit v14 on v13

--- a/solution.py
+++ b/solution.py
@@ -29,7 +29,7 @@
         name=name,
         out_shape=[jax.ShapeDtypeStruct(shape, jnp.float32) for shape in shapes],
         in_specs=[pl.BlockSpec(memory_space=space)] * len(arrays),
-        out_specs=[pl.BlockSpec(memory_space=space)] * len(shapes),
+        out_specs=[pl.BlockSpec(memory_space=pltpu.VMEM)] * len(shapes),
         scratch_shapes=scratch,
         compiler_params=pltpu.CompilerParams(vmem_limit_bytes=(24 if space is pltpu.VMEM else 60) << 20),
     )(*arrays)
@@ -54,17 +54,17 @@
 
 
 def split_kernel(*refs):
-    count = (len(refs) - 4) // 2
+    count = (len(refs) - 2) // 2
     sources, out_ref = refs[:count], refs[count]
-    blocks, out, in_sem, out_sem = refs[count + 1 : 2 * count + 1], *refs[2 * count + 1 :]
-    groups, _, lanes = out.shape
-    some, rows = groups // PIECES, out.shape[1] // count
-    loads, stores = [], []
+    blocks, sem = refs[count + 1 : 2 * count + 1], refs[2 * count + 1]
+    groups, _, lanes = out_ref.shape
+    some, rows = groups // PIECES, out_ref.shape[1] // count
+    loads = []
     for i in range(PIECES):
         at = slice(i * some * lanes, (i + 1) * some * lanes)
         for j in range(count):
             load = pltpu.make_async_copy(
-                sources[j].at[:, at], blocks[j].at[:, at], in_sem.at[count * i + j]
+                sources[j].at[:, at], blocks[j].at[:, at], sem.at[count * i + j]
             )
             load.start()
             loads.append(load)
@@ -72,13 +72,8 @@
         for j in range(count):
             loads[count * i + j].wait()
             for g in range(i * some, (i + 1) * some):
-                out[g, j * rows : (j + 1) * rows, :] = blocks[j][:, g * lanes : (g + 1) * lanes]
-        at = slice(i * some, (i + 1) * some)
-        store = pltpu.make_async_copy(out.at[at], out_ref.at[at], out_sem.at[i])
-        store.start()
-        stores.append(store)
-    for store in stores:
-        store.wait()
+                block = blocks[j][:, g * lanes : (g + 1) * lanes]
+                out_ref[g, j * rows : (j + 1) * rows, :] = block
 
 
 def beside(left, right):
@@ -233,9 +228,7 @@
     rows, cols = sources[0].shape
     shape = (lax.axis_size(ROWS), len(sources) * rows, LANE)
     scratch = [pltpu.VMEM((rows, cols), jnp.float32)] * len(sources) + [
-        pltpu.VMEM(shape, jnp.float32),
         pltpu.SemaphoreType.DMA((len(sources) * PIECES,)),
-        pltpu.SemaphoreType.DMA((PIECES,)),
     ]
     return call(split_kernel, name, [shape], sources, scratch, pl.ANY)[0]
 

time: 137 us -> 137 us (level)
  no operation moved by 1% of the time
where the time goes in v14:
time: 137 us
  blocking collectives  87.1 us (64%)
  starting transfers between devices  39.6 us (29%)
  Pallas kernels  7.08 us (5%)
  waiting for transfers between devices  2.13 us (2%)
    all_to_all x5, blocking collectives, exchanged(): return lax.all_to_all(blocks, axis, 0, 0, tiled=True)  87.1 us
    ppermute x6, starting transfers between devices, from_other_core(): return lax.ppermute(value, 'core', [(0, 1), (1, 0)])  39.6 us
    pallas_call x10, Pallas kernels, call(): pl.pallas_call(kernel, name=name, out_shape=[jax.ShapeDtypeStruct(shape,...  7.08 us
  transfers between devices with their start and end apart: 6, of which 3 were waited for; matrix products, arithmetic and copies ran while one was open for 0% of the time, Pallas kernels for 2%

profile of v14, /device:TPU:1, one launch (start us, length us, event | category | flops | bytes accessed | tf_op | source)
XLA Modules:
  0.0 136.7 jit_solution(8832429564708581518)
XLA Ops:
  0.6 3.3 %collective-permute-start.1 = (f32[32,4096]{1,0:T(8,128)}, f32[32,4096]{1,0:T(8,128)S(1)}, u32[]{:S(2)}, u32[]{:S(2)}) collective-permute-start(f32[32,4096]{1,0:T(8,128)} %param.6), channel_id=1, source_target_pairs={{0,1},{1,0},{2,3},{3,2},{4,5},{5,4},{6,7},{7,6},{8,9},{9,8},{10,11... | collective-permute-start | bytes 1572872 | tf_op jit(solution)/shard_map/ppermute | solution.py:23
  4.0 0.1 collective-permute-start
  4.1 1.9 %split.1 = f32[32,32,128]{2,1,0:T(8,128)} custom-call(f32[32,4096]{1,0:T(8,128)} %refs_0_.1), custom_call_target="tpu_custom_call" | custom-call | tf_op jit(solution)/shard_map/split/pallas_call | solution.py:27
  6.0 0.0 copy-start
  6.0 0.0 collective-permute-done
  6.0 0.0 collective-permute-done.1
  6.0 23.5 %all_to_all.40 = f32[32,32,128]{2,1,0:T(8,128)S(1)} all-to-all(f32[32,32,128]{2,1,0:T(8,128)} %split.1), channel_id=1, replica_groups=mesh['x'=4,'z'=8,'y'=4,'core'=2] {'x','z'}, dimensions={0} | all-to-all | bytes 1048576 | tf_op jit(solution)/shard_map/all_to_all | solution.py:19
  29.5 3.5 %collective-permute-start.2 = (f32[1024,128]{1,0:T(8,128)S(1)}, f32[1024,128]{1,0:T(8,128)S(1)}, u32[]{:S(2)}, u32[]{:S(2)}) collective-permute-start(f32[1024,128]{1,0:T(8,128)S(1)} %bitcast.28), channel_id=1, source_target_pairs={{0,1},{1,0},{2,3},{3,2},{4,5},{5,4},{6,7},{7,6},{8,9},{9,8},{10,11... | collective-permute-start | bytes 1572872 | tf_op jit(solution)/shard_map/ppermute | solution.py:23
  33.0 0.0 copy-done
  33.0 0.0 copy-start.1
  33.0 0.6 first_columns.1
  33.6 1.0 collective-permute-done.2.other_ref
  34.5 0.0 copy-done.1
  34.5 24.0 %conditional.1 = ((f32[128,256]{1,0:T(8,128)S(1)}, f32[1024,128]{1,0:T(8,128)S(1)}, f32[32,64,128]{2,1,0:T(8,128)S(1)})) conditional(s32[]{:T(128)} %convert_element_type.3, (f32[32,4096]{1,0:T(8,128)S(1)}, f32[32,4096]{1,0:T(8,128)S(1)}) %tuple.23, (f32[1024,128]{1,0:T(8,128)S(1)}, f32[128,128]{1,0:T(8,128)S(1)}, f32[1024,128]{1,0:T(8,128)S(1)}, ...), branch_computations={%region_0.0_spmd, %region_1.0_spmd} | conditional | bytes 2752552 | solution.py:259
  34.5 1.5 %split_shifted.1 = f32[32,64,128]{2,1,0:T(8,128)} custom-call(f32[32,4096]{1,0:T(8,128)S(1)} %get-tuple-element.12.refs_0_, f32[32,4096]{1,0:T(8,128)S(1)} %get-tuple-element.13.refs_1_), custom_call_target="tpu_custom_call" | custom-call | tf_op jit(solution)/shard_map/cond/branch_0_fun/split_shifted/pallas_call | solution.py:27
  36.0 22.5 %all_to_all.36 = f32[32,64,128]{2,1,0:T(8,128)S(1)} all-to-all(f32[32,64,128]{2,1,0:T(8,128)} %split_shifted.1), channel_id=1, replica_groups=mesh['x'=4,'z'=8,'y'=4,'core'=2] {'x','z'}, dimensions={0} | all-to-all | bytes 2097152 | tf_op jit(solution)/shard_map/cond/branch_0_fun/all_to_all | solution.py:19
  58.5 23.1 %collective-permute-start.3 = (f32[128,256]{1,0:T(8,128)S(1)}, f32[128,256]{1,0:T(8,128)S(1)}, u32[]{:S(2)}, u32[]{:S(2)}) collective-permute-start(f32[128,256]{1,0:T(8,128)S(1)} %get-tuple-element.30.x_ref), channel_id=1, source_target_pairs={{0,1},{1,0},{2,3},{3,2},{4,5},{5,4},{6,7},{7,6},{8,9},{9,8},{10,11... | collective-permute-start | bytes 393224 | tf_op jit(solution)/shard_map/ppermute | solution.py:23
  81.6 1.0 collective-permute-done.3.x_ref
  82.6 1.0 second_image.1
  83.6 14.9 %all_to_all.41 = f32[16,64,128]{2,1,0:T(8,128)S(1)} all-to-all(f32[16,64,128]{2,1,0:T(8,128)S(1)} %bitcast.18), channel_id=1, replica_groups=mesh['x'=4,'z'=8,'y'=4,'core'=2] {'x','y'}, dimensions={0} | all-to-all | bytes 1048576 | tf_op jit(solution)/shard_map/all_to_all | solution.py:19
  98.5 14.2 %all_to_all.42 = f32[8,64,128]{2,1,0:T(8,128)S(1)} all-to-all(f32[8,64,128]{2,1,0:T(8,128)S(1)} %bitcast.26), channel_id=1, replica_groups=mesh['x'=4,'z'=8,'y'=4,'core'=2] {'z'}, dimensions={0} | all-to-all | bytes 524288 | tf_op jit(solution)/shard_map/all_to_all | solution.py:19
  112.8 12.0 %all_to_all.43 = f32[16,64,128]{2,1,0:T(8,128)S(1)} all-to-all(f32[16,64,128]{2,1,0:T(8,128)S(1)} %bitcast.23), channel_id=1, replica_groups=mesh['x'=4,'z'=8,'y'=4,'core'=2] {'x','y'}, dimensions={0} | all-to-all | bytes 1048576 | tf_op jit(solution)/shard_map/all_to_all | solution.py:19
  124.8 3.4 %collective-permute-start.4 = (f32[1024,128]{1,0:T(8,128)S(1)}, f32[1024,128]{1,0:T(8,128)S(1)}, u32[]{:S(2)}, u32[]{:S(2)}) collective-permute-start(f32[1024,128]{1,0:T(8,128)S(1)} %bitcast.13), channel_id=1, source_target_pairs={{0,1},{1,0},{2,3},{3,2},{4,5},{5,4},{6,7},{7,6},{8,9},{9,8},{10,11... | collective-permute-start | bytes 1572872 | tf_op jit(solution)/shard_map/ppermute | solution.py:23
  128.3 6.1 %collective-permute-start.5 = (f32[264,128]{1,0:T(8,128)S(1)}, f32[264,128]{1,0:T(8,128)S(1)}, u32[]{:S(2)}, u32[]{:S(2)}) collective-permute-start(f32[264,128]{1,0:T(8,128)S(1)} %factors.1.after_ref.l_ref), channel_id=1, source_target_pairs={{0,1},{1,0},{2,3},{3,2},{4,5},{5,4},{6,7},{7,6},{8,9},{9,8},{10,11... | collective-permute-start | bytes 405512 | tf_op jit(solution)/shard_map/ppermute | solution.py:23
  134.4 0.0 collective-permute-done.4.other_ref
  134.4 0.8 cross.1.cross_ref
  135.2 0.2 collective-permute-done.5.l_other_ref
  135.4 1.3 results.1
  (6 shorter events, 0.1 us)
Async XLA Ops:
  0.6 5.4 %collective-permute-start.1 = (f32[32,4096]{1,0:T(8,128)}, f32[32,4096]{1,0:T(8,128)S(1)}, u32[]{:S(2)}, u32[]{:S(2)}) collective-permute-start(f32[32,4096]{1,0:T(8,128)} %param.6), channel_id=1, source_target_pairs={{0,1},{1,0},{2,3},{3,2},{4,5},{5,4},{6,7},{7,6},{8,9},{9,8},{10,11... | collective-permute-start | bytes 1572872 | tf_op jit(solution)/shard_map/ppermute | solution.py:23
  4.0 2.0 %collective-permute-start = (f32[128,128]{1,0:T(8,128)}, f32[128,128]{1,0:T(8,128)S(1)}, u32[]{:S(2)}, u32[]{:S(2)}) collective-permute-start(f32[128,128]{1,0:T(8,128)} %start_ref.1), channel_id=1, source_target_pairs={{0,1},{1,0},{2,3},{3,2},{4,5},{5,4},{6,7},{7,6},{8,9},{9,8},{10,11... | collective-permute-start | bytes 196616 | tf_op jit(solution)/shard_map/ppermute | solution.py:23
  6.0 27.0 %copy-start = (f32[128,128]{1,0:T(8,128)S(1)}, f32[128,128]{1,0:T(8,128)}, u32[]{:S(2)}) copy-start(f32[128,128]{1,0:T(8,128)} %start_ref.1) | copy-start | bytes 196612
  29.5 5.0 %collective-permute-start.2 = (f32[1024,128]{1,0:T(8,128)S(1)}, f32[1024,128]{1,0:T(8,128)S(1)}, u32[]{:S(2)}, u32[]{:S(2)}) collective-permute-start(f32[1024,128]{1,0:T(8,128)S(1)} %bitcast.28), channel_id=1, source_target_pairs={{0,1},{1,0},{2,3},{3,2},{4,5},{5,4},{6,7},{7,6},{8,9},{9,8},{10,11... | collective-permute-start | bytes 1572872 | tf_op jit(solution)/shard_map/ppermute | solution.py:23
  33.0 1.5 %copy-start.1 = (f32[32,4096]{1,0:T(8,128)S(1)}, f32[32,4096]{1,0:T(8,128)}, u32[]{:S(2)}) copy-start(f32[32,4096]{1,0:T(8,128)} %param.6) | copy-start | bytes 1572868
  58.5 24.1 %collective-permute-start.3 = (f32[128,256]{1,0:T(8,128)S(1)}, f32[128,256]{1,0:T(8,128)S(1)}, u32[]{:S(2)}, u32[]{:S(2)}) collective-permute-start(f32[128,256]{1,0:T(8,128)S(1)} %get-tuple-element.30.x_ref), channel_id=1, source_target_pairs={{0,1},{1,0},{2,3},{3,2},{4,5},{5,4},{6,7},{7,6},{8,9},{9,8},{10,11... | collective-permute-start | bytes 393224 | tf_op jit(solution)/shard_map/ppermute | solution.py:23
  124.8 9.6 %collective-permute-start.4 = (f32[1024,128]{1,0:T(8,128)S(1)}, f32[1024,128]{1,0:T(8,128)S(1)}, u32[]{:S(2)}, u32[]{:S(2)}) collective-permute-start(f32[1024,128]{1,0:T(8,128)S(1)} %bitcast.13), channel_id=1, source_target_pairs={{0,1},{1,0},{2,3},{3,2},{4,5},{5,4},{6,7},{7,6},{8,9},{9,8},{10,11... | collective-permute-start | bytes 1572872 | tf_op jit(solution)/shard_map/ppermute | solution.py:23
  128.3 7.1 %collective-permute-start.5 = (f32[264,128]{1,0:T(8,128)S(1)}, f32[264,128]{1,0:T(8,128)S(1)}, u32[]{:S(2)}, u32[]{:S(2)}) collective-permute-start(f32[264,128]{1,0:T(8,128)S(1)} %factors.1.after_ref.l_ref), channel_id=1, source_target_pairs={{0,1},{1,0},{2,3},{3,2},{4,5},{5,4},{6,7},{7,6},{8,9},{9,8},{10,11... | collective-permute-start | bytes 405512 | tf_op jit(solution)/shard_map/ppermute | solution.py:23

commit v15 on v13

--- a/solution.py
+++ b/solution.py
@@ -12,7 +12,7 @@
 COLS = ("y", "core")
 PLANE = ("x", "y")
 SUB, LANE = 8, 128
-PIECES = 4
+PIECES = 8
 
 
 def exchanged(blocks, axis):

time: 137 us -> 137 us (level)
  no operation moved by 1% of the time
where the time goes in v15:
time: 137 us
  blocking collectives  87.1 us (64%)
  starting transfers between devices  39.5 us (29%)
  Pallas kernels  7.05 us (5%)
  waiting for transfers between devices  2.13 us (2%)
    all_to_all x5, blocking collectives, exchanged(): return lax.all_to_all(blocks, axis, 0, 0, tiled=True)  87.1 us
    ppermute x6, starting transfers between devices, from_other_core(): return lax.ppermute(value, 'core', [(0, 1), (1, 0)])  39.5 us
    pallas_call x10, Pallas kernels, call(): pl.pallas_call(kernel, name=name, out_shape=[jax.ShapeDtypeStruct(shape,...  7.05 us
  transfers between devices with their start and end apart: 6, of which 3 were waited for; matrix products, arithmetic and copies ran while one was open for 0% of the time, Pallas kernels for 2%

profile of v15, /device:TPU:1, one launch (start us, length us, event | category | flops | bytes accessed | tf_op | source)
XLA Modules:
  0.0 136.6 jit_solution(852196942976133975)
XLA Ops:
  0.6 3.3 %collective-permute-start.1 = (f32[32,4096]{1,0:T(8,128)}, f32[32,4096]{1,0:T(8,128)S(1)}, u32[]{:S(2)}, u32[]{:S(2)}) collective-permute-start(f32[32,4096]{1,0:T(8,128)} %param.6), channel_id=1, source_target_pairs={{0,1},{1,0},{2,3},{3,2},{4,5},{5,4},{6,7},{7,6},{8,9},{9,8},{10,11... | collective-permute-start | bytes 1572872 | tf_op jit(solution)/shard_map/ppermute | solution.py:23
  4.0 0.1 collective-permute-start
  4.1 1.8 %split.1 = f32[32,32,128]{2,1,0:T(8,128)} custom-call(f32[32,4096]{1,0:T(8,128)} %refs_0_.1), custom_call_target="tpu_custom_call" | custom-call | tf_op jit(solution)/shard_map/split/pallas_call | solution.py:27
  5.9 0.0 copy-start
  5.9 0.0 collective-permute-done
  5.9 0.0 collective-permute-done.1
  5.9 23.5 %all_to_all.40 = f32[32,32,128]{2,1,0:T(8,128)S(1)} all-to-all(f32[32,32,128]{2,1,0:T(8,128)} %split.1), channel_id=1, replica_groups=mesh['x'=4,'z'=8,'y'=4,'core'=2] {'x','z'}, dimensions={0} | all-to-all | bytes 1048576 | tf_op jit(solution)/shard_map/all_to_all | solution.py:19
  29.4 3.5 %collective-permute-start.2 = (f32[1024,128]{1,0:T(8,128)S(1)}, f32[1024,128]{1,0:T(8,128)S(1)}, u32[]{:S(2)}, u32[]{:S(2)}) collective-permute-start(f32[1024,128]{1,0:T(8,128)S(1)} %bitcast.28), channel_id=1, source_target_pairs={{0,1},{1,0},{2,3},{3,2},{4,5},{5,4},{6,7},{7,6},{8,9},{9,8},{10,11... | collective-permute-start | bytes 1572872 | tf_op jit(solution)/shard_map/ppermute | solution.py:23
  32.9 0.0 copy-done
  32.9 0.0 copy-start.1
  32.9 0.6 first_columns.1
  33.5 1.0 collective-permute-done.2.other_ref
  34.4 0.0 copy-done.1
  34.4 24.1 %conditional.1 = ((f32[128,256]{1,0:T(8,128)S(1)}, f32[1024,128]{1,0:T(8,128)S(1)}, f32[32,64,128]{2,1,0:T(8,128)S(1)})) conditional(s32[]{:T(128)} %convert_element_type.3, (f32[32,4096]{1,0:T(8,128)S(1)}, f32[32,4096]{1,0:T(8,128)S(1)}) %tuple.23, (f32[1024,128]{1,0:T(8,128)S(1)}, f32[128,128]{1,0:T(8,128)S(1)}, f32[1024,128]{1,0:T(8,128)S(1)}, ...), branch_computations={%region_0.0_spmd, %region_1.0_spmd} | conditional | bytes 2752552 | solution.py:266
  34.4 1.5 %split_shifted.1 = f32[32,64,128]{2,1,0:T(8,128)} custom-call(f32[32,4096]{1,0:T(8,128)S(1)} %get-tuple-element.12.refs_0_, f32[32,4096]{1,0:T(8,128)S(1)} %get-tuple-element.13.refs_1_), custom_call_target="tpu_custom_call" | custom-call | tf_op jit(solution)/shard_map/cond/branch_0_fun/split_shifted/pallas_call | solution.py:27
  36.0 22.5 %all_to_all.36 = f32[32,64,128]{2,1,0:T(8,128)S(1)} all-to-all(f32[32,64,128]{2,1,0:T(8,128)} %split_shifted.1), channel_id=1, replica_groups=mesh['x'=4,'z'=8,'y'=4,'core'=2] {'x','z'}, dimensions={0} | all-to-all | bytes 2097152 | tf_op jit(solution)/shard_map/cond/branch_0_fun/all_to_all | solution.py:19
  58.5 23.0 %collective-permute-start.3 = (f32[128,256]{1,0:T(8,128)S(1)}, f32[128,256]{1,0:T(8,128)S(1)}, u32[]{:S(2)}, u32[]{:S(2)}) collective-permute-start(f32[128,256]{1,0:T(8,128)S(1)} %get-tuple-element.30.x_ref), channel_id=1, source_target_pairs={{0,1},{1,0},{2,3},{3,2},{4,5},{5,4},{6,7},{7,6},{8,9},{9,8},{10,11... | collective-permute-start | bytes 393224 | tf_op jit(solution)/shard_map/ppermute | solution.py:23
  81.5 1.0 collective-permute-done.3.x_ref
  82.5 1.0 second_image.1
  83.5 14.9 %all_to_all.41 = f32[16,64,128]{2,1,0:T(8,128)S(1)} all-to-all(f32[16,64,128]{2,1,0:T(8,128)S(1)} %bitcast.18), channel_id=1, replica_groups=mesh['x'=4,'z'=8,'y'=4,'core'=2] {'x','y'}, dimensions={0} | all-to-all | bytes 1048576 | tf_op jit(solution)/shard_map/all_to_all | solution.py:19
  98.4 14.2 %all_to_all.42 = f32[8,64,128]{2,1,0:T(8,128)S(1)} all-to-all(f32[8,64,128]{2,1,0:T(8,128)S(1)} %bitcast.26), channel_id=1, replica_groups=mesh['x'=4,'z'=8,'y'=4,'core'=2] {'z'}, dimensions={0} | all-to-all | bytes 524288 | tf_op jit(solution)/shard_map/all_to_all | solution.py:19
  112.7 12.0 %all_to_all.43 = f32[16,64,128]{2,1,0:T(8,128)S(1)} all-to-all(f32[16,64,128]{2,1,0:T(8,128)S(1)} %bitcast.23), channel_id=1, replica_groups=mesh['x'=4,'z'=8,'y'=4,'core'=2] {'x','y'}, dimensions={0} | all-to-all | bytes 1048576 | tf_op jit(solution)/shard_map/all_to_all | solution.py:19
  124.7 3.4 %collective-permute-start.4 = (f32[1024,128]{1,0:T(8,128)S(1)}, f32[1024,128]{1,0:T(8,128)S(1)}, u32[]{:S(2)}, u32[]{:S(2)}) collective-permute-start(f32[1024,128]{1,0:T(8,128)S(1)} %bitcast.13), channel_id=1, source_target_pairs={{0,1},{1,0},{2,3},{3,2},{4,5},{5,4},{6,7},{7,6},{8,9},{9,8},{10,11... | collective-permute-start | bytes 1572872 | tf_op jit(solution)/shard_map/ppermute | solution.py:23
  128.2 6.1 %collective-permute-start.5 = (f32[264,128]{1,0:T(8,128)S(1)}, f32[264,128]{1,0:T(8,128)S(1)}, u32[]{:S(2)}, u32[]{:S(2)}) collective-permute-start(f32[264,128]{1,0:T(8,128)S(1)} %factors.1.after_ref.l_ref), channel_id=1, source_target_pairs={{0,1},{1,0},{2,3},{3,2},{4,5},{5,4},{6,7},{7,6},{8,9},{9,8},{10,11... | collective-permute-start | bytes 405512 | tf_op jit(solution)/shard_map/ppermute | solution.py:23
  134.3 0.0 collective-permute-done.4.other_ref
  134.3 0.8 cross.1.cross_ref
  135.1 0.2 collective-permute-done.5.l_other_ref
  135.3 1.3 results.1
  (6 shorter events, 0.1 us)
Async XLA Ops:
  0.6 5.3 %collective-permute-start.1 = (f32[32,4096]{1,0:T(8,128)}, f32[32,4096]{1,0:T(8,128)S(1)}, u32[]{:S(2)}, u32[]{:S(2)}) collective-permute-start(f32[32,4096]{1,0:T(8,128)} %param.6), channel_id=1, source_target_pairs={{0,1},{1,0},{2,3},{3,2},{4,5},{5,4},{6,7},{7,6},{8,9},{9,8},{10,11... | collective-permute-start | bytes 1572872 | tf_op jit(solution)/shard_map/ppermute | solution.py:23
  4.0 1.9 %collective-permute-start = (f32[128,128]{1,0:T(8,128)}, f32[128,128]{1,0:T(8,128)S(1)}, u32[]{:S(2)}, u32[]{:S(2)}) collective-permute-start(f32[128,128]{1,0:T(8,128)} %start_ref.1), channel_id=1, source_target_pairs={{0,1},{1,0},{2,3},{3,2},{4,5},{5,4},{6,7},{7,6},{8,9},{9,8},{10,11... | collective-permute-start | bytes 196616 | tf_op jit(solution)/shard_map/ppermute | solution.py:23
  5.9 27.0 %copy-start = (f32[128,128]{1,0:T(8,128)S(1)}, f32[128,128]{1,0:T(8,128)}, u32[]{:S(2)}) copy-start(f32[128,128]{1,0:T(8,128)} %start_ref.1) | copy-start | bytes 196612
  29.4 5.0 %collective-permute-start.2 = (f32[1024,128]{1,0:T(8,128)S(1)}, f32[1024,128]{1,0:T(8,128)S(1)}, u32[]{:S(2)}, u32[]{:S(2)}) collective-permute-start(f32[1024,128]{1,0:T(8,128)S(1)} %bitcast.28), channel_id=1, source_target_pairs={{0,1},{1,0},{2,3},{3,2},{4,5},{5,4},{6,7},{7,6},{8,9},{9,8},{10,11... | collective-permute-start | bytes 1572872 | tf_op jit(solution)/shard_map/ppermute | solution.py:23
  32.9 1.5 %copy-start.1 = (f32[32,4096]{1,0:T(8,128)S(1)}, f32[32,4096]{1,0:T(8,128)}, u32[]{:S(2)}) copy-start(f32[32,4096]{1,0:T(8,128)} %param.6) | copy-start | bytes 1572868
  58.5 24.0 %collective-permute-start.3 = (f32[128,256]{1,0:T(8,128)S(1)}, f32[128,256]{1,0:T(8,128)S(1)}, u32[]{:S(2)}, u32[]{:S(2)}) collective-permute-start(f32[128,256]{1,0:T(8,128)S(1)} %get-tuple-element.30.x_ref), channel_id=1, source_target_pairs={{0,1},{1,0},{2,3},{3,2},{4,5},{5,4},{6,7},{7,6},{8,9},{9,8},{10,11... | collective-permute-start | bytes 393224 | tf_op jit(solution)/shard_map/ppermute | solution.py:23
  124.7 9.6 %collective-permute-start.4 = (f32[1024,128]{1,0:T(8,128)S(1)}, f32[1024,128]{1,0:T(8,128)S(1)}, u32[]{:S(2)}, u32[]{:S(2)}) collective-permute-start(f32[1024,128]{1,0:T(8,128)S(1)} %bitcast.13), channel_id=1, source_target_pairs={{0,1},{1,0},{2,3},{3,2},{4,5},{5,4},{6,7},{7,6},{8,9},{9,8},{10,11... | collective-permute-start | bytes 1572872 | tf_op jit(solution)/shard_map/ppermute | solution.py:23
  128.2 7.1 %collective-permute-start.5 = (f32[264,128]{1,0:T(8,128)S(1)}, f32[264,128]{1,0:T(8,128)S(1)}, u32[]{:S(2)}, u32[]{:S(2)}) collective-permute-start(f32[264,128]{1,0:T(8,128)S(1)} %factors.1.after_ref.l_ref), channel_id=1, source_target_pairs={{0,1},{1,0},{2,3},{3,2},{4,5},{5,4},{6,7},{7,6},{8,9},{9,8},{10,11... | collective-permute-start | bytes 405512 | tf_op jit(solution)/shard_map/ppermute | solution.py:23
